TPU v7x, 512 devices: a whole 4x4x16 slice. The times are simulated.
512 devices in a mesh: freq: 128 (over y_lo, x, z), row: 4 (over y_hi, core).
Axes of the slice: x: 4, y: 4 (y_hi: 2, y_lo: 2; y = y_hi * 2 + y_lo), z: 16, core: 2. Of those that a mesh axis runs over, the one named last changes fastest.
Arguments:
- operator: bfloat16 [128, 1024, 2, 1024], P('freq', 'row'), may hold values from -0.125 to 0.125
- recorded: bfloat16 [128, 1024, 2, 512], P('freq', 'row'), may hold values from -6 to 6
- filter_coefficients: float32 [3, 8, 1024], P(None, None, ('row', 'freq')), may hold values from -1.2 to 1.2
- tap_delays: int32 [8], replicated, may hold values from 0 to 63, as said below
Outputs:
- primaries: bfloat16 [1024, 512, 1024], P(('row', 'freq'))
Inputs may be any that keep to these rules, and one draw needn't show every extreme that they name: `tap_delays`: the delays are not distinct in general; at least one tap has delay 64 - 1.
All inputs are finite; a program needn't handle non-finite values.
Results may differ from a plain program's by a relative error of at most 0.008.
Values may be sent and summed in bfloat16 or wider, within the bound.
No kernel may reach another device: no remote copies, remote signals or barrier semaphores. Data moves between devices by JAX's collectives and lax.ppermute only.
A program may use at most 64 MiB of HBM per device.

v0:
```python
import math

import jax
import jax.numpy as jnp
from jax import lax
from jax.sharding import PartitionSpec as P

NT = 1024
MAXLAG = 64


shrink_level = 0.5


def padded_2(block, sides, width):
    for axis, dim in sides:
        count = lax.axis_size(axis)
        forward = [(i, i + 1) for i in range(count - 1)]
        backward = [(target, source) for source, target in forward]
        low = lax.ppermute(
            lax.slice_in_dim(block, block.shape[dim] - width, None, axis=dim), axis, forward
        )
        high = lax.ppermute(lax.slice_in_dim(block, 0, width, axis=dim), axis, backward)
        block = jnp.concatenate([low, block, high], axis=dim)
    return block


def inverse_lookup(harmonics, time_step_total):
    overtone_indices = jnp.arange(harmonics) + 1
    recording_epochs = jnp.arange(time_step_total)
    rotation_radians = (
        overtone_indices[:, None] * recording_epochs[None, :] % time_step_total
    ).astype(jnp.float32) * (2.0 * math.pi / time_step_total)
    scale = 1.0 / math.sqrt(harmonics)
    return jnp.stack(
        [jnp.cos(rotation_radians) * scale, -jnp.sin(rotation_radians) * scale], axis=1
    ).astype(jnp.bfloat16)


def complex_block(columns, segment):
    real_component = segment[:, 0]
    imag_part = segment[:, 1]
    upper = jnp.concatenate([real_component, imag_part], axis=1)
    lower = jnp.concatenate([-imag_part, real_component], axis=1)
    return jnp.dot(
        columns, jnp.concatenate([upper, lower], axis=0), preferred_element_type=jnp.float32
    )


def match_filter(border_rows, weights, tap_delays, row_count, time_step_total):
    padded = jnp.pad(border_rows, ((0, 0), (0, 0), (MAXLAG, 0)))
    estimate = jnp.zeros((row_count, border_rows.shape[1], time_step_total), jnp.float32)
    anchor = jnp.zeros((), jnp.int32)
    for tap_index in range(weights.shape[1]):
        begin = MAXLAG - tap_delays[tap_index]
        displaced_trace = lax.dynamic_slice(
            padded, (anchor, anchor, begin), (padded.shape[0], padded.shape[1], time_step_total)
        )
        for neighbour in range(3):
            factor = weights[neighbour, tap_index][:, None, None]
            estimate = estimate + factor * displaced_trace[
                neighbour : neighbour + row_count
            ].astype(jnp.float32)
    return estimate


def shrink(data_time, estimate):
    residual = data_time.astype(jnp.float32) - estimate
    return (jnp.sign(residual) * jnp.maximum(jnp.abs(residual) - shrink_level, 0.0)).astype(
        jnp.bfloat16
    )


def body(operator, recorded, filter_coefficients, tap_delays):
    local_rows = operator.shape[1]
    gather_total = recorded.shape[3]
    own_block = operator[0]
    segment = lax.all_gather(recorded, "row", axis=1, tiled=True)
    signal_length = segment.shape[1]
    columns = own_block.reshape(local_rows, 2 * signal_length)
    product = complex_block(columns, segment[0])
    spectra = product.astype(jnp.bfloat16).reshape(1, local_rows, 2, gather_total)
    predicted_traces, recorded_traces = (
        lax.all_to_all(spectra, "freq", split_axis=1, concat_axis=0, tiled=True),
        lax.all_to_all(recorded, "freq", split_axis=1, concat_axis=0, tiled=True),
    )
    table = inverse_lookup(predicted_traces.shape[0], NT)

    def to_time(traces):
        return jnp.einsum(
            "frcs,fct->rst", traces, table, preferred_element_type=jnp.float32
        ).astype(jnp.bfloat16)

    data_time = to_time(recorded_traces)
    border_rows = padded_2(to_time(predicted_traces), (("freq", 0),), 1)
    estimate = match_filter(
        border_rows, filter_coefficients, tap_delays, predicted_traces.shape[1], NT
    )
    return shrink(data_time, estimate)


def solution(mesh):
    in_specs = (
        P("freq", "row", None, None),
        P("freq", "row", None, None),
        P(None, None, ("row", "freq")),
        P(),
    )
    out_specs = P(("row", "freq"), None, None)
    return jax.shard_map(body, mesh=mesh, in_specs=in_specs, out_specs=out_specs, check_vma=False)
```

profile of v0, /device:TPU:8, one launch (start us, length us, event | category | flops | bytes accessed | tf_op | source)
XLA Modules:
  0.0 212.1 jit_solution(1492183056484388324)
XLA Ops:
  6.5 1.9 copy.18
  8.4 1.5 copy.29
  9.9 37.3 %all-gather.2.cloned.1.call-done = bf16[1,1024,2,512]{3,1,2,0:T(8,128)(2,1)} async-done(((bf16[1,256,2,512]{3,1,2,0:T(8,128)(2,1)}), bf16[1,1024,2,512]{3,1,2,0:T(8,128)(2,1)}) %all-gather.2.cloned.1.call-update) | async-done | bytes 2097168 | tf_op jit(solution)/shard_map/all_gather | solution.py:78
  47.3 1.8 slice_bitcast_fusion
  49.1 0.4 copy-done
  49.5 1.3 fusion.13
  50.8 1.2 copy.19
  52.0 17.7 %all-to-all-start.1 = ((bf16[1,256,2,512]{3,2,0,1:T(2,128)(2,1)}), bf16[1,256,2,512]{3,2,0,1:T(2,128)(2,1)S(1)}, u32[]{:S(2)}, u32[]{:S(2)}) async-start(bf16[1,256,2,512]{3,2,0,1:T(2,128)(2,1)} %copy.19), calls=%async_computation.1 | async-start | bytes 1048576 | tf_op jit(solution)/shard_map/all_to_all | solution.py:84
  69.8 2.2 %multiply_convert_fusion.2 = (bf16[128,1,1024]{0,2,1:T(8,128)(2,1)S(1)}, bf16[128,1,1024]{0,2,1:T(8,128)(2,1)S(1)}) fusion(s32[128]{0:T(128)S(1)} %iota_add_fusion), kind=kLoop, calls=%fused_computation.31 | loop fusion | flops 2490368 | bytes 524800 | tf_op jit(solution)/shard_map/convert.1
  72.0 30.1 %all-to-all-done.1 = bf16[1,256,2,512]{3,2,0,1:T(2,128)(2,1)S(1)} async-done(((bf16[1,256,2,512]{3,2,0,1:T(2,128)(2,1)}), bf16[1,256,2,512]{3,2,0,1:T(2,128)(2,1)S(1)}, u32[]{:S(2)}, u32[]{:S(2)}) %all-to-all-start.1) | async-done | bytes 524320 | tf_op jit(solution)/shard_map/all_to_all | solution.py:84
  102.1 0.7 bitcast_convert_fusion
  102.9 1.5 fusion.30
  104.4 3.1 %collective-permute-start = (bf16[1,512,1024]{1,2,0:T(8,128)(2,1)}, bf16[1,512,1024]{1,2,0:T(8,128)(2,1)S(1)}, u32[]{:S(2)}, u32[]{:S(2)}) collective-permute-start(bf16[1,512,1024]{1,2,0:T(8,128)(2,1)} %get-tuple-element.29), channel_id=1, source_target_pairs={{0,4},{4,8},{8,12},{12,16},{16,20},{20,24},{24,28},{28,32},{32,36}... | collective-permute-start | bytes 3145736 | tf_op jit(solution)/shard_map/ppermute | solution.py:20
  107.4 7.0 %collective-permute-start.1 = (bf16[1,512,1024]{1,2,0:T(8,128)(2,1)}, bf16[1,512,1024]{1,2,0:T(8,128)(2,1)}, u32[]{:S(2)}, u32[]{:S(2)}) collective-permute-start(bf16[1,512,1024]{1,2,0:T(8,128)(2,1)} %get-tuple-element.30), channel_id=1, source_target_pairs={{4,0},{8,4},{12,8},{16,12},{20,16},{24,20},{28,24},{32,28},{36,32}... | collective-permute-start | bytes 3145736 | tf_op jit(solution)/shard_map/ppermute | solution.py:23
  114.4 6.4 %all-to-all-start = ((bf16[1,256,2,512]{3,2,0,1:T(2,128)(2,1)}), bf16[1,256,2,512]{3,2,0,1:T(2,128)(2,1)}, u32[]{:S(2)}, u32[]{:S(2)}) async-start(bf16[1,256,2,512]{3,2,0,1:T(2,128)(2,1)} %bitcast.1), calls=%async_computation | async-start | bytes 1048576 | tf_op jit(solution)/shard_map/all_to_all | solution.py:85
  120.9 0.7 fusion.31
  131.8 0.2 slice_reduce_fusion.22
  132.1 0.5 slice_reduce_fusion.23
  132.5 17.4 %collective-permute-done = bf16[1,512,1024]{1,2,0:T(8,128)(2,1)S(1)} collective-permute-done((bf16[1,512,1024]{1,2,0:T(8,128)(2,1)}, bf16[1,512,1024]{1,2,0:T(8,128)(2,1)S(1)}, u32[]{:S(2)}, u32[]{:S(2)}) %collective-permute-start) | collective-permute-done | bytes 1048608 | tf_op jit(solution)/shard_map/ppermute | solution.py:20
  149.9 2.2 %collective-permute-done.1 = bf16[1,512,1024]{1,2,0:T(8,128)(2,1)} collective-permute-done((bf16[1,512,1024]{1,2,0:T(8,128)(2,1)}, bf16[1,512,1024]{1,2,0:T(8,128)(2,1)}, u32[]{:S(2)}, u32[]{:S(2)}) %collective-permute-start.1) | collective-permute-done | bytes 1048608 | tf_op jit(solution)/shard_map/ppermute | solution.py:23
  152.1 4.1 %fusion.4 = bf16[4,512,1088]{1,2,0:T(8,128)(2,1)} fusion(bf16[1,512,1024]{1,2,0:T(8,128)(2,1)} %collective-permute-done.1, bf16[2,512,1024]{1,2,0:T(8,128)(2,1)S(1)} %bitcast_convert_fusion, bf16[1,512,1024]{1,2,0:T(8,128)(2,1)S(1)} %collective-permute-done), kind=kLoop, calls=%fused_computation.5 | loop fusion | flops 22282240 | bytes 8650752 | tf_op jit(solution)/shard_map/concatenate | solution.py:24
  156.2 4.4 %all-to-all-done = bf16[1,256,2,512]{3,2,0,1:T(2,128)(2,1)} async-done(((bf16[1,256,2,512]{3,2,0,1:T(2,128)(2,1)}), bf16[1,256,2,512]{3,2,0,1:T(2,128)(2,1)}, u32[]{:S(2)}, u32[]{:S(2)}) %all-to-all-start) | async-done | bytes 524320 | tf_op jit(solution)/shard_map/all_to_all | solution.py:85
  160.6 42.3 %multiply_convert_fusion = bf16[2,512,1024]{1,2,0:T(8,128)(2,1)S(1)} fusion(bf16[4,512,1088]{1,2,0:T(8,128)(2,1)} %fusion.4, s32[]{:T(128)S(6)} %add.218, s32[]{:T(128)S(6)} %select_n.52, s32[]{:T(128)S(6)} %add.217, s32[]{:T(128)S(6)} %select_n.51, s32[]{:T(128)S(6)} %select_n.50, s32[]{:T(128)S(6)} %select_n.49, s32[]{:T(128)S(6)} %select_n.48, ...), kind=kOutput, calls=%fused_computation.17 | convolution fusion | flops 621805568 | bytes 53477608 | tf_op jit(solution)/shard_map/frcs,fct->rst/dot_general | solution.py:90
  202.9 2.4 %copy.23 = bf16[2,512,1024]{2,1,0:T(8,128)(2,1)} copy(bf16[2,512,1024]{1,2,0:T(8,128)(2,1)S(1)} %multiply_convert_fusion) | data formatting | bytes 4194304 | tf_op jit(solution)/shard_map/convert_element_type | solution.py:69
  (11 shorter events, 0.1 us)
Async XLA Ops:
  6.5 40.7 %all-gather.2.cloned.1.call-start = ((), (), s32[]{:S(2)}) async-start(), calls=%async_computation.2 | async-start | bytes 2621440 | tf_op jit(solution)/shard_map/all_gather | solution.py:78
  47.3 2.2 %copy-start = (bf16[1,1024,2,512]{3,1,2,0:T(8,128)(2,1)S(1)}, bf16[1,1024,2,512]{3,1,2,0:T(8,128)(2,1)}, u32[]{:S(2)}) copy-start(bf16[1,1024,2,512]{3,1,2,0:T(8,128)(2,1)} %all-gather.2.cloned.1.call-done) | copy-start | bytes 6291460
  52.0 50.1 %all-to-all-start.1 = ((bf16[1,256,2,512]{3,2,0,1:T(2,128)(2,1)}), bf16[1,256,2,512]{3,2,0,1:T(2,128)(2,1)S(1)}, u32[]{:S(2)}, u32[]{:S(2)}) async-start(bf16[1,256,2,512]{3,2,0,1:T(2,128)(2,1)} %copy.19), calls=%async_computation.1 | async-start | bytes 1048576 | tf_op jit(solution)/shard_map/all_to_all | solution.py:84
  72.0 32.4 %copy-start.1 = (bf16[128,1,1024]{0,2,1:T(8,128)(2,1)}, bf16[128,1,1024]{0,2,1:T(8,128)(2,1)S(1)}, u32[]{:S(2)}) copy-start(bf16[128,1,1024]{0,2,1:T(8,128)(2,1)S(1)} %get-tuple-element.42) | copy-start | bytes 786436
  102.1 18.7 %copy-start.3 = (s32[8]{0:T(128)S(1)}, s32[8]{0:T(128)}, u32[]{:S(2)}) copy-start(s32[8]{0:T(128)} %param.7) | copy-start | bytes 100
  102.1 29.7 %copy-start.2 = (f32[3,8,2]{1,2,0:T(2,128)S(1)}, f32[3,8,2]{1,2,0:T(2,128)}, u32[]{:S(2)}) copy-start(f32[3,8,2]{1,2,0:T(2,128)} %param.6) | copy-start | bytes 580
  104.4 45.5 %collective-permute-start = (bf16[1,512,1024]{1,2,0:T(8,128)(2,1)}, bf16[1,512,1024]{1,2,0:T(8,128)(2,1)S(1)}, u32[]{:S(2)}, u32[]{:S(2)}) collective-permute-start(bf16[1,512,1024]{1,2,0:T(8,128)(2,1)} %get-tuple-element.29), channel_id=1, source_target_pairs={{0,4},{4,8},{8,12},{12,16},{16,20},{20,24},{24,28},{28,32},{32,36}... | collective-permute-start | bytes 3145736 | tf_op jit(solution)/shard_map/ppermute | solution.py:20
  107.4 44.7 %collective-permute-start.1 = (bf16[1,512,1024]{1,2,0:T(8,128)(2,1)}, bf16[1,512,1024]{1,2,0:T(8,128)(2,1)}, u32[]{:S(2)}, u32[]{:S(2)}) collective-permute-start(bf16[1,512,1024]{1,2,0:T(8,128)(2,1)} %get-tuple-element.30), channel_id=1, source_target_pairs={{4,0},{8,4},{12,8},{16,12},{20,16},{24,20},{28,24},{32,28},{36,32}... | collective-permute-start | bytes 3145736 | tf_op jit(solution)/shard_map/ppermute | solution.py:23
  114.4 46.2 %all-to-all-start = ((bf16[1,256,2,512]{3,2,0,1:T(2,128)(2,1)}), bf16[1,256,2,512]{3,2,0,1:T(2,128)(2,1)}, u32[]{:S(2)}, u32[]{:S(2)}) async-start(bf16[1,256,2,512]{3,2,0,1:T(2,128)(2,1)} %bitcast.1), calls=%async_computation | async-start | bytes 1048576 | tf_op jit(solution)/shard_map/all_to_all | solution.py:85
Sparse Core Ops, SparseCore 0:
  9.4 37.7 all-gather.1
where the time goes:
time: 213 us; the launch traced here: 212 us
  waiting for transfers between devices  91.4 us (43%)
  matrix products  44.4 us (21%)
  starting transfers between devices  34.2 us (16%)
  between operations  23.8 us (11%)
  local copies, waits for them, and re-layouts  12 us (6%)
  other arithmetic  6.37 us (3%)
    dot_general x2, matrix products, to_time(): jnp.einsum('frcs,fct->rst', traces, table, preferred_element_type=jnp.flo...  43.1 us
    all_gather x1, waiting for transfers between devices, body(): segment = lax.all_gather(recorded, 'row', axis=1, tiled=True)  37.3 us
    all_to_all x1, waiting for transfers between devices, body(): lax.all_to_all(spectra, 'freq', split_axis=1, concat_axis=0, tiled=True)  30.1 us
    all_to_all x1, starting transfers between devices, body(): lax.all_to_all(spectra, 'freq', split_axis=1, concat_axis=0, tiled=True)  17.7 us
    ppermute x1, waiting for transfers between devices, padded_2(): lax.ppermute(lax.slice_in_dim(block, block.shape[dim] - width, None, axis...  17.4 us
    ppermute x1, starting transfers between devices, padded_2(): lax.ppermute(lax.slice_in_dim(block, 0, width, axis=dim), axis, backward)  6.99 us
    all_to_all x1, starting transfers between devices, body(): lax.all_to_all(recorded, 'freq', split_axis=1, concat_axis=0, tiled=True)  6.44 us
    all_to_all x1, waiting for transfers between devices, body(): lax.all_to_all(recorded, 'freq', split_axis=1, concat_axis=0, tiled=True)  4.4 us
  transfers between devices with their start and end apart: 5, of which 5 were waited for; matrix products, arithmetic and copies ran while one was open for 4% of the time, Pallas kernels for 0%

commit v1 on v0

v1 whole, which is shorter than its diff:
```python
import math

import jax
import jax.numpy as jnp
from jax import lax
from jax.sharding import PartitionSpec as P

NT = 1024
MAXLAG = 64
BLOCK = 128


shrink_level = 0.5


def inverse_lookup(harmonics, time_step_total):
    overtone_indices = jnp.arange(harmonics) + 1
    recording_epochs = jnp.arange(time_step_total)
    rotation_radians = (
        overtone_indices[:, None] * recording_epochs[None, :] % time_step_total
    ).astype(jnp.float32) * (2.0 * math.pi / time_step_total)
    scale = 1.0 / math.sqrt(harmonics)
    return jnp.stack(
        [jnp.cos(rotation_radians) * scale, -jnp.sin(rotation_radians) * scale], axis=1
    ).astype(jnp.bfloat16)


def filtered_tables(table, weights, tap_delays):
    harmonics = table.shape[0]
    neighbours, taps, stations = weights.shape
    kinds = neighbours * stations
    blocks = NT // BLOCK
    flat = jnp.pad(table.reshape(2 * harmonics, NT), ((0, 0), (MAXLAG, 0)))
    window = BLOCK + MAXLAG
    windows = jnp.stack(
        [flat[:, j * BLOCK : j * BLOCK + window] for j in range(blocks)], axis=1
    )
    lag = jnp.arange(BLOCK)[None, :] - jnp.arange(window)[:, None] + MAXLAG
    w = weights.transpose(1, 0, 2).reshape(taps, kinds)
    band = sum(
        w[k][None, :, None] * (lag == tap_delays[k]).astype(jnp.float32)[:, None, :]
        for k in range(taps)
    ).reshape(window, kinds * BLOCK)
    high = band.astype(jnp.bfloat16)
    low = (band - high.astype(jnp.float32)).astype(jnp.bfloat16)
    out = jnp.dot(
        jnp.concatenate([windows, windows], axis=2).reshape(-1, 2 * window),
        jnp.concatenate([high, low], axis=0),
        preferred_element_type=jnp.float32,
    ).astype(jnp.bfloat16)
    out = out.reshape(harmonics, 2, blocks, neighbours, stations, BLOCK)
    return out.transpose(3, 4, 0, 1, 2, 5).reshape(
        neighbours, stations, harmonics, 2, NT
    )


def body(operator, recorded, filter_coefficients, tap_delays):
    local_rows = operator.shape[1]
    freq_count = lax.axis_size("freq")
    row_count = lax.axis_size("row")
    row = lax.axis_index("row")

    def across(value, mask):
        return lax.ppermute(value, "row", [(i, i ^ mask) for i in range(row_count)])

    own = recorded[0]
    far = across(own, 2)
    recorded_traces = lax.all_to_all(
        recorded, "freq", split_axis=1, concat_axis=0, tiled=True
    )
    near = across(own, 1)
    far_near = across(far, 1)

    def complex_rows(mask):
        part = lax.dynamic_slice_in_dim(
            operator[0], (row ^ mask) * local_rows, local_rows, axis=2
        )
        real_part, imag_part = part[:, 0], part[:, 1]
        upper = jnp.stack([real_part, -imag_part], axis=-1)
        lower = jnp.stack([imag_part, real_part], axis=-1)
        return jnp.stack([upper, lower], axis=1)

    def product(mask, segment):
        return jnp.einsum(
            "rqsp,spc->rqc", complex_rows(mask), segment, preferred_element_type=jnp.float32
        )

    total = product(0, own) + product(1, near) + product(2, far) + product(3, far_near)
    spectra = total.astype(jnp.bfloat16)[None]
    traces = lax.all_to_all(spectra, "freq", split_axis=1, concat_axis=0, tiled=True)

    table = inverse_lookup(freq_count, NT)
    filter_coefficients, tap_delays, spectra = lax.optimization_barrier(
        (filter_coefficients, tap_delays, spectra)
    )
    filters = filtered_tables(table, filter_coefficients, tap_delays)

    def to_time(spectrum, basis):
        return jnp.einsum("fpc,fpt->ct", spectrum, basis, preferred_element_type=jnp.float32)

    forward = [(i, i + 1) for i in range(freq_count - 1)]
    backward = [(i + 1, i) for i in range(freq_count - 1)]
    before = lax.ppermute(traces[:, 1], "freq", forward)
    after = lax.ppermute(traces[:, 0], "freq", backward)
    data_time = [to_time(recorded_traces[:, s], table).astype(jnp.bfloat16) for s in range(2)]
    stations = [before, traces[:, 0], traces[:, 1], after]
    result = []
    for s in range(2):
        own_order = (1, 2, 0) if s == 0 else (0, 1, 2)
        estimate = sum(to_time(stations[s + n], filters[n, s]) for n in own_order)
        residual = data_time[s].astype(jnp.float32) - estimate
        result.append(
            (jnp.sign(residual) * jnp.maximum(jnp.abs(residual) - shrink_level, 0.0)).astype(
                jnp.bfloat16
            )
        )
    return jnp.stack(result)


def solution(mesh):
    in_specs = (
        P("freq", "row", None, None),
        P("freq", "row", None, None),
        P(None, None, ("row", "freq")),
        P(),
    )
    out_specs = P(("row", "freq"), None, None)
    return jax.shard_map(body, mesh=mesh, in_specs=in_specs, out_specs=out_specs, check_vma=False)
```

time: 213 us -> 126 us (0.59)
  waiting for transfers between devices: 91.4 us -> 22.5 us
  matrix products: 44.4 us -> 15.4 us
  between operations: 23.8 us -> 0.74 us
  starting transfers between devices: 34.2 us -> 49.6 us
  local copies, waits for them, and re-layouts: 12 us -> 26.2 us
  other arithmetic: 6.37 us -> 10.9 us
    all_gather x1 -> x0, waiting for transfers between devices: 37.3 us -> none  [body(): segment = lax.all_gather(recorded, 'row', axis=1, tiled=True)]
    dot_general x3 -> x13, matrix products: 44.4 us -> 15.4 us  [the longest x8 7.69 us: to_time(): jnp.einsum('fpc,fpt->ct', spectrum, basis, preferred_element_type=jnp.flo...]
    ppermute x2 -> x5, waiting for transfers between devices: 19.6 us -> 1.73 us  [the longest x1 1.34 us: body(): after = lax.ppermute(traces[:, 0], 'freq', backward)]
    all_to_all x1, waiting for transfers between devices: 30.1 us -> 13.4 us  [body(): lax.all_to_all(spectra, 'freq', split_axis=1, concat_axis=0, tiled=True)]
    all_to_all x1, starting transfers between devices: 6.44 us -> 20.7 us  [body(): lax.all_to_all(recorded, 'freq', split_axis=1, concat_axis=0, tiled=True)]
    ppermute x2 -> x5, starting transfers between devices: 10.1 us -> 18.6 us  [the longest x3 8.04 us: across(): return lax.ppermute(value, 'row', [(i, i ^ mask) for i in range(row_count)])]
    all_to_all x1, starting transfers between devices: 17.7 us -> 10.3 us  [body(): lax.all_to_all(spectra, 'freq', split_axis=1, concat_axis=0, tiled=True)]
    convert_element_type x0 -> x10, other arithmetic: none -> 6.39 us  [the longest x8 5.11 us: filtered_tables(): (lag == tap_delays[k]).astype(jnp.float32)[:, None, :]]
  transfers between devices with their start and end apart: 5 -> 7, of which waited for: 5 -> 4; matrix products, arithmetic and copies ran while one was open for 4% -> 34% of each run, Pallas kernels for 0% -> 0%
where the time goes in v1:
time: 126 us; the launch traced here: 125 us
  starting transfers between devices  49.6 us (39%)
  local copies, waits for them, and re-layouts  26.2 us (21%)
  waiting for transfers between devices  22.5 us (18%)
  matrix products  15.4 us (12%)
  other arithmetic  10.9 us (9%)
    all_to_all x1, starting transfers between devices, body(): lax.all_to_all(recorded, 'freq', split_axis=1, concat_axis=0, tiled=True)  20.7 us
    all_to_all x1, waiting for transfers between devices, body(): lax.all_to_all(spectra, 'freq', split_axis=1, concat_axis=0, tiled=True)  13.4 us
    all_to_all x1, starting transfers between devices, body(): lax.all_to_all(spectra, 'freq', split_axis=1, concat_axis=0, tiled=True)  10.3 us
    ppermute x3, starting transfers between devices, across(): return lax.ppermute(value, 'row', [(i, i ^ mask) for i in range(row_count)])  8.04 us
    dot_general x8, matrix products, to_time(): jnp.einsum('fpc,fpt->ct', spectrum, basis, preferred_element_type=jnp.flo...  7.69 us
    all_to_all x1, waiting for transfers between devices, body(): lax.all_to_all(recorded, 'freq', split_axis=1, concat_axis=0, tiled=True)  7.4 us
    ppermute x1, starting transfers between devices, body(): after = lax.ppermute(traces[:, 0], 'freq', backward)  6.97 us
    slice x1, local copies, waits for them, and re-layouts, body(): estimate = sum((to_time(stations[s + n], filters[n, s]) for n in own_order))  6.09 us
  transfers between devices with their start and end apart: 7, of which 4 were waited for; matrix products, arithmetic and copies ran while one was open for 34% of the time, Pallas kernels for 0%

profile of v1, /device:TPU:8, one launch (start us, length us, event | category | flops | bytes accessed | tf_op | source)
XLA Modules:
  0.0 125.3 jit_solution(16341863741445250477)
XLA Ops:
  0.0 2.0 %copy.151 = bf16[1,256,2,512]{3,1,2,0:T(8,128)(2,1)} copy(bf16[1,256,2,512]{3,2,1,0:T(2,128)(2,1)} %param.5) | data formatting | bytes 1048576 | tf_op args[1]
  2.0 4.2 %collective-permute-start.1 = (bf16[256,2,512]{2,0,1:T(8,128)(2,1)}, bf16[256,2,512]{2,0,1:T(8,128)(2,1)}, u32[]{:S(2)}, u32[]{:S(2)}) collective-permute-start(bf16[256,2,512]{2,0,1:T(8,128)(2,1)} %bitcast.308), channel_id=1, source_target_pairs={{0,2},{1,3},{2,0},{3,1},{4,6},{5,7},{6,4},{7,5},{8,10},{9,11},{10,... | collective-permute-start | bytes 1572872 | tf_op jit(solution)/shard_map/ppermute | solution.py:64
  6.2 1.9 %collective-permute-start = (bf16[256,2,512]{2,0,1:T(8,128)(2,1)}, bf16[256,2,512]{2,0,1:T(8,128)(2,1)}, u32[]{:S(2)}, u32[]{:S(2)}) collective-permute-start(bf16[256,2,512]{2,0,1:T(8,128)(2,1)} %bitcast.308), channel_id=1, source_target_pairs={{0,1},{1,0},{2,3},{3,2},{4,5},{5,4},{6,7},{7,6},{8,9},{9,8},{10,11... | collective-permute-start | bytes 1572872 | tf_op jit(solution)/shard_map/ppermute | solution.py:64
  8.1 20.7 %all-to-all-start = ((bf16[1,256,2,512]{3,2,0,1:T(2,128)(2,1)}), bf16[1,256,2,512]{3,2,0,1:T(2,128)(2,1)S(1)}, u32[]{:S(2)}, u32[]{:S(2)}) async-start(bf16[1,256,2,512]{3,2,0,1:T(2,128)(2,1)} %bitcast.320), calls=%async_computation | async-start | bytes 1048576 | tf_op jit(solution)/shard_map/all_to_all | solution.py:68
  33.2 2.2 %cosine_multiply_fusion = (bf16[128,1,1024]{0,2,1:T(8,128)(2,1)S(1)}, bf16[128,1,1024]{0,2,1:T(8,128)(2,1)S(1)}) fusion(s32[128]{0:T(128)S(1)} %iota_add_fusion), kind=kLoop, calls=%fused_computation.80 | loop fusion | flops 2490368 | bytes 524800 | tf_op jit(solution)/shard_map/mul | solution.py:24
  39.8 1.9 %collective-permute-start.2 = (bf16[256,2,512]{2,0,1:T(8,128)(2,1)}, bf16[256,2,512]{2,0,1:T(8,128)(2,1)S(1)}, u32[]{:S(2)}, u32[]{:S(2)}) collective-permute-start(bf16[256,2,512]{2,0,1:T(8,128)(2,1)} %collective-permute-done.1), channel_id=1, source_target_pairs={{0,1},{1,0},{2,3},{3,2},{4,5},{5,4},{6,7},{7,6},{8,9},{9,8},{10,11... | collective-permute-start | bytes 1572872 | tf_op jit(solution)/shard_map/ppermute | solution.py:64
  41.7 1.5 %convolution_bitcast_fusion.1 = f32[256,2,512]{2,0,1:T(8,128)S(1)} fusion(bf16[256,1,256,2]{2,0,3,1:T(8,128)(2,1)S(1)} %get-tuple-element.48, bf16[256,1,256,2]{2,0,3,1:T(8,128)(2,1)S(1)} %get-tuple-element.47, bf16[256,2,512]{2,0,1:T(8,128)(2,1)} %collective-permute-done.1), kind=kOutput, calls=%fused_computation.18 | convolution fusion | flops 268697600 | bytes 2097152 | tf_op jit(solution)/shard_map/rqsp,spc->rqc/dot_general | solution.py:84
  43.2 1.5 %fusion.7 = f32[256,2,512]{2,0,1:T(8,128)S(1)} fusion(f32[256,2,512]{2,0,1:T(8,128)S(1)} %convolution_bitcast_fusion.1, f32[256,2,512]{2,0,1:T(8,128)S(1)} %convolution_bitcast_fusion.3, bf16[256,1,256,2]{2,0,3,1:T(8,128)(2,1)S(1)} %get-tuple-element.44, bf16[256,1,256,2]{2,0,3,1:T(8,128)(2,1)S(1)} %get-tuple-element.43, ...), kind=kOutput, calls=%fused_computation.22 | convolution fusion | flops 269221888 | bytes 4194304 | tf_op jit(solution)/shard_map/rqsp,spc->rqc/dot_general | solution.py:84
  45.2 1.3 %copy.65 = bf16[1,256,2,512]{3,2,0,1:T(2,128)(2,1)} copy(bf16[1,256,2,512]{3,1,2,0:T(8,128)(2,1)S(1)} %fusion.10) | data formatting | bytes 1048576 | tf_op jit(solution)/shard_map/broadcast_in_dim | solution.py:89
  53.8 7.4 %all-to-all-done = bf16[1,256,2,512]{3,2,0,1:T(2,128)(2,1)S(1)} async-done(((bf16[1,256,2,512]{3,2,0,1:T(2,128)(2,1)}), bf16[1,256,2,512]{3,2,0,1:T(2,128)(2,1)S(1)}, u32[]{:S(2)}, u32[]{:S(2)}) %all-to-all-start) | async-done | bytes 524320 | tf_op jit(solution)/shard_map/all_to_all | solution.py:68
  61.2 10.3 %all-to-all-start.1 = ((bf16[1,256,2,512]{3,2,0,1:T(2,128)(2,1)}), bf16[1,256,2,512]{3,2,0,1:T(2,128)(2,1)}, u32[]{:S(2)}, u32[]{:S(2)}) async-start(bf16[1,256,2,512]{3,2,0,1:T(2,128)(2,1)} %copy.65), calls=%async_computation.1 | async-start | bytes 1048576 | tf_op jit(solution)/shard_map/all_to_all | solution.py:90
  73.3 3.9 %convolution_convert_fusion = bf16[2048,768]{1,0:T(8,128)(2,1)} fusion(bf16[256,8,384]{2,0,1:T(8,128)(2,1)S(1)} %pad_maximum_fusion.1, bf16[192,768]{1,0:T(8,128)(2,1)S(1)} %get-tuple-element.17, bf16[192,768]{1,0:T(8,128)(2,1)S(1)} %get-tuple-element.18), kind=kOutput, calls=%fused_computation | convolution fusion | flops 1210712064 | bytes 5308416 | tf_op jit(solution)/shard_map/dot_general | solution.py:46
  77.1 3.8 %reshape.313 = bf16[3,2,128,2,1024]{4,1,0,3,2:T(2,128)(2,1)S(1)} reshape(bf16[3,2,128,2,8,128]{5,4,1,0,3,2:T(8,128)(2,1)} %bitcast.309) | data formatting | bytes 6291456 | tf_op jit(solution)/shard_map/reshape | solution.py:52
  80.9 6.1 %fusion.86 = (bf16[1,1,128,2,1024]{4,1,0,3,2:T(2,128)(2,1)}, bf16[1,1,128,2,1024]{4,1,0,3,2:T(2,128)(2,1)}, bf16[1,1,128,2,1024]{4,1,0,3,2:T(2,128)(2,1)}, bf16[...) fusion(bf16[3,2,128,2,1024]{4,1,0,3,2:T(2,128)(2,1)S(1)} %reshape.313), kind=kLoop, calls=%fused_computation.175 | loop fusion | bytes 6291456 | tf_op jit(solution)/shard_map/slice | solution.py:110
  87.4 1.4 %bitcast_convert_fusion.1 = bf16[1024,512]{1,0:T(8,128)(2,1)} fusion(bf16[128,1,2,512]{3,2,1,0:T(2,128)(2,1)S(1)} %get-tuple-element.29, bf16[128,1,1024]{0,2,1:T(8,128)(2,1)S(1)} %copy-done.15, bf16[128,1,1024]{0,2,1:T(8,128)(2,1)S(1)} %copy-done.13), kind=kOutput, calls=%fused_computation.9 | convolution fusion | flops 269221888 | bytes 1835008 | tf_op jit(solution)/shard_map/fpc,fpt->ct/dot_general | solution.py:99
  88.8 1.4 %bitcast_convert_fusion = bf16[1024,512]{1,0:T(8,128)(2,1)} fusion(bf16[128,1,2,512]{3,2,1,0:T(2,128)(2,1)S(1)} %get-tuple-element.30, bf16[128,1,1024]{0,2,1:T(8,128)(2,1)S(1)} %copy-done.15, bf16[128,1,1024]{0,2,1:T(8,128)(2,1)S(1)} %copy-done.13), kind=kOutput, calls=%fused_computation.5 | convolution fusion | flops 269221888 | bytes 1835008 | tf_op jit(solution)/shard_map/fpc,fpt->ct/dot_general | solution.py:99
  90.2 13.4 %all-to-all-done.1 = bf16[1,256,2,512]{3,2,0,1:T(2,128)(2,1)} async-done(((bf16[1,256,2,512]{3,2,0,1:T(2,128)(2,1)}), bf16[1,256,2,512]{3,2,0,1:T(2,128)(2,1)}, u32[]{:S(2)}, u32[]{:S(2)}) %all-to-all-start.1) | async-done | bytes 524320 | tf_op jit(solution)/shard_map/all_to_all | solution.py:90
  103.6 1.4 %fusion.88 = (bf16[128,1,2,512]{3,2,1,0:T(2,128)(2,1)S(1)}, bf16[128,1,2,512]{3,2,1,0:T(2,128)(2,1)S(1)}) fusion(bf16[128,2,2,512]{3,2,1,0:T(2,128)(2,1)} %bitcast.39), kind=kLoop, calls=%fused_computation.177 | loop fusion | bytes 1048576 | tf_op jit(solution)/shard_map/slice | solution.py:106
  106.0 3.6 %collective-permute-start.3 = (bf16[128,2,512]{0,2,1:T(8,128)(2,1)S(1)}, bf16[128,2,512]{0,2,1:T(8,128)(2,1)S(1)}, u32[]{:S(2)}, u32[]{:S(2)}) collective-permute-start(bf16[128,2,512]{0,2,1:T(8,128)(2,1)S(1)} %bitcast.319), channel_id=1, source_target_pairs={{0,4},{4,8},{8,12},{12,16},{16,20},{20,24},{24,28},{28,32},{32,36}... | collective-permute-start | bytes 786440 | tf_op jit(solution)/shard_map/ppermute | solution.py:103
  110.7 7.0 %collective-permute-start.4 = (bf16[128,2,512]{0,2,1:T(8,128)(2,1)S(1)}, bf16[128,2,512]{0,2,1:T(8,128)(2,1)S(1)}, u32[]{:S(2)}, u32[]{:S(2)}) collective-permute-start(bf16[128,2,512]{0,2,1:T(8,128)(2,1)S(1)} %bitcast.318), channel_id=1, source_target_pairs={{4,0},{8,4},{12,8},{16,12},{20,16},{24,20},{28,24},{32,28},{36,32}... | collective-permute-start | bytes 786440 | tf_op jit(solution)/shard_map/ppermute | solution.py:104
  118.6 1.4 %fusion.4 = bf16[1,512,1024]{1,2,0:T(8,128)(2,1)S(1)} fusion(bf16[128,2,512]{0,2,1:T(8,128)(2,1)S(1)} %collective-permute-done.3, f32[512,1024,1]{0,1,2:T(8,128)S(1)} %fusion.38, f32[512,1024,1]{0,1,2:T(8,128)S(1)} %fusion.39, bf16[1024,512]{1,0:T(8,128)(2,1)S(1)} %copy-done.10, bf16[1,1,128,2,1024]{4,1,0,3,2:T(2,128)(2,1)S(1)} %copy-done.1), kind=kOutput, calls=%fused_computation.15 | convolution fusion | flops 273678336 | bytes 7077888 | tf_op jit(solution)/shard_map/fpc,fpt->ct/dot_general | solution.py:99
  120.0 1.3 %collective-permute-done.4 = bf16[128,2,512]{0,2,1:T(8,128)(2,1)S(1)} collective-permute-done((bf16[128,2,512]{0,2,1:T(8,128)(2,1)S(1)}, bf16[128,2,512]{0,2,1:T(8,128)(2,1)S(1)}, u32[]{:S(2)}, u32[]{:S(2)}) %collective-permute-start.4) | collective-permute-done | bytes 262176 | tf_op jit(solution)/shard_map/ppermute | solution.py:104
  121.3 1.4 %fusion.5 = bf16[1,512,1024]{1,2,0:T(8,128)(2,1)S(1)} fusion(bf16[128,2,512]{0,2,1:T(8,128)(2,1)S(1)} %collective-permute-done.4, f32[512,1024,1]{0,1,2:T(8,128)S(1)} %fusion.36, f32[512,1024,1]{0,1,2:T(8,128)S(1)} %fusion.37, bf16[1024,512]{1,0:T(8,128)(2,1)S(1)} %copy-done.9, bf16[1,1,128,2,1024]{4,1,0,3,2:T(2,128)(2,1)S(1)} %copy-done), kind=kOutput, calls=%fused_computation.16 | convolution fusion | flops 273678336 | bytes 7077888 | tf_op jit(solution)/shard_map/fpc,fpt->ct/dot_general | solution.py:99
  122.9 2.4 %copy.78 = bf16[2,512,1024]{2,1,0:T(8,128)(2,1)} copy(bf16[2,512,1024]{1,2,0:T(8,128)(2,1)S(1)} %pad_maximum_fusion) | data formatting | bytes 4194304 | tf_op jit(solution)/shard_map/stack | solution.py:117
  (129 shorter events, 21.4 us)
Async XLA Ops:
  0.0 28.8 %copy-start.11 = (bf16[1,256,2,1024]{3,2,1,0:T(2,128)(2,1)S(1)}, bf16[1,256,2,1024]{3,2,1,0:T(2,128)(2,1)}, u32[]{:S(2)}) copy-start(bf16[1,256,2,1024]{3,2,1,0:T(2,128)(2,1)} %param.4) | copy-start | bytes 3145732
  2.0 37.8 %collective-permute-start.1 = (bf16[256,2,512]{2,0,1:T(8,128)(2,1)}, bf16[256,2,512]{2,0,1:T(8,128)(2,1)}, u32[]{:S(2)}, u32[]{:S(2)}) collective-permute-start(bf16[256,2,512]{2,0,1:T(8,128)(2,1)} %bitcast.308), channel_id=1, source_target_pairs={{0,2},{1,3},{2,0},{3,1},{4,6},{5,7},{6,4},{7,5},{8,10},{9,11},{10,... | collective-permute-start | bytes 1572872 | tf_op jit(solution)/shard_map/ppermute | solution.py:64
  6.2 37.0 %collective-permute-start = (bf16[256,2,512]{2,0,1:T(8,128)(2,1)}, bf16[256,2,512]{2,0,1:T(8,128)(2,1)}, u32[]{:S(2)}, u32[]{:S(2)}) collective-permute-start(bf16[256,2,512]{2,0,1:T(8,128)(2,1)} %bitcast.308), channel_id=1, source_target_pairs={{0,1},{1,0},{2,3},{3,2},{4,5},{5,4},{6,7},{7,6},{8,9},{9,8},{10,11... | collective-permute-start | bytes 1572872 | tf_op jit(solution)/shard_map/ppermute | solution.py:64
  8.1 53.1 %all-to-all-start = ((bf16[1,256,2,512]{3,2,0,1:T(2,128)(2,1)}), bf16[1,256,2,512]{3,2,0,1:T(2,128)(2,1)S(1)}, u32[]{:S(2)}, u32[]{:S(2)}) async-start(bf16[1,256,2,512]{3,2,0,1:T(2,128)(2,1)} %bitcast.320), calls=%async_computation | async-start | bytes 1048576 | tf_op jit(solution)/shard_map/all_to_all | solution.py:68
  37.3 1.4 %copy-start.17 = (bf16[256,256,1]{1,0,2:T(8,128)(2,1)S(1)}, bf16[256,256,1]{1,0,2:T(8,128)(2,1)}, u32[]{:S(2)}) copy-start(bf16[256,256,1]{1,0,2:T(8,128)(2,1)} %fusion.82) | copy-start | bytes 393220
  37.3 1.4 %copy-start.22 = (bf16[256,256,1]{1,0,2:T(8,128)(2,1)S(1)}, bf16[256,256,1]{1,0,2:T(8,128)(2,1)}, u32[]{:S(2)}) copy-start(bf16[256,256,1]{1,0,2:T(8,128)(2,1)} %get-tuple-element.37) | copy-start | bytes 393220
  39.8 5.0 %collective-permute-start.2 = (bf16[256,2,512]{2,0,1:T(8,128)(2,1)}, bf16[256,2,512]{2,0,1:T(8,128)(2,1)S(1)}, u32[]{:S(2)}, u32[]{:S(2)}) collective-permute-start(bf16[256,2,512]{2,0,1:T(8,128)(2,1)} %collective-permute-done.1), channel_id=1, source_target_pairs={{0,1},{1,0},{2,3},{3,2},{4,5},{5,4},{6,7},{7,6},{8,9},{9,8},{10,11... | collective-permute-start | bytes 1572872 | tf_op jit(solution)/shard_map/ppermute | solution.py:64
  44.7 1.8 %copy-start.25 = (s32[8]{0:T(128)S(1)}, s32[8]{0:T(128)}, u32[]{:S(2)}) copy-start(s32[8]{0:T(128)} %param.7) | copy-start | bytes 100
  44.7 5.7 %copy-start.24 = (f32[3,8,2]{1,2,0:T(2,128)S(1)}, f32[3,8,2]{1,2,0:T(2,128)}, u32[]{:S(2)}) copy-start(f32[3,8,2]{1,2,0:T(2,128)} %param.6) | copy-start | bytes 580
  61.2 10.6 %copy-start.7 = (bf16[1,256,2,512]{3,2,0,1:T(2,128)(2,1)}, bf16[1,256,2,512]{3,2,0,1:T(2,128)(2,1)S(1)}, u32[]{:S(2)}) copy-start(bf16[1,256,2,512]{3,2,0,1:T(2,128)(2,1)S(1)} %all-to-all-done) | copy-start | bytes 1572868
  61.2 42.4 %all-to-all-start.1 = ((bf16[1,256,2,512]{3,2,0,1:T(2,128)(2,1)}), bf16[1,256,2,512]{3,2,0,1:T(2,128)(2,1)}, u32[]{:S(2)}, u32[]{:S(2)}) async-start(bf16[1,256,2,512]{3,2,0,1:T(2,128)(2,1)} %copy.65), calls=%async_computation.1 | async-start | bytes 1048576 | tf_op jit(solution)/shard_map/all_to_all | solution.py:90
  80.9 6.1 %copy-start.8 = (bf16[1,256,2,512]{3,2,0,1:T(2,128)(2,1)S(1)}, bf16[1,256,2,512]{3,2,0,1:T(2,128)(2,1)}, u32[]{:S(2)}) copy-start(bf16[1,256,2,512]{3,2,0,1:T(2,128)(2,1)} %copy-done.7) | copy-start | bytes 1572868
  80.9 6.5 %copy-start.13 = (bf16[128,1,1024]{0,2,1:T(8,128)(2,1)S(1)}, bf16[128,1,1024]{0,2,1:T(8,128)(2,1)}, u32[]{:S(2)}) copy-start(bf16[128,1,1024]{0,2,1:T(8,128)(2,1)} %copy-done.12) | copy-start | bytes 786436
  80.9 6.5 %copy-start.15 = (bf16[128,1,1024]{0,2,1:T(8,128)(2,1)S(1)}, bf16[128,1,1024]{0,2,1:T(8,128)(2,1)}, u32[]{:S(2)}) copy-start(bf16[128,1,1024]{0,2,1:T(8,128)(2,1)} %copy-done.14) | copy-start | bytes 786436
  88.8 16.7 %copy-start.5 = (bf16[1,1,128,2,1024]{4,1,0,3,2:T(2,128)(2,1)S(1)}, bf16[1,1,128,2,1024]{4,1,0,3,2:T(2,128)(2,1)}, u32[]{:S(2)}) copy-start(bf16[1,1,128,2,1024]{4,1,0,3,2:T(2,128)(2,1)} %get-tuple-element.22) | copy-start | bytes 1572868
  105.0 4.6 %copy-start.4 = (bf16[1,1,128,2,1024]{4,1,0,3,2:T(2,128)(2,1)S(1)}, bf16[1,1,128,2,1024]{4,1,0,3,2:T(2,128)(2,1)}, u32[]{:S(2)}) copy-start(bf16[1,1,128,2,1024]{4,1,0,3,2:T(2,128)(2,1)} %get-tuple-element.23) | copy-start | bytes 1572868
  106.0 4.2 %copy-start.3 = (bf16[1,1,128,2,1024]{4,1,0,3,2:T(2,128)(2,1)S(1)}, bf16[1,1,128,2,1024]{4,1,0,3,2:T(2,128)(2,1)}, u32[]{:S(2)}) copy-start(bf16[1,1,128,2,1024]{4,1,0,3,2:T(2,128)(2,1)} %get-tuple-element.21) | copy-start | bytes 1572868
  106.0 12.6 %collective-permute-start.3 = (bf16[128,2,512]{0,2,1:T(8,128)(2,1)S(1)}, bf16[128,2,512]{0,2,1:T(8,128)(2,1)S(1)}, u32[]{:S(2)}, u32[]{:S(2)}) collective-permute-start(bf16[128,2,512]{0,2,1:T(8,128)(2,1)S(1)} %bitcast.319), channel_id=1, source_target_pairs={{0,4},{4,8},{8,12},{12,16},{16,20},{20,24},{24,28},{28,32},{32,36}... | collective-permute-start | bytes 786440 | tf_op jit(solution)/shard_map/ppermute | solution.py:103
  110.1 7.6 %copy-start.2 = (bf16[1,1,128,2,1024]{4,1,0,3,2:T(2,128)(2,1)S(1)}, bf16[1,1,128,2,1024]{4,1,0,3,2:T(2,128)(2,1)}, u32[]{:S(2)}) copy-start(bf16[1,1,128,2,1024]{4,1,0,3,2:T(2,128)(2,1)} %get-tuple-element.20) | copy-start | bytes 1572868
  110.7 7.9 %copy-start.1 = (bf16[1,1,128,2,1024]{4,1,0,3,2:T(2,128)(2,1)S(1)}, bf16[1,1,128,2,1024]{4,1,0,3,2:T(2,128)(2,1)}, u32[]{:S(2)}) copy-start(bf16[1,1,128,2,1024]{4,1,0,3,2:T(2,128)(2,1)} %get-tuple-element.19) | copy-start | bytes 1572868
  110.7 7.9 %copy-start.10 = (bf16[1024,512]{1,0:T(8,128)(2,1)S(1)}, bf16[1024,512]{1,0:T(8,128)(2,1)}, u32[]{:S(2)}) copy-start(bf16[1024,512]{1,0:T(8,128)(2,1)} %bitcast_convert_fusion.1) | copy-start | bytes 3145732
  110.7 10.6 %collective-permute-start.4 = (bf16[128,2,512]{0,2,1:T(8,128)(2,1)S(1)}, bf16[128,2,512]{0,2,1:T(8,128)(2,1)S(1)}, u32[]{:S(2)}, u32[]{:S(2)}) collective-permute-start(bf16[128,2,512]{0,2,1:T(8,128)(2,1)S(1)} %bitcast.318), channel_id=1, source_target_pairs={{4,0},{8,4},{12,8},{16,12},{20,16},{24,20},{28,24},{32,28},{36,32}... | collective-permute-start | bytes 786440 | tf_op jit(solution)/shard_map/ppermute | solution.py:104
  118.6 2.7 %copy-start = (bf16[1,1,128,2,1024]{4,1,0,3,2:T(2,128)(2,1)S(1)}, bf16[1,1,128,2,1024]{4,1,0,3,2:T(2,128)(2,1)}, u32[]{:S(2)}) copy-start(bf16[1,1,128,2,1024]{4,1,0,3,2:T(2,128)(2,1)} %get-tuple-element.24) | copy-start | bytes 1572868
  118.6 2.7 %copy-start.9 = (bf16[1024,512]{1,0:T(8,128)(2,1)S(1)}, bf16[1024,512]{1,0:T(8,128)(2,1)}, u32[]{:S(2)}) copy-start(bf16[1024,512]{1,0:T(8,128)(2,1)} %bitcast_convert_fusion) | copy-start | bytes 3145732
  (9 other events, 8.9 us)

commit v2 on v1

v2 whole, which is shorter than its diff:
```python
import math

import jax
import jax.numpy as jnp
from jax import lax
from jax.experimental import pallas as pl
from jax.experimental.layout import Layout, with_layout_constraint
from jax.experimental.pallas import tpu as pltpu
from jax.sharding import PartitionSpec as P


NT = 1024
BLOCK = 128
COLUMNS = 256


shrink_level = 0.5


def lookup_rows(frequency_index):
    harmonics = frequency_index.shape[0]
    recording_epochs = jnp.arange(NT)
    rotation_radians = (
        frequency_index[:, None] * recording_epochs[None, :] % NT
    ).astype(jnp.float32) * (2.0 * math.pi / NT)
    scale = 1.0 / math.sqrt(harmonics)
    return jnp.stack(
        [jnp.cos(rotation_radians) * scale, -jnp.sin(rotation_radians) * scale], axis=1
    ).astype(jnp.bfloat16).reshape(2 * harmonics, NT)


def band_matrix(weights_ref, delays_ref, neighbour, station, first):
    taps = delays_ref.shape[0]
    shape = (2 * BLOCK, BLOCK)
    before = lax.broadcasted_iota(jnp.int32, shape, 0)
    lag = lax.broadcasted_iota(jnp.int32, shape, 1) - before + BLOCK
    band = jnp.zeros(shape, jnp.float32)
    for k in range(taps):
        weight = weights_ref[(neighbour * taps + k) * 2 + station]
        band += jnp.where(lag == delays_ref[k], weight, 0.0)
    band = jnp.where(first & (before < BLOCK), 0.0, band)
    high = band.astype(jnp.bfloat16)
    return high, (band - high.astype(jnp.float32)).astype(jnp.bfloat16)


def tables_kernel(weights_ref, delays_ref, last_ref, here_ref, out_ref):
    station = pl.program_id(0)
    first = pl.program_id(1) == 0
    rows = here_ref.shape[0]
    window = jnp.concatenate([last_ref[...], here_ref[...]], axis=1)
    for neighbour in range(3):
        parts = band_matrix(weights_ref, delays_ref, neighbour, station, first)
        filtered = sum(
            jnp.dot(window, part, preferred_element_type=jnp.float32) for part in parts
        )
        out_ref[0, pl.ds(neighbour * rows, rows)] = filtered.astype(jnp.bfloat16)


def filtered_tables(table, weights, tap_delays):
    rows = table.shape[0]
    return pl.pallas_call(
        tables_kernel,
        grid=(2, NT // BLOCK),
        out_shape=jax.ShapeDtypeStruct((2, 3 * rows, NT), jnp.bfloat16),
        in_specs=[
            pl.BlockSpec(memory_space=pltpu.SMEM),
            pl.BlockSpec(memory_space=pltpu.SMEM),
            pl.BlockSpec((rows, BLOCK), lambda s, b: (0, jnp.maximum(b - 1, 0))),
            pl.BlockSpec((rows, BLOCK), lambda s, b: (0, b)),
        ],
        out_specs=pl.BlockSpec((1, 3 * rows, BLOCK), lambda s, b: (s, 0, b)),
        cost_estimate=pl.CostEstimate(
            flops=48 * rows * NT * BLOCK, bytes_accessed=16 * rows * NT, transcendentals=0
        ),
        name="tables",
    )(weights.reshape(-1), tap_delays, table, table)


def across_time(spectrum, basis):
    return lax.dot_general(
        spectrum, basis, (((0,), (0,)), ((), ())), preferred_element_type=jnp.float32
    )


def data_kernel(recorded_ref, table_ref, out_ref):
    out_ref[0] = across_time(recorded_ref[0], table_ref[...]).astype(jnp.bfloat16)


def data_part(recorded, table):
    _, rows, columns = recorded.shape
    return pl.pallas_call(
        data_kernel,
        grid=(2, columns // COLUMNS),
        out_shape=jax.ShapeDtypeStruct((2, columns, NT), jnp.bfloat16),
        in_specs=[
            pl.BlockSpec((1, rows, COLUMNS), lambda s, c: (s, 0, c)),
            pl.BlockSpec((rows, NT), lambda s, c: (0, 0)),
        ],
        out_specs=pl.BlockSpec((1, COLUMNS, NT), lambda s, c: (s, c, 0)),
        cost_estimate=pl.CostEstimate(
            flops=4 * rows * columns * NT, bytes_accessed=6 * columns * NT, transcendentals=0
        ),
        name="data",
    )(recorded, table)


def final_kernel(before_ref, first_ref, second_ref, after_ref, basis_ref, data_ref, out_ref):
    station = pl.program_id(0)

    def finish(refs):
        spectra = jnp.concatenate([ref[...] for ref in refs], axis=0)
        residual = data_ref[0].astype(jnp.float32) - across_time(spectra, basis_ref[0])
        shrunk = residual - jnp.clip(residual, -shrink_level, shrink_level)
        out_ref[0] = shrunk.astype(jnp.bfloat16)

    @pl.when(station == 0)
    def _():
        finish([before_ref, first_ref, second_ref])

    @pl.when(station == 1)
    def _():
        finish([first_ref, second_ref, after_ref])


def final_part(before, first, second, after, basis, data):
    rows, columns = before.shape
    spectra = pl.BlockSpec((rows, COLUMNS), lambda s, c: (0, c))
    return pl.pallas_call(
        final_kernel,
        grid=(2, columns // COLUMNS),
        out_shape=jax.ShapeDtypeStruct((2, columns, NT), jnp.bfloat16),
        in_specs=[
            spectra,
            spectra,
            spectra,
            spectra,
            pl.BlockSpec((1, 3 * rows, NT), lambda s, c: (s, 0, 0)),
            pl.BlockSpec((1, COLUMNS, NT), lambda s, c: (s, c, 0)),
        ],
        out_specs=pl.BlockSpec((1, COLUMNS, NT), lambda s, c: (s, c, 0)),
        cost_estimate=pl.CostEstimate(
            flops=12 * rows * columns * NT, bytes_accessed=12 * columns * NT, transcendentals=0
        ),
        name="final",
    )(before, first, second, after, basis, data)


def body(operator, recorded, filter_coefficients, tap_delays):
    local_rows = operator.shape[1]
    columns = recorded.shape[3]
    freq_count = lax.axis_size("freq")
    row_count = lax.axis_size("row")
    row = lax.axis_index("row")

    plain = Layout(major_to_minor=(0, 1, 2, 3))

    def across(value, mask):
        pairs = [(i, i ^ mask) for i in range(row_count)]
        return with_layout_constraint(lax.ppermute(value, "row", pairs), plain)

    recorded_traces = lax.all_to_all(
        recorded, "freq", split_axis=1, concat_axis=0, tiled=True
    )
    far = across(recorded, 2)
    near = across(recorded, 1)
    far_near = across(far, 1)

    planes = lax.optimization_barrier(operator[0].transpose(1, 0, 2))

    def product(mask, segment):
        real_part, imag_part = lax.dynamic_slice_in_dim(
            planes, (row ^ mask) * local_rows, local_rows, axis=2
        )
        block = jnp.stack(
            [jnp.stack([real_part, -imag_part]), jnp.stack([imag_part, real_part])]
        )
        return jnp.einsum(
            "qprs,spc->rqc", block, segment[0], preferred_element_type=jnp.float32
        )

    total = product(0, recorded) + product(1, near)
    total = total + product(2, far) + product(3, far_near)
    spectra = total.astype(jnp.bfloat16)[None]
    traces = lax.all_to_all(spectra, "freq", split_axis=1, concat_axis=0, tiled=True)

    frequency_index, weights, _ = lax.optimization_barrier(
        (jnp.arange(freq_count) + 1, filter_coefficients, spectra)
    )
    table = lookup_rows(frequency_index)
    basis = filtered_tables(table, weights, tap_delays)

    def by_station(gathered):
        return [gathered[:, s].reshape(2 * freq_count, columns) for s in range(2)]

    recorded_traces = jnp.stack(by_station(recorded_traces))
    data = data_part(recorded_traces, table)

    forward = [(i, i + 1) for i in range(freq_count - 1)]
    backward = [(i + 1, i) for i in range(freq_count - 1)]
    first, second = by_station(traces)
    before = lax.ppermute(second, "freq", forward)
    after = lax.ppermute(first, "freq", backward)
    return final_part(before, first, second, after, basis, data)


def solution(mesh):
    in_specs = (
        P("freq", "row", None, None),
        P("freq", "row", None, None),
        P(None, None, ("row", "freq")),
        P(),
    )
    out_specs = P(("row", "freq"), None, None)


    return jax.shard_map(body, mesh=mesh, in_specs=in_specs, out_specs=out_specs, check_vma=False)
```

time: 126 us -> 134 us (1.063)
  the two profiles are of different devices: /device:TPU:8 before, /device:TPU:2 now
where the time goes in v2:
time: 134 us; the launch traced here: 132 us
  blocking collectives  52.5 us (39%)
  Pallas kernels  25.7 us (19%)
  starting transfers between devices  25.4 us (19%)
  waiting for transfers between devices  15 us (11%)
  local copies, waits for them, and re-layouts  6.84 us (5%)
  other arithmetic  3.79 us (3%)
  matrix products  2.81 us (2%)
    all_to_all x1, blocking collectives, body(): lax.all_to_all(spectra, 'freq', split_axis=1, concat_axis=0, tiled=True)  52.5 us
    pallas_call x1, Pallas kernels, filtered_tables(): pl.pallas_call(tables_kernel, grid=(2, NT // BLOCK), out_shape=jax.ShapeD...  14.7 us
    ppermute x3, waiting for transfers between devices, across(): return with_layout_constraint(lax.ppermute(value, 'row', pairs), plain)  10.3 us
    ppermute x3, starting transfers between devices, across(): return with_layout_constraint(lax.ppermute(value, 'row', pairs), plain)  8.92 us
    all_to_all x1, starting transfers between devices, body(): lax.all_to_all(recorded, 'freq', split_axis=1, concat_axis=0, tiled=True)  8.5 us
    pallas_call x1, Pallas kernels, final_part(): pl.pallas_call(final_kernel, grid=(2, columns // COLUMNS), out_shape=jax....  6.73 us
    all_to_all x1, waiting for transfers between devices, body(): lax.all_to_all(recorded, 'freq', split_axis=1, concat_axis=0, tiled=True)  4.66 us
    ppermute x1, starting transfers between devices, body(): after = lax.ppermute(first, 'freq', backward)  4.58 us
  transfers between devices with their start and end apart: 6, of which 3 were waited for; matrix products, arithmetic and copies ran while one was open for 8% of the time, Pallas kernels for 14%

profile of v2, /device:TPU:2, one launch (start us, length us, event | category | flops | bytes accessed | tf_op | source)
XLA Modules:
  0.0 132.3 jit_solution(3554110376339508853)
XLA Ops:
  0.0 1.9 %collective-permute-start = (bf16[1,256,2,512]{3,2,1,0:T(2,128)(2,1)}, bf16[1,256,2,512]{3,2,1,0:T(2,128)(2,1)S(1)}, u32[]{:S(2)}, u32[]{:S(2)}) collective-permute-start(bf16[1,256,2,512]{3,2,1,0:T(2,128)(2,1)} %param.5), channel_id=1, source_target_pairs={{0,1},{1,0},{2,3},{3,2},{4,5},{5,4},{6,7},{7,6},{8,9},{9,8},{10,11... | collective-permute-start | bytes 1572872 | tf_op jit(solution)/shard_map/ppermute | solution.py:159
  1.9 5.1 %collective-permute-start.1 = (bf16[1,256,2,512]{3,2,1,0:T(2,128)(2,1)}, bf16[1,256,2,512]{3,2,1,0:T(2,128)(2,1)S(1)}, u32[]{:S(2)}, u32[]{:S(2)}) collective-permute-start(bf16[1,256,2,512]{3,2,1,0:T(2,128)(2,1)} %param.5), channel_id=1, source_target_pairs={{0,2},{1,3},{2,0},{3,1},{4,6},{5,7},{6,4},{7,5},{8,10},{9,11},{10,... | collective-permute-start | bytes 1572872 | tf_op jit(solution)/shard_map/ppermute | solution.py:159
  7.1 1.5 %copy.75 = bf16[1,256,2,1024]{3,1,2,0:T(8,128)(2,1)S(1)} copy(bf16[1,256,2,1024]{3,2,1,0:T(2,128)(2,1)} %param.4) | data formatting | bytes 2097152 | tf_op args[0]
  9.0 1.5 %convolution_bitcast_fusion.3 = f32[2,256,512]{2,1,0:T(8,128)S(1)} fusion(bf16[1,2,256,256]{3,2,1,0:T(8,128)(2,1)S(1)} %get-tuple-element.36, bf16[1,2,256,256]{3,2,1,0:T(8,128)(2,1)S(1)} %get-tuple-element.35, bf16[256,2,512]{2,1,0:T(2,128)(2,1)} %bitcast.4), kind=kOutput, calls=%fused_computation.3 | convolution fusion | flops 268697600 | bytes 2097152 | tf_op jit(solution)/shard_map/qprs,spc->rqc/dot_general | solution.py:177
  10.5 9.4 %collective-permute-done.1 = bf16[1,256,2,512]{3,2,1,0:T(2,128)(2,1)S(1)} collective-permute-done((bf16[1,256,2,512]{3,2,1,0:T(2,128)(2,1)}, bf16[1,256,2,512]{3,2,1,0:T(2,128)(2,1)S(1)}, u32[]{:S(2)}, u32[]{:S(2)}) %collective-permute-start.1) | collective-permute-done | bytes 524320 | tf_op jit(solution)/shard_map/ppermute | solution.py:159
  19.9 1.9 %collective-permute-start.2 = (bf16[1,256,2,512]{3,2,1,0:T(2,128)(2,1)S(1)}, bf16[1,256,2,512]{3,2,1,0:T(2,128)(2,1)S(1)}, u32[]{:S(2)}, u32[]{:S(2)}) collective-permute-start(bf16[1,256,2,512]{3,2,1,0:T(2,128)(2,1)S(1)} %collective-permute-done.1), channel_id=1, source_target_pairs={{0,1},{1,0},{2,3},{3,2},{4,5},{5,4},{6,7},{7,6},{8,9},{9,8},{10,11... | collective-permute-start | bytes 1572872 | tf_op jit(solution)/shard_map/ppermute | solution.py:159
  22.3 0.4 fusion.1
  22.7 0.9 collective-permute-done.2
  24.1 0.5 copy.42
  24.7 52.5 %all_to_all.24 = bf16[1,256,2,512]{3,2,0,1:T(2,128)(2,1)S(1)} all-to-all(bf16[1,256,2,512]{3,2,0,1:T(2,128)(2,1)S(1)} %copy.42), channel_id=1, replica_groups=mesh['freq'=128,'row'=4] {'freq'}, dimensions={1} | all-to-all | bytes 1048576 | tf_op jit(solution)/shard_map/all_to_all | solution.py:184
  77.2 8.5 %all-to-all-start.1 = ((bf16[1,256,2,512]{3,2,0,1:T(2,128)(2,1)}), bf16[1,256,2,512]{3,2,0,1:T(2,128)(2,1)S(1)}, u32[]{:S(2)}, u32[]{:S(2)}) async-start(bf16[1,256,2,512]{3,2,0,1:T(2,128)(2,1)} %bitcast.30), calls=%async_computation.1 | async-start | bytes 1048576 | tf_op jit(solution)/shard_map/all_to_all | solution.py:161
  85.8 0.6 reshape.112.weights_ref
  86.4 2.4 %multiply_convert_fusion.1 = (bf16[128,1,1024]{2,0,1:T(8,128)(2,1)S(1)}, bf16[128,1,1024]{2,0,1:T(8,128)(2,1)S(1)}) fusion(s32[128]{0:T(128)S(1)} %iota_add_fusion), kind=kLoop, calls=%fused_computation.39 | loop fusion | flops 2490368 | bytes 524800 | tf_op jit(solution)/shard_map/convert
  88.9 0.5 copy.46
  89.5 1.0 convert_element_type.28.last_ref.here_ref.table_ref
  90.5 14.7 %tables.1.basis_ref = bf16[2,768,1024]{2,1,0:T(8,128)(2,1)} custom-call(f32[48]{0:T(128)} %reshape.112.weights_ref, s32[8]{0:T(128)} %delays_ref.1, bf16[256,1024]{1,0:T(8,128)(2,1)} %convert_element_type.28.last_ref.here_ref.table_ref, bf16[256,1024]{1,0:T(8,128)(2,1)} %convert_element_type.28.last_ref.here_ref.table_ref), custom_call_target="tpu_custom_call" | custom-call | flops 1610612736 | bytes 4194304 | tf_op jit(solution)/shard_map/tables/pallas_call | solution.py:61
  105.7 3.4 %collective-permute-start.3 = (bf16[256,512]{1,0:T(8,128)(2,1)S(1)}, bf16[256,512]{1,0:T(8,128)(2,1)S(1)}, u32[]{:S(2)}, u32[]{:S(2)}) collective-permute-start(bf16[256,512]{1,0:T(8,128)(2,1)S(1)} %reshape_squeeze.6.second_ref), channel_id=1, source_target_pairs={{0,4},{4,8},{8,12},{12,16},{16,20},{20,24},{24,28},{28,32},{32,36}... | collective-permute-start | bytes 786440 | tf_op jit(solution)/shard_map/ppermute | solution.py:201
  109.1 4.6 %collective-permute-start.4 = (bf16[256,512]{1,0:T(8,128)(2,1)S(1)}, bf16[256,512]{1,0:T(8,128)(2,1)S(1)}, u32[]{:S(2)}, u32[]{:S(2)}) collective-permute-start(bf16[256,512]{1,0:T(8,128)(2,1)S(1)} %reshape_squeeze.7.first_ref), channel_id=1, source_target_pairs={{4,0},{8,4},{12,8},{16,12},{20,16},{24,20},{28,24},{32,28},{36,32}... | collective-permute-start | bytes 786440 | tf_op jit(solution)/shard_map/ppermute | solution.py:202
  113.7 4.7 %all-to-all-done.1 = bf16[1,256,2,512]{3,2,0,1:T(2,128)(2,1)S(1)} async-done(((bf16[1,256,2,512]{3,2,0,1:T(2,128)(2,1)}), bf16[1,256,2,512]{3,2,0,1:T(2,128)(2,1)S(1)}, u32[]{:S(2)}, u32[]{:S(2)}) %all-to-all-start.1) | async-done | bytes 524320 | tf_op jit(solution)/shard_map/all_to_all | solution.py:161
  118.9 0.9 pad_maximum_fusion.1.recorded_ref
  119.8 4.3 %data.1.data_ref = bf16[2,512,1024]{2,1,0:T(8,128)(2,1)} custom-call(bf16[2,256,512]{2,1,0:T(8,128)(2,1)} %pad_maximum_fusion.1.recorded_ref, bf16[256,1024]{1,0:T(8,128)(2,1)} %convert_element_type.28.last_ref.here_ref.table_ref), custom_call_target="tpu_custom_call" | custom-call | flops 536870912 | bytes 3145728 | tf_op jit(solution)/shard_map/data/pallas_call | solution.py:91
  124.1 0.7 copy-done.2
  124.8 0.7 copy-done.3
  125.5 6.7 %final.1 = bf16[2,512,1024]{2,1,0:T(8,128)(2,1)} custom-call(bf16[256,512]{1,0:T(8,128)(2,1)} %copy-done.2, bf16[256,512]{1,0:T(8,128)(2,1)} %copy-done, bf16[256,512]{1,0:T(8,128)(2,1)} %copy-done.1, bf16[256,512]{1,0:T(8,128)(2,1)} %copy-done.3, bf16[2,768,1024]{2,1,0:T(8,128)(2,1)} %tables.1.basis_ref, bf16[2,512,1024]{2,1,0:T(8,128)(2,1)} %data.1.data_ref), custom_call_target="tpu_custom_call" | custom-call | flops 1610612736 | bytes 6291456 | tf_op jit(solution)/shard_map/final/pallas_call | solution.py:128
  (27 shorter events, 2.6 us)
Async XLA Ops:
  0.0 22.3 %collective-permute-start = (bf16[1,256,2,512]{3,2,1,0:T(2,128)(2,1)}, bf16[1,256,2,512]{3,2,1,0:T(2,128)(2,1)S(1)}, u32[]{:S(2)}, u32[]{:S(2)}) collective-permute-start(bf16[1,256,2,512]{3,2,1,0:T(2,128)(2,1)} %param.5), channel_id=1, source_target_pairs={{0,1},{1,0},{2,3},{3,2},{4,5},{5,4},{6,7},{7,6},{8,9},{9,8},{10,11... | collective-permute-start | bytes 1572872 | tf_op jit(solution)/shard_map/ppermute | solution.py:159
  1.9 17.9 %collective-permute-start.1 = (bf16[1,256,2,512]{3,2,1,0:T(2,128)(2,1)}, bf16[1,256,2,512]{3,2,1,0:T(2,128)(2,1)S(1)}, u32[]{:S(2)}, u32[]{:S(2)}) collective-permute-start(bf16[1,256,2,512]{3,2,1,0:T(2,128)(2,1)} %param.5), channel_id=1, source_target_pairs={{0,2},{1,3},{2,0},{3,1},{4,6},{5,7},{6,4},{7,5},{8,10},{9,11},{10,... | collective-permute-start | bytes 1572872 | tf_op jit(solution)/shard_map/ppermute | solution.py:159
  19.9 3.8 %collective-permute-start.2 = (bf16[1,256,2,512]{3,2,1,0:T(2,128)(2,1)S(1)}, bf16[1,256,2,512]{3,2,1,0:T(2,128)(2,1)S(1)}, u32[]{:S(2)}, u32[]{:S(2)}) collective-permute-start(bf16[1,256,2,512]{3,2,1,0:T(2,128)(2,1)S(1)} %collective-permute-done.1), channel_id=1, source_target_pairs={{0,1},{1,0},{2,3},{3,2},{4,5},{5,4},{6,7},{7,6},{8,9},{9,8},{10,11... | collective-permute-start | bytes 1572872 | tf_op jit(solution)/shard_map/ppermute | solution.py:159
  24.1 61.6 %copy-start.4 = (f32[3,8,2]{1,2,0:T(2,128)S(1)}, f32[3,8,2]{1,2,0:T(2,128)}, u32[]{:S(2)}) copy-start(f32[3,8,2]{1,2,0:T(2,128)} %param.6) | copy-start | bytes 580
  77.2 41.2 %all-to-all-start.1 = ((bf16[1,256,2,512]{3,2,0,1:T(2,128)(2,1)}), bf16[1,256,2,512]{3,2,0,1:T(2,128)(2,1)S(1)}, u32[]{:S(2)}, u32[]{:S(2)}) async-start(bf16[1,256,2,512]{3,2,0,1:T(2,128)(2,1)} %bitcast.30), calls=%async_computation.1 | async-start | bytes 1048576 | tf_op jit(solution)/shard_map/all_to_all | solution.py:161
  105.6 18.5 %copy-start = (bf16[256,512]{1,0:T(8,128)(2,1)}, bf16[256,512]{1,0:T(8,128)(2,1)S(1)}, u32[]{:S(2)}) copy-start(bf16[256,512]{1,0:T(8,128)(2,1)S(1)} %reshape_squeeze.7.first_ref) | copy-start | bytes 786436
  105.7 18.4 %copy-start.1 = (bf16[256,512]{1,0:T(8,128)(2,1)}, bf16[256,512]{1,0:T(8,128)(2,1)S(1)}, u32[]{:S(2)}) copy-start(bf16[256,512]{1,0:T(8,128)(2,1)S(1)} %reshape_squeeze.6.second_ref) | copy-start | bytes 786436
  105.7 18.4 %collective-permute-start.3 = (bf16[256,512]{1,0:T(8,128)(2,1)S(1)}, bf16[256,512]{1,0:T(8,128)(2,1)S(1)}, u32[]{:S(2)}, u32[]{:S(2)}) collective-permute-start(bf16[256,512]{1,0:T(8,128)(2,1)S(1)} %reshape_squeeze.6.second_ref), channel_id=1, source_target_pairs={{0,4},{4,8},{8,12},{12,16},{16,20},{20,24},{24,28},{28,32},{32,36}... | collective-permute-start | bytes 786440 | tf_op jit(solution)/shard_map/ppermute | solution.py:201
  109.1 15.0 %collective-permute-start.4 = (bf16[256,512]{1,0:T(8,128)(2,1)S(1)}, bf16[256,512]{1,0:T(8,128)(2,1)S(1)}, u32[]{:S(2)}, u32[]{:S(2)}) collective-permute-start(bf16[256,512]{1,0:T(8,128)(2,1)S(1)} %reshape_squeeze.7.first_ref), channel_id=1, source_target_pairs={{4,0},{8,4},{12,8},{16,12},{20,16},{24,20},{28,24},{32,28},{36,32}... | collective-permute-start | bytes 786440 | tf_op jit(solution)/shard_map/ppermute | solution.py:202
  124.1 0.7 copy-start.2
  124.8 0.7 copy-start.3

commit v3 on v2

--- a/solution.py
+++ b/solution.py
@@ -29,31 +29,39 @@
     ).astype(jnp.bfloat16).reshape(2 * harmonics, NT)
 
 
-def band_matrix(weights_ref, delays_ref, neighbour, station, first):
-    taps = delays_ref.shape[0]
-    shape = (2 * BLOCK, BLOCK)
-    before = lax.broadcasted_iota(jnp.int32, shape, 0)
-    lag = lax.broadcasted_iota(jnp.int32, shape, 1) - before + BLOCK
-    band = jnp.zeros(shape, jnp.float32)
-    for k in range(taps):
-        weight = weights_ref[(neighbour * taps + k) * 2 + station]
-        band += jnp.where(lag == delays_ref[k], weight, 0.0)
-    band = jnp.where(first & (before < BLOCK), 0.0, band)
-    high = band.astype(jnp.bfloat16)
-    return high, (band - high.astype(jnp.float32)).astype(jnp.bfloat16)
-
-
-def tables_kernel(weights_ref, delays_ref, last_ref, here_ref, out_ref):
+def tables_kernel(weights_ref, delays_ref, last_ref, here_ref, out_ref, high_ref, low_ref):
     station = pl.program_id(0)
     first = pl.program_id(1) == 0
     rows = here_ref.shape[0]
-    window = jnp.concatenate([last_ref[...], here_ref[...]], axis=1)
-    for neighbour in range(3):
-        parts = band_matrix(weights_ref, delays_ref, neighbour, station, first)
-        filtered = sum(
-            jnp.dot(window, part, preferred_element_type=jnp.float32) for part in parts
-        )
-        out_ref[0, pl.ds(neighbour * rows, rows)] = filtered.astype(jnp.bfloat16)
+    taps = delays_ref.shape[0]
+
+    @pl.when(first)
+    def _():
+        shape = (2 * BLOCK, BLOCK)
+        lag = (
+            lax.broadcasted_iota(jnp.int32, shape, 1)
+            - lax.broadcasted_iota(jnp.int32, shape, 0)
+            + BLOCK
+        )
+        for part in range(3):
+            neighbour = lax.rem(part + 1 - station, 3)
+            band = jnp.zeros(shape, jnp.float32)
+            for k in range(taps):
+                weight = weights_ref[(neighbour * taps + k) * 2 + station]
+                band += jnp.where(lag == delays_ref[k], weight, 0.0)
+            high = band.astype(jnp.bfloat16)
+            at = pl.ds(part * BLOCK, BLOCK)
+            high_ref[:, at] = high
+            low_ref[:, at] = (band - high.astype(jnp.float32)).astype(jnp.bfloat16)
+
+    last = jnp.where(first, jnp.zeros_like(last_ref[...]), last_ref[...])
+    window = jnp.concatenate([last, here_ref[...]], axis=1)
+    filtered = jnp.dot(window, high_ref[...], preferred_element_type=jnp.float32)
+    filtered += jnp.dot(window, low_ref[...], preferred_element_type=jnp.float32)
+    for part in range(3):
+        out_ref[0, pl.ds(part * rows, rows)] = filtered[
+            :, part * BLOCK : (part + 1) * BLOCK
+        ].astype(jnp.bfloat16)
 
 
 def filtered_tables(table, weights, tap_delays):
@@ -69,6 +77,7 @@
             pl.BlockSpec((rows, BLOCK), lambda s, b: (0, b)),
         ],
         out_specs=pl.BlockSpec((1, 3 * rows, BLOCK), lambda s, b: (s, 0, b)),
+        scratch_shapes=[pltpu.VMEM((2 * BLOCK, 3 * BLOCK), jnp.bfloat16)] * 2,
         cost_estimate=pl.CostEstimate(
             flops=48 * rows * NT * BLOCK, bytes_accessed=16 * rows * NT, transcendentals=0
         ),
@@ -104,25 +113,40 @@
     )(recorded, table)
 
 
-def final_kernel(before_ref, first_ref, second_ref, after_ref, basis_ref, data_ref, out_ref):
-    station = pl.program_id(0)
-
-    def finish(refs):
-        spectra = jnp.concatenate([ref[...] for ref in refs], axis=0)
-        residual = data_ref[0].astype(jnp.float32) - across_time(spectra, basis_ref[0])
-        shrunk = residual - jnp.clip(residual, -shrink_level, shrink_level)
-        out_ref[0] = shrunk.astype(jnp.bfloat16)
-
-    @pl.when(station == 0)
-    def _():
-        finish([before_ref, first_ref, second_ref])
-
-    @pl.when(station == 1)
-    def _():
-        finish([first_ref, second_ref, after_ref])
-
-
-def final_part(before, first, second, after, basis, data):
+def own_kernel(first_ref, second_ref, basis_ref, data_ref, out_ref):
+    spectra = jnp.concatenate([first_ref[...], second_ref[...]], axis=0)
+    out_ref[0] = data_ref[0].astype(jnp.float32) - across_time(spectra, basis_ref[0])
+
+
+def own_part(first, second, basis, data):
+    rows, columns = first.shape
+    spectra = pl.BlockSpec((rows, COLUMNS), lambda s, c: (0, c))
+    return pl.pallas_call(
+        own_kernel,
+        grid=(2, columns // COLUMNS),
+        out_shape=jax.ShapeDtypeStruct((2, columns, NT), jnp.float32),
+        in_specs=[
+            spectra,
+            spectra,
+            pl.BlockSpec((1, 2 * rows, NT), lambda s, c: (s, 0, 0)),
+            pl.BlockSpec((1, COLUMNS, NT), lambda s, c: (s, c, 0)),
+        ],
+        out_specs=pl.BlockSpec((1, COLUMNS, NT), lambda s, c: (s, c, 0)),
+        cost_estimate=pl.CostEstimate(
+            flops=8 * rows * columns * NT, bytes_accessed=12 * columns * NT, transcendentals=0
+        ),
+        name="own",
+    )(first, second, basis, data)
+
+
+def final_kernel(before_ref, after_ref, basis_ref, rest_ref, out_ref):
+    halo = jnp.where(pl.program_id(0) == 0, before_ref[...], after_ref[...])
+    residual = rest_ref[0] - across_time(halo, basis_ref[0])
+    shrunk = residual - jnp.clip(residual, -shrink_level, shrink_level)
+    out_ref[0] = shrunk.astype(jnp.bfloat16)
+
+
+def final_part(before, after, basis, rest):
     rows, columns = before.shape
     spectra = pl.BlockSpec((rows, COLUMNS), lambda s, c: (0, c))
     return pl.pallas_call(
@@ -132,17 +156,15 @@
         in_specs=[
             spectra,
             spectra,
-            spectra,
-            spectra,
-            pl.BlockSpec((1, 3 * rows, NT), lambda s, c: (s, 0, 0)),
+            pl.BlockSpec((1, rows, NT), lambda s, c: (s, 2, 0)),
             pl.BlockSpec((1, COLUMNS, NT), lambda s, c: (s, c, 0)),
         ],
         out_specs=pl.BlockSpec((1, COLUMNS, NT), lambda s, c: (s, c, 0)),
         cost_estimate=pl.CostEstimate(
-            flops=12 * rows * columns * NT, bytes_accessed=12 * columns * NT, transcendentals=0
+            flops=4 * rows * columns * NT, bytes_accessed=14 * columns * NT, transcendentals=0
         ),
         name="final",
-    )(before, first, second, after, basis, data)
+    )(before, after, basis, rest)
 
 
 def body(operator, recorded, filter_coefficients, tap_delays):
@@ -183,11 +205,8 @@
     spectra = total.astype(jnp.bfloat16)[None]
     traces = lax.all_to_all(spectra, "freq", split_axis=1, concat_axis=0, tiled=True)
 
-    frequency_index, weights, _ = lax.optimization_barrier(
-        (jnp.arange(freq_count) + 1, filter_coefficients, spectra)
-    )
-    table = lookup_rows(frequency_index)
-    basis = filtered_tables(table, weights, tap_delays)
+    table = lookup_rows(jnp.arange(freq_count) + 1)
+    basis = filtered_tables(table, filter_coefficients, tap_delays)
 
     def by_station(gathered):
         return [gathered[:, s].reshape(2 * freq_count, columns) for s in range(2)]
@@ -200,7 +219,8 @@
     first, second = by_station(traces)
     before = lax.ppermute(second, "freq", forward)
     after = lax.ppermute(first, "freq", backward)
-    return final_part(before, first, second, after, basis, data)
+    rest = own_part(first, second, basis, data)
+    return final_part(before, after, basis, rest)
 
 
 def solution(mesh):

time: 134 us -> 126 us (0.940)
  the two profiles are of different devices: /device:TPU:2 before, /device:TPU:24 now
where the time goes in v3:
time: 126 us; the launch traced here: 125 us
  starting transfers between devices  48.8 us (39%)
  waiting for transfers between devices  33.6 us (27%)
  Pallas kernels  28.3 us (22%)
  local copies, waits for them, and re-layouts  8.3 us (7%)
  other arithmetic  3.77 us (3%)
  matrix products  1.77 us (1%)
    all_to_all x1, starting transfers between devices, body(): lax.all_to_all(recorded, 'freq', split_axis=1, concat_axis=0, tiled=True)  20.7 us
    all_to_all x1, waiting for transfers between devices, body(): lax.all_to_all(spectra, 'freq', split_axis=1, concat_axis=0, tiled=True)  14.4 us
    ppermute x3, waiting for transfers between devices, across(): return with_layout_constraint(lax.ppermute(value, 'row', pairs), plain)  12.7 us
    pallas_call x1, Pallas kernels, filtered_tables(): pl.pallas_call(tables_kernel, grid=(2, NT // BLOCK), out_shape=jax.ShapeD...  12.5 us
    all_to_all x1, starting transfers between devices, body(): lax.all_to_all(spectra, 'freq', split_axis=1, concat_axis=0, tiled=True)  11.1 us
    ppermute x1, starting transfers between devices, body(): after = lax.ppermute(first, 'freq', backward)  7 us
    ppermute x3, starting transfers between devices, across(): return with_layout_constraint(lax.ppermute(value, 'row', pairs), plain)  6.98 us
    all_to_all x1, waiting for transfers between devices, body(): lax.all_to_all(recorded, 'freq', split_axis=1, concat_axis=0, tiled=True)  6.47 us
  transfers between devices with their start and end apart: 7, of which 4 were waited for; matrix products, arithmetic and copies ran while one was open for 9% of the time, Pallas kernels for 18%

profile of v3, /device:TPU:24, one launch (start us, length us, event | category | flops | bytes accessed | tf_op | source)
XLA Modules:
  0.0 124.8 jit_solution(1673035260967028007)
XLA Ops:
  0.0 20.7 %all-to-all-start.1 = ((bf16[1,256,2,512]{3,2,0,1:T(2,128)(2,1)}), bf16[1,256,2,512]{3,2,0,1:T(2,128)(2,1)S(1)}, u32[]{:S(2)}, u32[]{:S(2)}) async-start(bf16[1,256,2,512]{3,2,0,1:T(2,128)(2,1)} %bitcast.86), calls=%async_computation.1 | async-start | bytes 1048576 | tf_op jit(solution)/shard_map/all_to_all | solution.py:183
  20.7 3.1 %collective-permute-start.1 = (bf16[1,256,2,512]{3,2,1,0:T(2,128)(2,1)}, bf16[1,256,2,512]{3,2,1,0:T(2,128)(2,1)S(1)}, u32[]{:S(2)}, u32[]{:S(2)}) collective-permute-start(bf16[1,256,2,512]{3,2,1,0:T(2,128)(2,1)} %param.5), channel_id=1, source_target_pairs={{0,2},{1,3},{2,0},{3,1},{4,6},{5,7},{6,4},{7,5},{8,10},{9,11},{10,... | collective-permute-start | bytes 1572872 | tf_op jit(solution)/shard_map/ppermute | solution.py:181
  23.8 1.9 %collective-permute-start = (bf16[1,256,2,512]{3,2,1,0:T(2,128)(2,1)}, bf16[1,256,2,512]{3,2,1,0:T(2,128)(2,1)S(1)}, u32[]{:S(2)}, u32[]{:S(2)}) collective-permute-start(bf16[1,256,2,512]{3,2,1,0:T(2,128)(2,1)} %param.5), channel_id=1, source_target_pairs={{0,1},{1,0},{2,3},{3,2},{4,5},{5,4},{6,7},{7,6},{8,9},{9,8},{10,11... | collective-permute-start | bytes 1572872 | tf_op jit(solution)/shard_map/ppermute | solution.py:181
  25.8 1.5 %copy.75 = bf16[1,256,2,1024]{3,1,2,0:T(8,128)(2,1)S(1)} copy(bf16[1,256,2,1024]{3,2,1,0:T(2,128)(2,1)} %param.4) | data formatting | bytes 2097152 | tf_op args[0]
  27.7 0.6 copy-done.2
  28.8 11.8 %collective-permute-done.1 = bf16[1,256,2,512]{3,2,1,0:T(2,128)(2,1)S(1)} collective-permute-done((bf16[1,256,2,512]{3,2,1,0:T(2,128)(2,1)}, bf16[1,256,2,512]{3,2,1,0:T(2,128)(2,1)S(1)}, u32[]{:S(2)}, u32[]{:S(2)}) %collective-permute-start.1) | collective-permute-done | bytes 524320 | tf_op jit(solution)/shard_map/ppermute | solution.py:181
  40.6 1.9 %collective-permute-start.2 = (bf16[1,256,2,512]{3,2,1,0:T(2,128)(2,1)S(1)}, bf16[1,256,2,512]{3,2,1,0:T(2,128)(2,1)S(1)}, u32[]{:S(2)}, u32[]{:S(2)}) collective-permute-start(bf16[1,256,2,512]{3,2,1,0:T(2,128)(2,1)S(1)} %collective-permute-done.1), channel_id=1, source_target_pairs={{0,1},{1,0},{2,3},{3,2},{4,5},{5,4},{6,7},{7,6},{8,9},{9,8},{10,11... | collective-permute-start | bytes 1572872 | tf_op jit(solution)/shard_map/ppermute | solution.py:181
  43.5 0.9 collective-permute-done.2
  44.8 1.3 %copy.42 = bf16[1,256,2,512]{3,2,0,1:T(2,128)(2,1)} copy(bf16[1,256,2,512]{3,1,2,0:T(8,128)(2,1)S(1)} %fusion.4) | data formatting | bytes 1048576 | tf_op jit(solution)/shard_map/broadcast_in_dim | solution.py:205
  46.2 6.5 %all-to-all-done.1 = bf16[1,256,2,512]{3,2,0,1:T(2,128)(2,1)S(1)} async-done(((bf16[1,256,2,512]{3,2,0,1:T(2,128)(2,1)}), bf16[1,256,2,512]{3,2,0,1:T(2,128)(2,1)S(1)}, u32[]{:S(2)}, u32[]{:S(2)}) %all-to-all-start.1) | async-done | bytes 524320 | tf_op jit(solution)/shard_map/all_to_all | solution.py:183
  52.6 11.1 %all-to-all-start = ((bf16[1,256,2,512]{3,2,0,1:T(2,128)(2,1)}), bf16[1,256,2,512]{3,2,0,1:T(2,128)(2,1)S(1)}, u32[]{:S(2)}, u32[]{:S(2)}) async-start(bf16[1,256,2,512]{3,2,0,1:T(2,128)(2,1)} %copy.42), calls=%async_computation | async-start | bytes 1048576 | tf_op jit(solution)/shard_map/all_to_all | solution.py:206
  63.8 2.5 %multiply_convert_fusion.1 = (bf16[128,1,1024]{2,0,1:T(8,128)(2,1)S(1)}, bf16[128,1,1024]{2,0,1:T(8,128)(2,1)S(1)}) fusion(s32[128]{0:T(128)S(1)} %iota_add_fusion), kind=kLoop, calls=%fused_computation.39 | loop fusion | flops 2490368 | bytes 524800 | tf_op jit(solution)/shard_map/convert
  66.9 1.0 convert_element_type.30.last_ref.here_ref.table_ref
  68.0 0.7 reshape.118.weights_ref
  68.6 12.5 %tables.1.basis_ref = bf16[2,768,1024]{2,1,0:T(8,128)(2,1)} custom-call(f32[48]{0:T(128)} %reshape.118.weights_ref, s32[8]{0:T(128)} %delays_ref.1, bf16[256,1024]{1,0:T(8,128)(2,1)} %convert_element_type.30.last_ref.here_ref.table_ref, bf16[256,1024]{1,0:T(8,128)(2,1)} %convert_element_type.30.last_ref.here_ref.table_ref), custom_call_target="tpu_custom_call" | custom-call | flops 1610612736 | bytes 4194304 | tf_op jit(solution)/shard_map/tables/pallas_call | solution.py:69
  81.7 14.4 %all-to-all-done = bf16[1,256,2,512]{3,2,0,1:T(2,128)(2,1)S(1)} async-done(((bf16[1,256,2,512]{3,2,0,1:T(2,128)(2,1)}), bf16[1,256,2,512]{3,2,0,1:T(2,128)(2,1)S(1)}, u32[]{:S(2)}, u32[]{:S(2)}) %all-to-all-start) | async-done | bytes 524320 | tf_op jit(solution)/shard_map/all_to_all | solution.py:206
  96.7 3.1 %collective-permute-start.3 = (bf16[256,512]{1,0:T(8,128)(2,1)S(1)}, bf16[256,512]{1,0:T(8,128)(2,1)S(1)}, u32[]{:S(2)}, u32[]{:S(2)}) collective-permute-start(bf16[256,512]{1,0:T(8,128)(2,1)S(1)} %reshape_squeeze.6.second_ref), channel_id=1, source_target_pairs={{0,4},{4,8},{8,12},{12,16},{16,20},{20,24},{24,28},{28,32},{32,36}... | collective-permute-start | bytes 786440 | tf_op jit(solution)/shard_map/ppermute | solution.py:220
  99.7 7.0 %collective-permute-start.4 = (bf16[256,512]{1,0:T(8,128)(2,1)S(1)}, bf16[256,512]{1,0:T(8,128)(2,1)S(1)}, u32[]{:S(2)}, u32[]{:S(2)}) collective-permute-start(bf16[256,512]{1,0:T(8,128)(2,1)S(1)} %reshape_squeeze.7.first_ref), channel_id=1, source_target_pairs={{4,0},{8,4},{12,8},{16,12},{20,16},{24,20},{28,24},{32,28},{36,32}... | collective-permute-start | bytes 786440 | tf_op jit(solution)/shard_map/ppermute | solution.py:221
  106.7 0.8 pad_maximum_fusion.1.recorded_ref
  107.6 4.3 %data.1.data_ref = bf16[2,512,1024]{2,1,0:T(8,128)(2,1)} custom-call(bf16[2,256,512]{2,1,0:T(8,128)(2,1)} %pad_maximum_fusion.1.recorded_ref, bf16[256,1024]{1,0:T(8,128)(2,1)} %convert_element_type.30.last_ref.here_ref.table_ref), custom_call_target="tpu_custom_call" | custom-call | flops 536870912 | bytes 3145728 | tf_op jit(solution)/shard_map/data/pallas_call | solution.py:100
  111.9 6.2 %own.1.rest_ref = f32[2,512,1024]{2,1,0:T(8,128)} custom-call(bf16[256,512]{1,0:T(8,128)(2,1)} %copy-done, bf16[256,512]{1,0:T(8,128)(2,1)} %copy-done.1, bf16[2,768,1024]{2,1,0:T(8,128)(2,1)} %tables.1.basis_ref, bf16[2,512,1024]{2,1,0:T(8,128)(2,1)} %data.1.data_ref), custom_call_target="tpu_custom_call" | custom-call | flops 1073741824 | bytes 6291456 | tf_op jit(solution)/shard_map/own/pallas_call | solution.py:124
  118.0 0.7 copy-done.3
  118.7 0.7 copy-done.4
  119.4 5.3 %final.1 = bf16[2,512,1024]{2,1,0:T(8,128)(2,1)} custom-call(bf16[256,512]{1,0:T(8,128)(2,1)} %copy-done.3, bf16[256,512]{1,0:T(8,128)(2,1)} %copy-done.4, bf16[2,768,1024]{2,1,0:T(8,128)(2,1)} %tables.1.basis_ref, f32[2,512,1024]{2,1,0:T(8,128)} %own.1.rest_ref), custom_call_target="tpu_custom_call" | custom-call | flops 536870912 | bytes 7340032 | tf_op jit(solution)/shard_map/final/pallas_call | solution.py:152
  (31 shorter events, 4.0 us)
Async XLA Ops:
  0.0 52.6 %all-to-all-start.1 = ((bf16[1,256,2,512]{3,2,0,1:T(2,128)(2,1)}), bf16[1,256,2,512]{3,2,0,1:T(2,128)(2,1)S(1)}, u32[]{:S(2)}, u32[]{:S(2)}) async-start(bf16[1,256,2,512]{3,2,0,1:T(2,128)(2,1)} %bitcast.86), calls=%async_computation.1 | async-start | bytes 1048576 | tf_op jit(solution)/shard_map/all_to_all | solution.py:183
  20.7 19.9 %collective-permute-start.1 = (bf16[1,256,2,512]{3,2,1,0:T(2,128)(2,1)}, bf16[1,256,2,512]{3,2,1,0:T(2,128)(2,1)S(1)}, u32[]{:S(2)}, u32[]{:S(2)}) collective-permute-start(bf16[1,256,2,512]{3,2,1,0:T(2,128)(2,1)} %param.5), channel_id=1, source_target_pairs={{0,2},{1,3},{2,0},{3,1},{4,6},{5,7},{6,4},{7,5},{8,10},{9,11},{10,... | collective-permute-start | bytes 1572872 | tf_op jit(solution)/shard_map/ppermute | solution.py:181
  23.8 19.2 %collective-permute-start = (bf16[1,256,2,512]{3,2,1,0:T(2,128)(2,1)}, bf16[1,256,2,512]{3,2,1,0:T(2,128)(2,1)S(1)}, u32[]{:S(2)}, u32[]{:S(2)}) collective-permute-start(bf16[1,256,2,512]{3,2,1,0:T(2,128)(2,1)} %param.5), channel_id=1, source_target_pairs={{0,1},{1,0},{2,3},{3,2},{4,5},{5,4},{6,7},{7,6},{8,9},{9,8},{10,11... | collective-permute-start | bytes 1572872 | tf_op jit(solution)/shard_map/ppermute | solution.py:181
  27.3 1.0 copy-start.2
  40.6 3.8 %collective-permute-start.2 = (bf16[1,256,2,512]{3,2,1,0:T(2,128)(2,1)S(1)}, bf16[1,256,2,512]{3,2,1,0:T(2,128)(2,1)S(1)}, u32[]{:S(2)}, u32[]{:S(2)}) collective-permute-start(bf16[1,256,2,512]{3,2,1,0:T(2,128)(2,1)S(1)} %collective-permute-done.1), channel_id=1, source_target_pairs={{0,1},{1,0},{2,3},{3,2},{4,5},{5,4},{6,7},{7,6},{8,9},{9,8},{10,11... | collective-permute-start | bytes 1572872 | tf_op jit(solution)/shard_map/ppermute | solution.py:181
  44.8 23.0 %copy-start.5 = (f32[3,8,2]{1,2,0:T(2,128)S(1)}, f32[3,8,2]{1,2,0:T(2,128)}, u32[]{:S(2)}) copy-start(f32[3,8,2]{1,2,0:T(2,128)} %param.6) | copy-start | bytes 580
  52.6 43.4 %all-to-all-start = ((bf16[1,256,2,512]{3,2,0,1:T(2,128)(2,1)}), bf16[1,256,2,512]{3,2,0,1:T(2,128)(2,1)S(1)}, u32[]{:S(2)}, u32[]{:S(2)}) async-start(bf16[1,256,2,512]{3,2,0,1:T(2,128)(2,1)} %copy.42), calls=%async_computation | async-start | bytes 1048576 | tf_op jit(solution)/shard_map/all_to_all | solution.py:206
  96.5 15.3 %copy-start.1 = (bf16[256,512]{1,0:T(8,128)(2,1)}, bf16[256,512]{1,0:T(8,128)(2,1)S(1)}, u32[]{:S(2)}) copy-start(bf16[256,512]{1,0:T(8,128)(2,1)S(1)} %reshape_squeeze.6.second_ref) | copy-start | bytes 786436
  96.7 15.2 %copy-start = (bf16[256,512]{1,0:T(8,128)(2,1)}, bf16[256,512]{1,0:T(8,128)(2,1)S(1)}, u32[]{:S(2)}) copy-start(bf16[256,512]{1,0:T(8,128)(2,1)S(1)} %reshape_squeeze.7.first_ref) | copy-start | bytes 786436
  96.7 21.4 %collective-permute-start.3 = (bf16[256,512]{1,0:T(8,128)(2,1)S(1)}, bf16[256,512]{1,0:T(8,128)(2,1)S(1)}, u32[]{:S(2)}, u32[]{:S(2)}) collective-permute-start(bf16[256,512]{1,0:T(8,128)(2,1)S(1)} %reshape_squeeze.6.second_ref), channel_id=1, source_target_pairs={{0,4},{4,8},{8,12},{12,16},{16,20},{20,24},{24,28},{28,32},{32,36}... | collective-permute-start | bytes 786440 | tf_op jit(solution)/shard_map/ppermute | solution.py:220
  99.7 18.3 %collective-permute-start.4 = (bf16[256,512]{1,0:T(8,128)(2,1)S(1)}, bf16[256,512]{1,0:T(8,128)(2,1)S(1)}, u32[]{:S(2)}, u32[]{:S(2)}) collective-permute-start(bf16[256,512]{1,0:T(8,128)(2,1)S(1)} %reshape_squeeze.7.first_ref), channel_id=1, source_target_pairs={{4,0},{8,4},{12,8},{16,12},{20,16},{24,20},{28,24},{32,28},{36,32}... | collective-permute-start | bytes 786440 | tf_op jit(solution)/shard_map/ppermute | solution.py:221
  118.0 0.7 copy-start.3
  118.7 0.7 copy-start.4

commit v4 on v3

--- a/solution.py
+++ b/solution.py
@@ -11,7 +11,6 @@
 
 NT = 1024
 BLOCK = 128
-COLUMNS = 256
 
 
 shrink_level = 0.5
@@ -85,88 +84,6 @@
     )(weights.reshape(-1), tap_delays, table, table)
 
 
-def across_time(spectrum, basis):
-    return lax.dot_general(
-        spectrum, basis, (((0,), (0,)), ((), ())), preferred_element_type=jnp.float32
-    )
-
-
-def data_kernel(recorded_ref, table_ref, out_ref):
-    out_ref[0] = across_time(recorded_ref[0], table_ref[...]).astype(jnp.bfloat16)
-
-
-def data_part(recorded, table):
-    _, rows, columns = recorded.shape
-    return pl.pallas_call(
-        data_kernel,
-        grid=(2, columns // COLUMNS),
-        out_shape=jax.ShapeDtypeStruct((2, columns, NT), jnp.bfloat16),
-        in_specs=[
-            pl.BlockSpec((1, rows, COLUMNS), lambda s, c: (s, 0, c)),
-            pl.BlockSpec((rows, NT), lambda s, c: (0, 0)),
-        ],
-        out_specs=pl.BlockSpec((1, COLUMNS, NT), lambda s, c: (s, c, 0)),
-        cost_estimate=pl.CostEstimate(
-            flops=4 * rows * columns * NT, bytes_accessed=6 * columns * NT, transcendentals=0
-        ),
-        name="data",
-    )(recorded, table)
-
-
-def own_kernel(first_ref, second_ref, basis_ref, data_ref, out_ref):
-    spectra = jnp.concatenate([first_ref[...], second_ref[...]], axis=0)
-    out_ref[0] = data_ref[0].astype(jnp.float32) - across_time(spectra, basis_ref[0])
-
-
-def own_part(first, second, basis, data):
-    rows, columns = first.shape
-    spectra = pl.BlockSpec((rows, COLUMNS), lambda s, c: (0, c))
-    return pl.pallas_call(
-        own_kernel,
-        grid=(2, columns // COLUMNS),
-        out_shape=jax.ShapeDtypeStruct((2, columns, NT), jnp.float32),
-        in_specs=[
-            spectra,
-            spectra,
-            pl.BlockSpec((1, 2 * rows, NT), lambda s, c: (s, 0, 0)),
-            pl.BlockSpec((1, COLUMNS, NT), lambda s, c: (s, c, 0)),
-        ],
-        out_specs=pl.BlockSpec((1, COLUMNS, NT), lambda s, c: (s, c, 0)),
-        cost_estimate=pl.CostEstimate(
-            flops=8 * rows * columns * NT, bytes_accessed=12 * columns * NT, transcendentals=0
-        ),
-        name="own",
-    )(first, second, basis, data)
-
-
-def final_kernel(before_ref, after_ref, basis_ref, rest_ref, out_ref):
-    halo = jnp.where(pl.program_id(0) == 0, before_ref[...], after_ref[...])
-    residual = rest_ref[0] - across_time(halo, basis_ref[0])
-    shrunk = residual - jnp.clip(residual, -shrink_level, shrink_level)
-    out_ref[0] = shrunk.astype(jnp.bfloat16)
-
-
-def final_part(before, after, basis, rest):
-    rows, columns = before.shape
-    spectra = pl.BlockSpec((rows, COLUMNS), lambda s, c: (0, c))
-    return pl.pallas_call(
-        final_kernel,
-        grid=(2, columns // COLUMNS),
-        out_shape=jax.ShapeDtypeStruct((2, columns, NT), jnp.bfloat16),
-        in_specs=[
-            spectra,
-            spectra,
-            pl.BlockSpec((1, rows, NT), lambda s, c: (s, 2, 0)),
-            pl.BlockSpec((1, COLUMNS, NT), lambda s, c: (s, c, 0)),
-        ],
-        out_specs=pl.BlockSpec((1, COLUMNS, NT), lambda s, c: (s, c, 0)),
-        cost_estimate=pl.CostEstimate(
-            flops=4 * rows * columns * NT, bytes_accessed=14 * columns * NT, transcendentals=0
-        ),
-        name="final",
-    )(before, after, basis, rest)
-
-
 def body(operator, recorded, filter_coefficients, tap_delays):
     local_rows = operator.shape[1]
     columns = recorded.shape[3]
@@ -205,22 +122,45 @@
     spectra = total.astype(jnp.bfloat16)[None]
     traces = lax.all_to_all(spectra, "freq", split_axis=1, concat_axis=0, tiled=True)
 
-    table = lookup_rows(jnp.arange(freq_count) + 1)
-    basis = filtered_tables(table, filter_coefficients, tap_delays)
+    frequency_index, weights, _ = lax.optimization_barrier(
+        (jnp.arange(freq_count) + 1, filter_coefficients, spectra)
+    )
+    table = lookup_rows(frequency_index)
+    basis = filtered_tables(table, weights, tap_delays)
 
-    def by_station(gathered):
-        return [gathered[:, s].reshape(2 * freq_count, columns) for s in range(2)]
+    def station_rows(gathered, s):
+        return gathered[:, s].reshape(2 * freq_count, columns)
 
-    recorded_traces = jnp.stack(by_station(recorded_traces))
-    data = data_part(recorded_traces, table)
+    def turned(spectra):
+        return with_layout_constraint(spectra.T, Layout(major_to_minor=(0, 1)))
+
+    def to_time(spectra, basis):
+        return with_layout_constraint(
+            jnp.dot(spectra, basis, preferred_element_type=jnp.float32),
+            Layout(major_to_minor=(0, 1)),
+        )
+
+    rows = 2 * freq_count
+    data = [
+        to_time(turned(station_rows(recorded_traces, s)), table).astype(jnp.bfloat16)
+        for s in range(2)
+    ]
 
     forward = [(i, i + 1) for i in range(freq_count - 1)]
     backward = [(i + 1, i) for i in range(freq_count - 1)]
-    first, second = by_station(traces)
+    first, second = station_rows(traces, 0), station_rows(traces, 1)
     before = lax.ppermute(second, "freq", forward)
     after = lax.ppermute(first, "freq", backward)
-    rest = own_part(first, second, basis, data)
-    return final_part(before, after, basis, rest)
+    own = turned(jnp.concatenate([first, second], axis=0))
+    rest = [
+        data[s].astype(jnp.float32) - to_time(own, basis[s, : 2 * rows]) for s in range(2)
+    ]
+    result = []
+    for s, halo in enumerate((before, after)):
+        residual = rest[s] - to_time(turned(halo), basis[s, 2 * rows :])
+        shrunk = residual - jnp.clip(residual, -shrink_level, shrink_level)
+        result.append(shrunk.astype(jnp.bfloat16))
+    return jnp.stack(result)
 
 
 def solution(mesh):

time: 126 us -> 118 us (0.937)
  the two profiles are of different devices: /device:TPU:24 before, /device:TPU:8 now
where the time goes in v4:
time: 118 us; the launch traced here: 117 us
  starting transfers between devices  53.1 us (45%)
  waiting for transfers between devices  32.3 us (27%)
  Pallas kernels  12.6 us (11%)
  local copies, waits for them, and re-layouts  7.61 us (6%)
  matrix products  6.42 us (5%)
  other arithmetic  4.41 us (4%)
    all_to_all x1, starting transfers between devices, body(): lax.all_to_all(recorded, 'freq', split_axis=1, concat_axis=0, tiled=True)  20.7 us
    ppermute x3, waiting for transfers between devices, across(): return with_layout_constraint(lax.ppermute(value, 'row', pairs), plain)  15 us
    all_to_all x1, starting transfers between devices, body(): lax.all_to_all(spectra, 'freq', split_axis=1, concat_axis=0, tiled=True)  14.1 us
    all_to_all x1, waiting for transfers between devices, body(): lax.all_to_all(spectra, 'freq', split_axis=1, concat_axis=0, tiled=True)  13 us
    pallas_call x1, Pallas kernels, filtered_tables(): pl.pallas_call(tables_kernel, grid=(2, NT // BLOCK), out_shape=jax.ShapeD...  12.6 us
    ppermute x3, starting transfers between devices, across(): return with_layout_constraint(lax.ppermute(value, 'row', pairs), plain)  8.04 us
    ppermute x1, starting transfers between devices, body(): after = lax.ppermute(first, 'freq', backward)  7.01 us
    dot_general x6, matrix products, to_time(): jnp.dot(spectra, basis, preferred_element_type=jnp.float32)  4.65 us
  transfers between devices with their start and end apart: 7, of which 5 were waited for; matrix products, arithmetic and copies ran while one was open for 13% of the time, Pallas kernels for 11%

profile of v4, /device:TPU:8, one launch (start us, length us, event | category | flops | bytes accessed | tf_op | source)
XLA Modules:
  0.0 116.7 jit_solution(7346035006443600814)
XLA Ops:
  0.0 20.7 %all-to-all-start = ((bf16[1,256,2,512]{3,2,0,1:T(2,128)(2,1)}), bf16[1,256,2,512]{3,2,0,1:T(2,128)(2,1)S(1)}, u32[]{:S(2)}, u32[]{:S(2)}) async-start(bf16[1,256,2,512]{3,2,0,1:T(2,128)(2,1)} %bitcast.124), calls=%async_computation | async-start | bytes 1048576 | tf_op jit(solution)/shard_map/all_to_all | solution.py:100
  20.7 1.9 %collective-permute-start = (bf16[1,256,2,512]{3,2,1,0:T(2,128)(2,1)}, bf16[1,256,2,512]{3,2,1,0:T(2,128)(2,1)S(1)}, u32[]{:S(2)}, u32[]{:S(2)}) collective-permute-start(bf16[1,256,2,512]{3,2,1,0:T(2,128)(2,1)} %param.5), channel_id=1, source_target_pairs={{0,1},{1,0},{2,3},{3,2},{4,5},{5,4},{6,7},{7,6},{8,9},{9,8},{10,11... | collective-permute-start | bytes 1572872 | tf_op jit(solution)/shard_map/ppermute | solution.py:98
  22.6 4.2 %collective-permute-start.1 = (bf16[1,256,2,512]{3,2,1,0:T(2,128)(2,1)}, bf16[1,256,2,512]{3,2,1,0:T(2,128)(2,1)S(1)}, u32[]{:S(2)}, u32[]{:S(2)}) collective-permute-start(bf16[1,256,2,512]{3,2,1,0:T(2,128)(2,1)} %param.5), channel_id=1, source_target_pairs={{0,2},{1,3},{2,0},{3,1},{4,6},{5,7},{6,4},{7,5},{8,10},{9,11},{10,... | collective-permute-start | bytes 1572872 | tf_op jit(solution)/shard_map/ppermute | solution.py:98
  26.8 1.5 %copy.93 = bf16[1,256,2,1024]{3,1,2,0:T(8,128)(2,1)S(1)} copy(bf16[1,256,2,1024]{3,2,1,0:T(2,128)(2,1)} %param.4) | data formatting | bytes 2097152 | tf_op args[0]
  28.8 0.6 copy-done.2
  29.9 14.1 %collective-permute-done.1 = bf16[1,256,2,512]{3,2,1,0:T(2,128)(2,1)S(1)} collective-permute-done((bf16[1,256,2,512]{3,2,1,0:T(2,128)(2,1)}, bf16[1,256,2,512]{3,2,1,0:T(2,128)(2,1)S(1)}, u32[]{:S(2)}, u32[]{:S(2)}) %collective-permute-start.1) | collective-permute-done | bytes 524320 | tf_op jit(solution)/shard_map/ppermute | solution.py:98
  44.0 1.9 %collective-permute-start.2 = (bf16[1,256,2,512]{3,2,1,0:T(2,128)(2,1)S(1)}, bf16[1,256,2,512]{3,2,1,0:T(2,128)(2,1)S(1)}, u32[]{:S(2)}, u32[]{:S(2)}) collective-permute-start(bf16[1,256,2,512]{3,2,1,0:T(2,128)(2,1)S(1)} %collective-permute-done.1), channel_id=1, source_target_pairs={{0,1},{1,0},{2,3},{3,2},{4,5},{5,4},{6,7},{7,6},{8,9},{9,8},{10,11... | collective-permute-start | bytes 1572872 | tf_op jit(solution)/shard_map/ppermute | solution.py:98
  46.8 0.9 collective-permute-done.2
  48.2 1.3 %copy.58 = bf16[1,256,2,512]{3,2,0,1:T(2,128)(2,1)} copy(bf16[1,256,2,512]{3,1,2,0:T(8,128)(2,1)S(1)} %fusion.8) | data formatting | bytes 1048576 | tf_op jit(solution)/shard_map/broadcast_in_dim | solution.py:122
  49.6 3.1 %all-to-all-done = bf16[1,256,2,512]{3,2,0,1:T(2,128)(2,1)S(1)} async-done(((bf16[1,256,2,512]{3,2,0,1:T(2,128)(2,1)}), bf16[1,256,2,512]{3,2,0,1:T(2,128)(2,1)S(1)}, u32[]{:S(2)}, u32[]{:S(2)}) %all-to-all-start) | async-done | bytes 524320 | tf_op jit(solution)/shard_map/all_to_all | solution.py:100
  52.6 14.1 %all-to-all-start.1 = ((bf16[1,256,2,512]{3,2,0,1:T(2,128)(2,1)}), bf16[1,256,2,512]{3,2,0,1:T(2,128)(2,1)S(1)}, u32[]{:S(2)}, u32[]{:S(2)}) async-start(bf16[1,256,2,512]{3,2,0,1:T(2,128)(2,1)} %copy.58), calls=%async_computation.1 | async-start | bytes 1048576 | tf_op jit(solution)/shard_map/all_to_all | solution.py:123
  66.8 0.7 reshape.112.weights_ref
  67.5 2.4 %multiply_convert_fusion.1 = (bf16[128,1,1024]{2,0,1:T(8,128)(2,1)S(1)}, bf16[128,1,1024]{2,0,1:T(8,128)(2,1)S(1)}) fusion(s32[128]{0:T(128)S(1)} %iota_add_fusion), kind=kLoop, calls=%fused_computation.54 | loop fusion | flops 2490368 | bytes 524800 | tf_op jit(solution)/shard_map/convert
  70.6 1.0 convert_element_type.46.last_ref.here_ref
  71.5 12.6 %tables.1 = bf16[2,768,1024]{2,1,0:T(8,128)(2,1)} custom-call(f32[48]{0:T(128)} %reshape.112.weights_ref, s32[8]{0:T(128)} %delays_ref.1, bf16[256,1024]{1,0:T(8,128)(2,1)} %convert_element_type.46.last_ref.here_ref, bf16[256,1024]{1,0:T(8,128)(2,1)} %convert_element_type.46.last_ref.here_ref), custom_call_target="tpu_custom_call" | custom-call | flops 1610612736 | bytes 4194304 | tf_op jit(solution)/shard_map/tables/pallas_call | solution.py:68
  86.0 13.0 %all-to-all-done.1 = bf16[1,256,2,512]{3,2,0,1:T(2,128)(2,1)S(1)} async-done(((bf16[1,256,2,512]{3,2,0,1:T(2,128)(2,1)}), bf16[1,256,2,512]{3,2,0,1:T(2,128)(2,1)S(1)}, u32[]{:S(2)}, u32[]{:S(2)}) %all-to-all-start.1) | async-done | bytes 524320 | tf_op jit(solution)/shard_map/all_to_all | solution.py:123
  99.9 3.3 %collective-permute-start.3 = (bf16[256,512]{0,1:T(8,128)(2,1)S(1)}, bf16[256,512]{0,1:T(8,128)(2,1)S(1)}, u32[]{:S(2)}, u32[]{:S(2)}) collective-permute-start(bf16[256,512]{0,1:T(8,128)(2,1)S(1)} %copy.62), channel_id=1, source_target_pairs={{0,4},{4,8},{8,12},{12,16},{16,20},{20,24},{24,28},{28,32},{32,36}... | collective-permute-start | bytes 786440 | tf_op jit(solution)/shard_map/ppermute | solution.py:152
  103.2 7.0 %collective-permute-start.4 = (bf16[256,512]{0,1:T(8,128)(2,1)S(1)}, bf16[256,512]{0,1:T(8,128)(2,1)S(1)}, u32[]{:S(2)}, u32[]{:S(2)}) collective-permute-start(bf16[256,512]{0,1:T(8,128)(2,1)S(1)} %copy.61), channel_id=1, source_target_pairs={{4,0},{8,4},{12,8},{16,12},{20,16},{24,20},{28,24},{32,28},{36,32}... | collective-permute-start | bytes 786440 | tf_op jit(solution)/shard_map/ppermute | solution.py:153
  110.2 1.9 %fusion.9 = f32[512,1024]{1,0:T(8,128)S(1)} fusion(bf16[2,768,1024]{2,1,0:T(8,128)(2,1)} %tables.1, bf16[256,512]{0,1:T(8,128)(2,1)S(1)} %copy.62, bf16[256,512]{0,1:T(8,128)(2,1)S(1)} %copy.61), kind=kOutput, calls=%fused_computation.19 | convolution fusion | flops 537919488 | bytes 3670016 | tf_op jit(solution)/shard_map/dot_general | solution.py:139
  112.2 0.7 fusion.10
  112.9 1.2 %collective-permute-done.4 = bf16[256,512]{0,1:T(8,128)(2,1)S(1)} collective-permute-done((bf16[256,512]{0,1:T(8,128)(2,1)S(1)}, bf16[256,512]{0,1:T(8,128)(2,1)S(1)}, u32[]{:S(2)}, u32[]{:S(2)}) %collective-permute-start.4) | collective-permute-done | bytes 262176 | tf_op jit(solution)/shard_map/ppermute | solution.py:153
  114.1 0.5 fusion.2
  114.7 0.6 fusion.3
  115.2 1.5 %pad_maximum_fusion = bf16[2,512,1024]{2,1,0:T(8,128)(2,1)} fusion(bf16[1,512,1024]{2,1,0:T(8,128)(2,1)S(1)} %fusion.2, bf16[1,512,1024]{2,1,0:T(8,128)(2,1)S(1)} %fusion.3), kind=kLoop, calls=%fused_computation.4 | loop fusion | flops 1048576 | bytes 4194304 | tf_op jit(solution)/shard_map/stack | solution.py:163
  (34 shorter events, 5.6 us)
Async XLA Ops:
  0.0 52.6 %all-to-all-start = ((bf16[1,256,2,512]{3,2,0,1:T(2,128)(2,1)}), bf16[1,256,2,512]{3,2,0,1:T(2,128)(2,1)S(1)}, u32[]{:S(2)}, u32[]{:S(2)}) async-start(bf16[1,256,2,512]{3,2,0,1:T(2,128)(2,1)} %bitcast.124), calls=%async_computation | async-start | bytes 1048576 | tf_op jit(solution)/shard_map/all_to_all | solution.py:100
  20.7 25.7 %collective-permute-start = (bf16[1,256,2,512]{3,2,1,0:T(2,128)(2,1)}, bf16[1,256,2,512]{3,2,1,0:T(2,128)(2,1)S(1)}, u32[]{:S(2)}, u32[]{:S(2)}) collective-permute-start(bf16[1,256,2,512]{3,2,1,0:T(2,128)(2,1)} %param.5), channel_id=1, source_target_pairs={{0,1},{1,0},{2,3},{3,2},{4,5},{5,4},{6,7},{7,6},{8,9},{9,8},{10,11... | collective-permute-start | bytes 1572872 | tf_op jit(solution)/shard_map/ppermute | solution.py:98
  22.6 21.4 %collective-permute-start.1 = (bf16[1,256,2,512]{3,2,1,0:T(2,128)(2,1)}, bf16[1,256,2,512]{3,2,1,0:T(2,128)(2,1)S(1)}, u32[]{:S(2)}, u32[]{:S(2)}) collective-permute-start(bf16[1,256,2,512]{3,2,1,0:T(2,128)(2,1)} %param.5), channel_id=1, source_target_pairs={{0,2},{1,3},{2,0},{3,1},{4,6},{5,7},{6,4},{7,5},{8,10},{9,11},{10,... | collective-permute-start | bytes 1572872 | tf_op jit(solution)/shard_map/ppermute | solution.py:98
  28.4 1.0 copy-start.2
  44.0 3.8 %collective-permute-start.2 = (bf16[1,256,2,512]{3,2,1,0:T(2,128)(2,1)S(1)}, bf16[1,256,2,512]{3,2,1,0:T(2,128)(2,1)S(1)}, u32[]{:S(2)}, u32[]{:S(2)}) collective-permute-start(bf16[1,256,2,512]{3,2,1,0:T(2,128)(2,1)S(1)} %collective-permute-done.1), channel_id=1, source_target_pairs={{0,1},{1,0},{2,3},{3,2},{4,5},{5,4},{6,7},{7,6},{8,9},{9,8},{10,11... | collective-permute-start | bytes 1572872 | tf_op jit(solution)/shard_map/ppermute | solution.py:98
  47.8 19.0 %copy-start.3 = (f32[3,8,2]{1,2,0:T(2,128)S(1)}, f32[3,8,2]{1,2,0:T(2,128)}, u32[]{:S(2)}) copy-start(f32[3,8,2]{1,2,0:T(2,128)} %param.6) | copy-start | bytes 580
  52.6 46.4 %all-to-all-start.1 = ((bf16[1,256,2,512]{3,2,0,1:T(2,128)(2,1)}), bf16[1,256,2,512]{3,2,0,1:T(2,128)(2,1)S(1)}, u32[]{:S(2)}, u32[]{:S(2)}) async-start(bf16[1,256,2,512]{3,2,0,1:T(2,128)(2,1)} %copy.58), calls=%async_computation.1 | async-start | bytes 1048576 | tf_op jit(solution)/shard_map/all_to_all | solution.py:123
  84.1 1.0 copy-start
  99.9 12.3 %copy-start.1 = (bf16[2,768,1024]{2,1,0:T(8,128)(2,1)S(1)}, bf16[2,768,1024]{2,1,0:T(8,128)(2,1)}, u32[]{:S(2)}) copy-start(bf16[2,768,1024]{2,1,0:T(8,128)(2,1)} %tables.1) | copy-start | bytes 9437188
  99.9 14.8 %collective-permute-start.3 = (bf16[256,512]{0,1:T(8,128)(2,1)S(1)}, bf16[256,512]{0,1:T(8,128)(2,1)S(1)}, u32[]{:S(2)}, u32[]{:S(2)}) collective-permute-start(bf16[256,512]{0,1:T(8,128)(2,1)S(1)} %copy.62), channel_id=1, source_target_pairs={{0,4},{4,8},{8,12},{12,16},{16,20},{20,24},{24,28},{28,32},{32,36}... | collective-permute-start | bytes 786440 | tf_op jit(solution)/shard_map/ppermute | solution.py:152
  103.2 10.9 %collective-permute-start.4 = (bf16[256,512]{0,1:T(8,128)(2,1)S(1)}, bf16[256,512]{0,1:T(8,128)(2,1)S(1)}, u32[]{:S(2)}, u32[]{:S(2)}) collective-permute-start(bf16[256,512]{0,1:T(8,128)(2,1)S(1)} %copy.61), channel_id=1, source_target_pairs={{4,0},{8,4},{12,8},{16,12},{20,16},{24,20},{28,24},{32,28},{36,32}... | collective-permute-start | bytes 786440 | tf_op jit(solution)/shard_map/ppermute | solution.py:153

commit v5 on v4

--- a/solution.py
+++ b/solution.py
@@ -6,11 +6,15 @@
 from jax.experimental import pallas as pl
 from jax.experimental.layout import Layout, with_layout_constraint
 from jax.experimental.pallas import tpu as pltpu
+from jax.sharding import Mesh
 from jax.sharding import PartitionSpec as P
 
 
 NT = 1024
 BLOCK = 128
+FREQ = ("yl", "x", "z")
+ROW = ("yh", "core")
+SIZES = (2, 4, 16, 2, 2)
 
 
 shrink_level = 0.5
@@ -87,19 +91,23 @@
 def body(operator, recorded, filter_coefficients, tap_delays):
     local_rows = operator.shape[1]
     columns = recorded.shape[3]
-    freq_count = lax.axis_size("freq")
-    row_count = lax.axis_size("row")
-    row = lax.axis_index("row")
+    freq_count = lax.axis_size(FREQ)
+    row_count = lax.axis_size(ROW)
+    row = lax.axis_index(ROW)
 
     plain = Layout(major_to_minor=(0, 1, 2, 3))
 
     def across(value, mask):
         pairs = [(i, i ^ mask) for i in range(row_count)]
-        return with_layout_constraint(lax.ppermute(value, "row", pairs), plain)
-
-    recorded_traces = lax.all_to_all(
-        recorded, "freq", split_axis=1, concat_axis=0, tiled=True
-    )
+        return with_layout_constraint(lax.ppermute(value, ROW, pairs), plain)
+
+    spread, width, rungs = (lax.axis_size(axis) for axis in FREQ)
+    spots = spread * width
+    pairs = local_rows // freq_count
+
+    by_target = recorded.reshape(spots, rungs, pairs, 2, columns).transpose(1, 0, 2, 3, 4)
+    line = lax.all_to_all(by_target, "z", split_axis=0, concat_axis=0, tiled=True)
+
     far = across(recorded, 2)
     near = across(recorded, 1)
     far_near = across(far, 1)
@@ -120,16 +128,37 @@
     total = product(0, recorded) + product(1, near)
     total = total + product(2, far) + product(3, far_near)
     spectra = total.astype(jnp.bfloat16)[None]
-    traces = lax.all_to_all(spectra, "freq", split_axis=1, concat_axis=0, tiled=True)
-
-    frequency_index, weights, _ = lax.optimization_barrier(
-        (jnp.arange(freq_count) + 1, filter_coefficients, spectra)
-    )
-    table = lookup_rows(frequency_index)
-    basis = filtered_tables(table, weights, tap_delays)
+    traces = lax.all_to_all(spectra, FREQ, split_axis=1, concat_axis=0, tiled=True)
+
+    own_y, own_x = lax.axis_index("yl"), lax.axis_index("x")
+
+    def natural(array):
+        return with_layout_constraint(array, Layout(major_to_minor=tuple(range(array.ndim))))
+
+    line = line.reshape(rungs, spread, width, pairs, 2, columns)
+    stays = lax.dynamic_index_in_dim(line, own_y, axis=1, keepdims=False)
+    leaves = lax.dynamic_index_in_dim(line, own_y ^ 1, axis=1, keepdims=False)
+    plane = jnp.stack([stays, natural(lax.ppermute(natural(leaves), "yl", [(0, 1), (1, 0)]))])
+    pieces = []
+    for dx in range(width):
+        target = lax.rem(own_x + dx, width)
+        piece = natural(lax.dynamic_index_in_dim(plane, target, axis=2, keepdims=False))
+        if dx:
+            links = [(x, (x + dx) % width) for x in range(width)]
+            piece = natural(lax.ppermute(piece, "x", links))
+        pieces.append(piece)
+    sources = [
+        (own_y ^ dy) * width + lax.rem(own_x + width - dx, width)
+        for dx in range(width)
+        for dy in range(spread)
+    ]
+    recorded_traces = natural(jnp.stack(pieces).reshape(freq_count, pairs, 2, columns))
+
+    table = lookup_rows(jnp.arange(freq_count) + 1)
+    basis = filtered_tables(table, filter_coefficients, tap_delays)
 
     def station_rows(gathered, s):
-        return gathered[:, s].reshape(2 * freq_count, columns)
+        return gathered[:, s].reshape(-1, columns)
 
     def turned(spectra):
         return with_layout_constraint(spectra.T, Layout(major_to_minor=(0, 1)))
@@ -141,16 +170,23 @@
         )
 
     rows = 2 * freq_count
+    near_first = jnp.concatenate(
+        [
+            lax.dynamic_slice_in_dim(table, source * 2 * rungs, 2 * rungs, axis=0)
+            for source in sources
+        ],
+        axis=0,
+    )
     data = [
-        to_time(turned(station_rows(recorded_traces, s)), table).astype(jnp.bfloat16)
+        to_time(turned(station_rows(recorded_traces, s)), near_first).astype(jnp.bfloat16)
         for s in range(2)
     ]
 
     forward = [(i, i + 1) for i in range(freq_count - 1)]
     backward = [(i + 1, i) for i in range(freq_count - 1)]
     first, second = station_rows(traces, 0), station_rows(traces, 1)
-    before = lax.ppermute(second, "freq", forward)
-    after = lax.ppermute(first, "freq", backward)
+    before = lax.ppermute(second, FREQ, forward)
+    after = lax.ppermute(first, FREQ, backward)
     own = turned(jnp.concatenate([first, second], axis=0))
     rest = [
         data[s].astype(jnp.float32) - to_time(own, basis[s, : 2 * rows]) for s in range(2)
@@ -164,13 +200,15 @@
 
 
 def solution(mesh):
+    physical = Mesh(mesh.devices.reshape(SIZES), FREQ + ROW)
     in_specs = (
-        P("freq", "row", None, None),
-        P("freq", "row", None, None),
-        P(None, None, ("row", "freq")),
+        P(FREQ, ROW, None, None),
+        P(FREQ, ROW, None, None),
+        P(None, None, ROW + FREQ),
         P(),
     )
-    out_specs = P(("row", "freq"), None, None)
-
-
-    return jax.shard_map(body, mesh=mesh, in_specs=in_specs, out_specs=out_specs, check_vma=False)
+    out_specs = P(ROW + FREQ, None, None)
+
+    return jax.shard_map(
+        body, mesh=physical, in_specs=in_specs, out_specs=out_specs, check_vma=False
+    )

time: 118 us -> 120 us (1.017)
  the two profiles are of different devices: /device:TPU:8 before, /device:TPU:96 now
where the time goes in v5:
time: 120 us; the launch traced here: 119 us
  starting transfers between devices  56.3 us (47%)
  waiting for transfers between devices  20 us (17%)
  Pallas kernels  12.6 us (10%)
  matrix products  11.1 us (9%)
  local copies, waits for them, and re-layouts  9.81 us (8%)
  other arithmetic  8.48 us (7%)
    all_to_all x1, starting transfers between devices, body(): lax.all_to_all(by_target, 'z', split_axis=0, concat_axis=0, tiled=True)  14.3 us
    pallas_call x1, Pallas kernels, filtered_tables(): pl.pallas_call(tables_kernel, grid=(2, NT // BLOCK), out_shape=jax.ShapeD...  12.6 us
    all_to_all x1, waiting for transfers between devices, body(): lax.all_to_all(by_target, 'z', split_axis=0, concat_axis=0, tiled=True)  12.4 us
    all_to_all x1, starting transfers between devices, body(): lax.all_to_all(spectra, FREQ, split_axis=1, concat_axis=0, tiled=True)  11.3 us
    ppermute x3, starting transfers between devices, body(): piece = natural(lax.ppermute(piece, 'x', links))  11.1 us
    ppermute x3, starting transfers between devices, across(): return with_layout_constraint(lax.ppermute(value, ROW, pairs), plain)  9.06 us
    dot_general x4, matrix products, product(): jnp.einsum('qprs,spc->rqc', block, segment[0], preferred_element_type=jnp...  6.47 us
    ppermute x1, starting transfers between devices, body(): before = lax.ppermute(second, FREQ, forward)  4.85 us
  transfers between devices with their start and end apart: 11, of which 3 were waited for; matrix products, arithmetic and copies ran while one was open for 22% of the time, Pallas kernels for 11%

profile of v5, /device:TPU:96, one launch (start us, length us, event | category | flops | bytes accessed | tf_op | source)
XLA Modules:
  0.0 118.9 jit_solution(2748365218733303824)
XLA Ops:
  0.0 5.2 %collective-permute-start.5 = (bf16[1,256,2,512]{3,2,1,0:T(2,128)(2,1)}, bf16[1,256,2,512]{3,2,1,0:T(2,128)(2,1)}, u32[]{:S(2)}, u32[]{:S(2)}) collective-permute-start(bf16[1,256,2,512]{3,2,1,0:T(2,128)(2,1)} %param.5), channel_id=1, source_target_pairs={{0,2},{1,3},{2,0},{3,1},{4,6},{5,7},{6,4},{7,5},{8,10},{9,11},{10,... | collective-permute-start | bytes 1572872 | tf_op jit(solution)/shard_map/ppermute | solution.py:102
  5.2 1.9 %collective-permute-start.4 = (bf16[1,256,2,512]{3,2,1,0:T(2,128)(2,1)}, bf16[1,256,2,512]{3,2,1,0:T(2,128)(2,1)}, u32[]{:S(2)}, u32[]{:S(2)}) collective-permute-start(bf16[1,256,2,512]{3,2,1,0:T(2,128)(2,1)} %param.5), channel_id=1, source_target_pairs={{0,1},{1,0},{2,3},{3,2},{4,5},{5,4},{6,7},{7,6},{8,9},{9,8},{10,11... | collective-permute-start | bytes 1572872 | tf_op jit(solution)/shard_map/ppermute | solution.py:102
  7.2 2.3 %copy.67 = bf16[16,8,2,2,512]{4,3,2,1,0:T(2,128)(2,1)} copy(bf16[16,8,2,2,512]{4,3,2,0,1:T(2,128)(2,1)} %bitcast.136) | data formatting | bytes 1048576 | tf_op jit(solution)/shard_map/transpose | solution.py:108
  9.5 14.3 %all-to-all-start = ((bf16[16,8,2,2,512]{4,3,2,1,0:T(2,128)(2,1)}), bf16[16,8,2,2,512]{4,3,2,1,0:T(2,128)(2,1)S(1)}, u32[]{:S(2)}, u32[]{:S(2)}) async-start(bf16[16,8,2,2,512]{4,3,2,1,0:T(2,128)(2,1)} %copy.67), calls=%async_computation | async-start | bytes 1048576 | tf_op jit(solution)/shard_map/all_to_all | solution.py:109
  24.1 2.5 %multiply_convert_fusion.1 = (bf16[128,1,1024]{2,0,1:T(8,128)(2,1)S(1)}, bf16[128,1,1024]{2,0,1:T(8,128)(2,1)S(1)}) fusion(s32[128]{0:T(128)S(1)} %iota_add_fusion), kind=kLoop, calls=%fused_computation.55 | loop fusion | flops 2490368 | bytes 524800 | tf_op jit(solution)/shard_map/convert
  30.2 2.8 %convolution_bitcast_fusion.3 = f32[2,256,512]{2,1,0:T(8,128)} fusion(bf16[1,2,256,256]{3,2,1,0:T(8,128)(2,1)} %get-tuple-element.38, bf16[1,2,256,256]{3,2,1,0:T(8,128)(2,1)} %get-tuple-element.37, bf16[256,2,512]{2,1,0:T(2,128)(2,1)} %bitcast.137), kind=kOutput, calls=%fused_computation.12 | convolution fusion | flops 268697600 | bytes 2097152 | tf_op jit(solution)/shard_map/qprs,spc->rqc/dot_general | solution.py:124
  33.0 1.9 %collective-permute-start.6 = (bf16[1,256,2,512]{3,2,1,0:T(2,128)(2,1)}, bf16[1,256,2,512]{3,2,1,0:T(2,128)(2,1)S(1)}, u32[]{:S(2)}, u32[]{:S(2)}) collective-permute-start(bf16[1,256,2,512]{3,2,1,0:T(2,128)(2,1)} %collective-permute-done.5), channel_id=1, source_target_pairs={{0,1},{1,0},{2,3},{3,2},{4,5},{5,4},{6,7},{7,6},{8,9},{9,8},{10,11... | collective-permute-start | bytes 1572872 | tf_op jit(solution)/shard_map/ppermute | solution.py:102
  35.0 1.7 %convolution_bitcast_fusion.1 = f32[2,256,512]{2,1,0:T(8,128)S(1)} fusion(bf16[1,2,256,256]{3,2,1,0:T(8,128)(2,1)} %get-tuple-element.40, bf16[1,2,256,256]{3,2,1,0:T(8,128)(2,1)} %get-tuple-element.39, bf16[256,2,512]{2,1,0:T(2,128)(2,1)} %bitcast.32), kind=kOutput, calls=%fused_computation.10 | convolution fusion | flops 268697600 | bytes 2097152 | tf_op jit(solution)/shard_map/qprs,spc->rqc/dot_general | solution.py:124
  36.8 1.5 %fusion.5 = f32[2,256,512]{2,1,0:T(8,128)S(1)} fusion(f32[2,256,512]{2,1,0:T(8,128)S(1)} %convolution_bitcast_fusion.1, f32[2,256,512]{2,1,0:T(8,128)S(1)} %copy-done.4, bf16[1,2,256,256]{3,2,1,0:T(8,128)(2,1)S(1)} %copy-done.2, bf16[1,2,256,256]{3,2,1,0:T(8,128)(2,1)S(1)} %get-tuple-element.35, bf16[256,2,512]{2,1,0:T(2,128)(2,1)} %bitcast.26), kind=kOutput, calls=%fused_computation.14 | convolution fusion | flops 269221888 | bytes 4194304 | tf_op jit(solution)/shard_map/qprs,spc->rqc/dot_general | solution.py:124
  38.7 1.3 %copy.78 = bf16[1,256,2,512]{3,2,0,1:T(2,128)(2,1)} copy(bf16[1,256,2,512]{3,1,2,0:T(8,128)(2,1)S(1)} %fusion.8) | data formatting | bytes 1048576 | tf_op jit(solution)/shard_map/broadcast_in_dim | solution.py:130
  40.1 12.4 %all-to-all-done = bf16[16,8,2,2,512]{4,3,2,1,0:T(2,128)(2,1)S(1)} async-done(((bf16[16,8,2,2,512]{4,3,2,1,0:T(2,128)(2,1)}), bf16[16,8,2,2,512]{4,3,2,1,0:T(2,128)(2,1)S(1)}, u32[]{:S(2)}, u32[]{:S(2)}) %all-to-all-start) | async-done | bytes 524320 | tf_op jit(solution)/shard_map/all_to_all | solution.py:109
  52.4 11.3 %all-to-all-start.1 = ((bf16[1,256,2,512]{3,2,0,1:T(2,128)(2,1)}), bf16[1,256,2,512]{3,2,0,1:T(2,128)(2,1)S(1)}, u32[]{:S(2)}, u32[]{:S(2)}) async-start(bf16[1,256,2,512]{3,2,0,1:T(2,128)(2,1)} %copy.78), calls=%async_computation.1 | async-start | bytes 1048576 | tf_op jit(solution)/shard_map/all_to_all | solution.py:131
  65.3 3.7 %collective-permute-start = (bf16[16,4,2,2,512]{4,3,2,1,0:T(2,128)(2,1)S(1)}, bf16[16,4,2,2,512]{4,3,2,1,0:T(2,128)(2,1)S(1)}, u32[]{:S(2)}, u32[]{:S(2)}) collective-permute-start(bf16[16,4,2,2,512]{4,3,2,1,0:T(2,128)(2,1)S(1)} %bitcast.138), channel_id=1, source_target_pairs={{0,256},{256,0},{1,257},{257,1},{2,258},{258,2},{3,259},{259,3},{4... | collective-permute-start | bytes 786440 | tf_op jit(solution)/shard_map/ppermute | solution.py:141
  69.1 12.6 %tables.1 = bf16[2,768,1024]{2,1,0:T(8,128)(2,1)} custom-call(f32[48]{0:T(128)} %reshape.128.weights_ref, s32[8]{0:T(128)} %delays_ref.1, bf16[256,1024]{1,0:T(8,128)(2,1)} %copy-done.1, bf16[256,1024]{1,0:T(8,128)(2,1)} %copy-done.1), custom_call_target="tpu_custom_call" | custom-call | flops 1610612736 | bytes 4194304 | tf_op jit(solution)/shard_map/tables/pallas_call | solution.py:72
  82.7 5.1 %collective-permute-start.2 = (bf16[2,16,2,2,512]{4,3,2,1,0:T(2,128)(2,1)S(1)}, bf16[2,16,2,2,512]{4,3,2,1,0:T(2,128)(2,1)S(1)}, u32[]{:S(2)}, u32[]{:S(2)}) collective-permute-start(bf16[2,16,2,2,512]{4,3,2,1,0:T(2,128)(2,1)S(1)} %get-tuple-element.27), channel_id=1, source_target_pairs={{0,128},{64,192},{128,0},{192,64},{1,129},{65,193},{129,1},{193,65... | collective-permute-start | bytes 393224 | tf_op jit(solution)/shard_map/ppermute | solution.py:148
  87.8 3.0 %collective-permute-start.3 = (bf16[2,16,2,2,512]{4,3,2,1,0:T(2,128)(2,1)S(1)}, bf16[2,16,2,2,512]{4,3,2,1,0:T(2,128)(2,1)S(1)}, u32[]{:S(2)}, u32[]{:S(2)}) collective-permute-start(bf16[2,16,2,2,512]{4,3,2,1,0:T(2,128)(2,1)S(1)} %get-tuple-element.28), channel_id=1, source_target_pairs={{0,192},{64,0},{128,64},{192,128},{1,193},{65,1},{129,65},{193,129... | collective-permute-start | bytes 393224 | tf_op jit(solution)/shard_map/ppermute | solution.py:148
  90.8 3.1 %collective-permute-start.1 = (bf16[2,16,2,2,512]{4,3,2,1,0:T(2,128)(2,1)S(1)}, bf16[2,16,2,2,512]{4,3,2,1,0:T(2,128)(2,1)S(1)}, u32[]{:S(2)}, u32[]{:S(2)}) collective-permute-start(bf16[2,16,2,2,512]{4,3,2,1,0:T(2,128)(2,1)S(1)} %get-tuple-element.26), channel_id=1, source_target_pairs={{0,64},{64,128},{128,192},{192,0},{1,65},{65,129},{129,193},{193,1... | collective-permute-start | bytes 393224 | tf_op jit(solution)/shard_map/ppermute | solution.py:148
  95.5 3.3 %collective-permute-done.1 = bf16[2,16,2,2,512]{4,3,2,1,0:T(2,128)(2,1)S(1)} collective-permute-done((bf16[2,16,2,2,512]{4,3,2,1,0:T(2,128)(2,1)S(1)}, bf16[2,16,2,2,512]{4,3,2,1,0:T(2,128)(2,1)S(1)}, u32[]{:S(2)}, u32[]{:S(2)}) %collective-permute-start.1) | collective-permute-done | bytes 131104 | tf_op jit(solution)/shard_map/ppermute | solution.py:148
  98.8 1.0 pad_maximum_fusion.1
  102.5 4.9 %collective-permute-start.7 = (bf16[256,512]{0,1:T(8,128)(2,1)S(1)}, bf16[256,512]{0,1:T(8,128)(2,1)S(1)}, u32[]{:S(2)}, u32[]{:S(2)}) collective-permute-start(bf16[256,512]{0,1:T(8,128)(2,1)S(1)} %copy.82), channel_id=1, source_target_pairs={{0,4},{4,8},{8,12},{12,16},{16,20},{20,24},{24,28},{28,32},{32,36}... | collective-permute-start | bytes 786440 | tf_op jit(solution)/shard_map/ppermute | solution.py:188
  107.3 1.9 %collective-permute-start.8 = (bf16[256,512]{0,1:T(8,128)(2,1)S(1)}, bf16[256,512]{0,1:T(8,128)(2,1)S(1)}, u32[]{:S(2)}, u32[]{:S(2)}) collective-permute-start(bf16[256,512]{0,1:T(8,128)(2,1)S(1)} %copy.81), channel_id=1, source_target_pairs={{4,0},{8,4},{12,8},{16,12},{20,16},{24,20},{28,24},{32,28},{36,32}... | collective-permute-start | bytes 786440 | tf_op jit(solution)/shard_map/ppermute | solution.py:189
  109.2 1.9 %fusion.10 = f32[512,1024]{1,0:T(8,128)S(1)} fusion(bf16[2,768,1024]{2,1,0:T(8,128)(2,1)} %tables.1, bf16[256,512]{0,1:T(8,128)(2,1)S(1)} %copy.82, bf16[256,512]{0,1:T(8,128)(2,1)S(1)} %copy.81), kind=kOutput, calls=%fused_computation.21 | convolution fusion | flops 537919488 | bytes 3670016 | tf_op jit(solution)/shard_map/dot_general | solution.py:168
  112.5 4.3 %collective-permute-done.8 = bf16[256,512]{0,1:T(8,128)(2,1)S(1)} collective-permute-done((bf16[256,512]{0,1:T(8,128)(2,1)S(1)}, bf16[256,512]{0,1:T(8,128)(2,1)S(1)}, u32[]{:S(2)}, u32[]{:S(2)}) %collective-permute-start.8) | collective-permute-done | bytes 262176 | tf_op jit(solution)/shard_map/ppermute | solution.py:189
  117.3 1.5 %pad_maximum_fusion = bf16[2,512,1024]{2,1,0:T(8,128)(2,1)} fusion(bf16[1,512,1024]{2,1,0:T(8,128)(2,1)S(1)} %fusion.2, bf16[1,512,1024]{2,1,0:T(8,128)(2,1)S(1)} %fusion.3), kind=kLoop, calls=%fused_computation.4 | loop fusion | flops 1048576 | bytes 4194304 | tf_op jit(solution)/shard_map/stack | solution.py:199
  (61 shorter events, 12.9 us)
Async XLA Ops:
  0.0 23.8 %copy-start.3 = (bf16[1,256,2,1024]{3,2,1,0:T(2,128)(2,1)S(1)}, bf16[1,256,2,1024]{3,2,1,0:T(2,128)(2,1)}, u32[]{:S(2)}) copy-start(bf16[1,256,2,1024]{3,2,1,0:T(2,128)(2,1)} %param.4) | copy-start | bytes 3145732
  0.0 33.0 %collective-permute-start.5 = (bf16[1,256,2,512]{3,2,1,0:T(2,128)(2,1)}, bf16[1,256,2,512]{3,2,1,0:T(2,128)(2,1)}, u32[]{:S(2)}, u32[]{:S(2)}) collective-permute-start(bf16[1,256,2,512]{3,2,1,0:T(2,128)(2,1)} %param.5), channel_id=1, source_target_pairs={{0,2},{1,3},{2,0},{3,1},{4,6},{5,7},{6,4},{7,5},{8,10},{9,11},{10,... | collective-permute-start | bytes 1572872 | tf_op jit(solution)/shard_map/ppermute | solution.py:102
  5.2 31.5 %collective-permute-start.4 = (bf16[1,256,2,512]{3,2,1,0:T(2,128)(2,1)}, bf16[1,256,2,512]{3,2,1,0:T(2,128)(2,1)}, u32[]{:S(2)}, u32[]{:S(2)}) collective-permute-start(bf16[1,256,2,512]{3,2,1,0:T(2,128)(2,1)} %param.5), channel_id=1, source_target_pairs={{0,1},{1,0},{2,3},{3,2},{4,5},{5,4},{6,7},{7,6},{8,9},{9,8},{10,11... | collective-permute-start | bytes 1572872 | tf_op jit(solution)/shard_map/ppermute | solution.py:102
  9.5 42.9 %all-to-all-start = ((bf16[16,8,2,2,512]{4,3,2,1,0:T(2,128)(2,1)}), bf16[16,8,2,2,512]{4,3,2,1,0:T(2,128)(2,1)S(1)}, u32[]{:S(2)}, u32[]{:S(2)}) async-start(bf16[16,8,2,2,512]{4,3,2,1,0:T(2,128)(2,1)} %copy.67), calls=%async_computation | async-start | bytes 1048576 | tf_op jit(solution)/shard_map/all_to_all | solution.py:109
  30.2 38.8 %copy-start.1 = (bf16[256,1024]{1,0:T(8,128)(2,1)}, bf16[256,1024]{1,0:T(8,128)(2,1)S(1)}, u32[]{:S(2)}) copy-start(bf16[256,1024]{1,0:T(8,128)(2,1)S(1)} %convert_element_type.46.last_ref.here_ref) | copy-start | bytes 1572868
  30.2 6.5 %copy-start.2 = (bf16[1,2,256,256]{3,2,1,0:T(8,128)(2,1)S(1)}, bf16[1,2,256,256]{3,2,1,0:T(8,128)(2,1)}, u32[]{:S(2)}) copy-start(bf16[1,2,256,256]{3,2,1,0:T(8,128)(2,1)} %get-tuple-element.36) | copy-start | bytes 786436
  33.0 5.2 %collective-permute-start.6 = (bf16[1,256,2,512]{3,2,1,0:T(2,128)(2,1)}, bf16[1,256,2,512]{3,2,1,0:T(2,128)(2,1)S(1)}, u32[]{:S(2)}, u32[]{:S(2)}) collective-permute-start(bf16[1,256,2,512]{3,2,1,0:T(2,128)(2,1)} %collective-permute-done.5), channel_id=1, source_target_pairs={{0,1},{1,0},{2,3},{3,2},{4,5},{5,4},{6,7},{7,6},{8,9},{9,8},{10,11... | collective-permute-start | bytes 1572872 | tf_op jit(solution)/shard_map/ppermute | solution.py:102
  35.0 1.8 %copy-start.4 = (f32[2,256,512]{2,1,0:T(8,128)S(1)}, f32[2,256,512]{2,1,0:T(8,128)}, u32[]{:S(2)}) copy-start(f32[2,256,512]{2,1,0:T(8,128)} %convolution_bitcast_fusion.3) | copy-start | bytes 3145732
  38.3 25.6 %copy-start.5 = (f32[3,8,2]{1,2,0:T(2,128)S(1)}, f32[3,8,2]{1,2,0:T(2,128)}, u32[]{:S(2)}) copy-start(f32[3,8,2]{1,2,0:T(2,128)} %param.6) | copy-start | bytes 580
  52.4 49.1 %all-to-all-start.1 = ((bf16[1,256,2,512]{3,2,0,1:T(2,128)(2,1)}), bf16[1,256,2,512]{3,2,0,1:T(2,128)(2,1)S(1)}, u32[]{:S(2)}, u32[]{:S(2)}) async-start(bf16[1,256,2,512]{3,2,0,1:T(2,128)(2,1)} %copy.78), calls=%async_computation.1 | async-start | bytes 1048576 | tf_op jit(solution)/shard_map/all_to_all | solution.py:131
  65.3 16.6 %collective-permute-start = (bf16[16,4,2,2,512]{4,3,2,1,0:T(2,128)(2,1)S(1)}, bf16[16,4,2,2,512]{4,3,2,1,0:T(2,128)(2,1)S(1)}, u32[]{:S(2)}, u32[]{:S(2)}) collective-permute-start(bf16[16,4,2,2,512]{4,3,2,1,0:T(2,128)(2,1)S(1)} %bitcast.138), channel_id=1, source_target_pairs={{0,256},{256,0},{1,257},{257,1},{2,258},{258,2},{3,259},{259,3},{4... | collective-permute-start | bytes 786440 | tf_op jit(solution)/shard_map/ppermute | solution.py:141
  82.7 12.8 %collective-permute-start.2 = (bf16[2,16,2,2,512]{4,3,2,1,0:T(2,128)(2,1)S(1)}, bf16[2,16,2,2,512]{4,3,2,1,0:T(2,128)(2,1)S(1)}, u32[]{:S(2)}, u32[]{:S(2)}) collective-permute-start(bf16[2,16,2,2,512]{4,3,2,1,0:T(2,128)(2,1)S(1)} %get-tuple-element.27), channel_id=1, source_target_pairs={{0,128},{64,192},{128,0},{192,64},{1,129},{65,193},{129,1},{193,65... | collective-permute-start | bytes 393224 | tf_op jit(solution)/shard_map/ppermute | solution.py:148
  87.8 7.7 %collective-permute-start.3 = (bf16[2,16,2,2,512]{4,3,2,1,0:T(2,128)(2,1)S(1)}, bf16[2,16,2,2,512]{4,3,2,1,0:T(2,128)(2,1)S(1)}, u32[]{:S(2)}, u32[]{:S(2)}) collective-permute-start(bf16[2,16,2,2,512]{4,3,2,1,0:T(2,128)(2,1)S(1)} %get-tuple-element.28), channel_id=1, source_target_pairs={{0,192},{64,0},{128,64},{192,128},{1,193},{65,1},{129,65},{193,129... | collective-permute-start | bytes 393224 | tf_op jit(solution)/shard_map/ppermute | solution.py:148
  90.8 8.1 %collective-permute-start.1 = (bf16[2,16,2,2,512]{4,3,2,1,0:T(2,128)(2,1)S(1)}, bf16[2,16,2,2,512]{4,3,2,1,0:T(2,128)(2,1)S(1)}, u32[]{:S(2)}, u32[]{:S(2)}) collective-permute-start(bf16[2,16,2,2,512]{4,3,2,1,0:T(2,128)(2,1)S(1)} %get-tuple-element.26), channel_id=1, source_target_pairs={{0,64},{64,128},{128,192},{192,0},{1,65},{65,129},{129,193},{193,1... | collective-permute-start | bytes 393224 | tf_op jit(solution)/shard_map/ppermute | solution.py:148
  102.4 8.7 %copy-start = (bf16[2,768,1024]{2,1,0:T(8,128)(2,1)S(1)}, bf16[2,768,1024]{2,1,0:T(8,128)(2,1)}, u32[]{:S(2)}) copy-start(bf16[2,768,1024]{2,1,0:T(8,128)(2,1)} %tables.1) | copy-start | bytes 9437188
  102.5 9.5 %collective-permute-start.7 = (bf16[256,512]{0,1:T(8,128)(2,1)S(1)}, bf16[256,512]{0,1:T(8,128)(2,1)S(1)}, u32[]{:S(2)}, u32[]{:S(2)}) collective-permute-start(bf16[256,512]{0,1:T(8,128)(2,1)S(1)} %copy.82), channel_id=1, source_target_pairs={{0,4},{4,8},{8,12},{12,16},{16,20},{20,24},{24,28},{28,32},{32,36}... | collective-permute-start | bytes 786440 | tf_op jit(solution)/shard_map/ppermute | solution.py:188
  107.3 9.5 %collective-permute-start.8 = (bf16[256,512]{0,1:T(8,128)(2,1)S(1)}, bf16[256,512]{0,1:T(8,128)(2,1)S(1)}, u32[]{:S(2)}, u32[]{:S(2)}) collective-permute-start(bf16[256,512]{0,1:T(8,128)(2,1)S(1)} %copy.81), channel_id=1, source_target_pairs={{4,0},{8,4},{12,8},{16,12},{20,16},{24,20},{28,24},{32,28},{36,32}... | collective-permute-start | bytes 786440 | tf_op jit(solution)/shard_map/ppermute | solution.py:189

commit v6 on v5

--- a/solution.py
+++ b/solution.py
@@ -32,60 +32,59 @@
     ).astype(jnp.bfloat16).reshape(2 * harmonics, NT)
 
 
-def tables_kernel(weights_ref, delays_ref, last_ref, here_ref, out_ref, high_ref, low_ref):
+def tables_kernel(weights_ref, delays_ref, table_ref, out_ref):
     station = pl.program_id(0)
-    first = pl.program_id(1) == 0
-    rows = here_ref.shape[0]
+    rows = table_ref.shape[0]
     taps = delays_ref.shape[0]
 
-    @pl.when(first)
-    def _():
-        shape = (2 * BLOCK, BLOCK)
-        lag = (
-            lax.broadcasted_iota(jnp.int32, shape, 1)
-            - lax.broadcasted_iota(jnp.int32, shape, 0)
-            + BLOCK
-        )
+    shape = (2 * BLOCK, BLOCK)
+    lag = (
+        lax.broadcasted_iota(jnp.int32, shape, 1)
+        - lax.broadcasted_iota(jnp.int32, shape, 0)
+        + BLOCK
+    )
+    highs, lows = [], []
+    for part in range(3):
+        neighbour = lax.rem(part + 1 - station, 3)
+        band = jnp.zeros(shape, jnp.float32)
+        for k in range(taps):
+            weight = weights_ref[(neighbour * taps + k) * 2 + station]
+            band += jnp.where(lag == delays_ref[k], weight, 0.0)
+        highs.append(band.astype(jnp.bfloat16))
+        lows.append((band - highs[-1].astype(jnp.float32)).astype(jnp.bfloat16))
+    high = jnp.concatenate(highs, axis=1)
+    low = jnp.concatenate(lows, axis=1)
+
+    for block in range(NT // BLOCK):
+        if block == 0:
+            window, skip = table_ref[:, :BLOCK], BLOCK
+        else:
+            window, skip = table_ref[:, (block - 1) * BLOCK : (block + 1) * BLOCK], 0
+        filtered = jnp.dot(window, high[skip:], preferred_element_type=jnp.float32)
+        filtered += jnp.dot(window, low[skip:], preferred_element_type=jnp.float32)
         for part in range(3):
-            neighbour = lax.rem(part + 1 - station, 3)
-            band = jnp.zeros(shape, jnp.float32)
-            for k in range(taps):
-                weight = weights_ref[(neighbour * taps + k) * 2 + station]
-                band += jnp.where(lag == delays_ref[k], weight, 0.0)
-            high = band.astype(jnp.bfloat16)
-            at = pl.ds(part * BLOCK, BLOCK)
-            high_ref[:, at] = high
-            low_ref[:, at] = (band - high.astype(jnp.float32)).astype(jnp.bfloat16)
-
-    last = jnp.where(first, jnp.zeros_like(last_ref[...]), last_ref[...])
-    window = jnp.concatenate([last, here_ref[...]], axis=1)
-    filtered = jnp.dot(window, high_ref[...], preferred_element_type=jnp.float32)
-    filtered += jnp.dot(window, low_ref[...], preferred_element_type=jnp.float32)
-    for part in range(3):
-        out_ref[0, pl.ds(part * rows, rows)] = filtered[
-            :, part * BLOCK : (part + 1) * BLOCK
-        ].astype(jnp.bfloat16)
+            out_ref[0, pl.ds(part * rows, rows), pl.ds(block * BLOCK, BLOCK)] = filtered[
+                :, part * BLOCK : (part + 1) * BLOCK
+            ].astype(jnp.bfloat16)
 
 
 def filtered_tables(table, weights, tap_delays):
     rows = table.shape[0]
     return pl.pallas_call(
         tables_kernel,
-        grid=(2, NT // BLOCK),
+        grid=(2,),
         out_shape=jax.ShapeDtypeStruct((2, 3 * rows, NT), jnp.bfloat16),
         in_specs=[
             pl.BlockSpec(memory_space=pltpu.SMEM),
             pl.BlockSpec(memory_space=pltpu.SMEM),
-            pl.BlockSpec((rows, BLOCK), lambda s, b: (0, jnp.maximum(b - 1, 0))),
-            pl.BlockSpec((rows, BLOCK), lambda s, b: (0, b)),
+            pl.BlockSpec((rows, NT), lambda s: (0, 0)),
         ],
-        out_specs=pl.BlockSpec((1, 3 * rows, BLOCK), lambda s, b: (s, 0, b)),
-        scratch_shapes=[pltpu.VMEM((2 * BLOCK, 3 * BLOCK), jnp.bfloat16)] * 2,
+        out_specs=pl.BlockSpec((1, 3 * rows, NT), lambda s: (s, 0, 0)),
         cost_estimate=pl.CostEstimate(
             flops=48 * rows * NT * BLOCK, bytes_accessed=16 * rows * NT, transcendentals=0
         ),
         name="tables",
-    )(weights.reshape(-1), tap_delays, table, table)
+    )(weights.reshape(-1), tap_delays, table)
 
 
 def body(operator, recorded, filter_coefficients, tap_delays):

time: 120 us -> 116 us (0.967)
  the two profiles are of different devices: /device:TPU:96 before, /device:TPU:8 now
where the time goes in v6:
time: 116 us; the launch traced here: 115 us
  starting transfers between devices  60 us (52%)
  waiting for transfers between devices  19.9 us (17%)
  matrix products  11.1 us (10%)
  local copies, waits for them, and re-layouts  9.81 us (8%)
  other arithmetic  8.47 us (7%)
  Pallas kernels  5.31 us (5%)
    all_to_all x1, starting transfers between devices, body(): lax.all_to_all(by_target, 'z', split_axis=0, concat_axis=0, tiled=True)  15.2 us
    all_to_all x1, waiting for transfers between devices, body(): lax.all_to_all(by_target, 'z', split_axis=0, concat_axis=0, tiled=True)  12.8 us
    all_to_all x1, starting transfers between devices, body(): lax.all_to_all(spectra, FREQ, split_axis=1, concat_axis=0, tiled=True)  12.2 us
    ppermute x3, starting transfers between devices, body(): piece = natural(lax.ppermute(piece, 'x', links))  11.4 us
    ppermute x3, starting transfers between devices, across(): return with_layout_constraint(lax.ppermute(value, ROW, pairs), plain)  8.36 us
    ppermute x1, starting transfers between devices, body(): after = lax.ppermute(first, FREQ, backward)  7.02 us
    dot_general x4, matrix products, product(): jnp.einsum('qprs,spc->rqc', block, segment[0], preferred_element_type=jnp...  6.47 us
    pallas_call x1, Pallas kernels, filtered_tables(): pl.pallas_call(tables_kernel, grid=(2,), out_shape=jax.ShapeDtypeStruct((...  5.31 us
  transfers between devices with their start and end apart: 11, of which 4 were waited for; matrix products, arithmetic and copies ran while one was open for 23% of the time, Pallas kernels for 5%

profile of v6, /device:TPU:8, one launch (start us, length us, event | category | flops | bytes accessed | tf_op | source)
XLA Modules:
  0.0 115.3 jit_solution(9523581246221546199)
XLA Ops:
  0.0 4.3 %collective-permute-start.5 = (bf16[1,256,2,512]{3,2,1,0:T(2,128)(2,1)}, bf16[1,256,2,512]{3,2,1,0:T(2,128)(2,1)}, u32[]{:S(2)}, u32[]{:S(2)}) collective-permute-start(bf16[1,256,2,512]{3,2,1,0:T(2,128)(2,1)} %param.5), channel_id=1, source_target_pairs={{0,2},{1,3},{2,0},{3,1},{4,6},{5,7},{6,4},{7,5},{8,10},{9,11},{10,... | collective-permute-start | bytes 1572872 | tf_op jit(solution)/shard_map/ppermute | solution.py:101
  4.3 1.9 %collective-permute-start.4 = (bf16[1,256,2,512]{3,2,1,0:T(2,128)(2,1)}, bf16[1,256,2,512]{3,2,1,0:T(2,128)(2,1)}, u32[]{:S(2)}, u32[]{:S(2)}) collective-permute-start(bf16[1,256,2,512]{3,2,1,0:T(2,128)(2,1)} %param.5), channel_id=1, source_target_pairs={{0,1},{1,0},{2,3},{3,2},{4,5},{5,4},{6,7},{7,6},{8,9},{9,8},{10,11... | collective-permute-start | bytes 1572872 | tf_op jit(solution)/shard_map/ppermute | solution.py:101
  6.3 2.3 %copy.67 = bf16[16,8,2,2,512]{4,3,2,1,0:T(2,128)(2,1)} copy(bf16[16,8,2,2,512]{4,3,2,0,1:T(2,128)(2,1)} %bitcast.136) | data formatting | bytes 1048576 | tf_op jit(solution)/shard_map/transpose | solution.py:107
  8.6 15.2 %all-to-all-start = ((bf16[16,8,2,2,512]{4,3,2,1,0:T(2,128)(2,1)}), bf16[16,8,2,2,512]{4,3,2,1,0:T(2,128)(2,1)S(1)}, u32[]{:S(2)}, u32[]{:S(2)}) async-start(bf16[16,8,2,2,512]{4,3,2,1,0:T(2,128)(2,1)} %copy.67), calls=%async_computation | async-start | bytes 1048576 | tf_op jit(solution)/shard_map/all_to_all | solution.py:108
  24.2 2.5 %multiply_convert_fusion.1 = (bf16[128,1,1024]{2,0,1:T(8,128)(2,1)S(1)}, bf16[128,1,1024]{2,0,1:T(8,128)(2,1)S(1)}) fusion(s32[128]{0:T(128)S(1)} %iota_add_fusion), kind=kLoop, calls=%fused_computation.55 | loop fusion | flops 2490368 | bytes 524800 | tf_op jit(solution)/shard_map/convert
  30.2 2.8 %convolution_bitcast_fusion.3 = f32[2,256,512]{2,1,0:T(8,128)} fusion(bf16[1,2,256,256]{3,2,1,0:T(8,128)(2,1)} %get-tuple-element.38, bf16[1,2,256,256]{3,2,1,0:T(8,128)(2,1)} %get-tuple-element.37, bf16[256,2,512]{2,1,0:T(2,128)(2,1)} %bitcast.137), kind=kOutput, calls=%fused_computation.12 | convolution fusion | flops 268697600 | bytes 2097152 | tf_op jit(solution)/shard_map/qprs,spc->rqc/dot_general | solution.py:123
  33.1 2.1 %collective-permute-start.6 = (bf16[1,256,2,512]{3,2,1,0:T(2,128)(2,1)}, bf16[1,256,2,512]{3,2,1,0:T(2,128)(2,1)S(1)}, u32[]{:S(2)}, u32[]{:S(2)}) collective-permute-start(bf16[1,256,2,512]{3,2,1,0:T(2,128)(2,1)} %collective-permute-done.5), channel_id=1, source_target_pairs={{0,1},{1,0},{2,3},{3,2},{4,5},{5,4},{6,7},{7,6},{8,9},{9,8},{10,11... | collective-permute-start | bytes 1572872 | tf_op jit(solution)/shard_map/ppermute | solution.py:101
  35.2 1.7 %convolution_bitcast_fusion.1 = f32[2,256,512]{2,1,0:T(8,128)S(1)} fusion(bf16[1,2,256,256]{3,2,1,0:T(8,128)(2,1)} %get-tuple-element.40, bf16[1,2,256,256]{3,2,1,0:T(8,128)(2,1)} %get-tuple-element.39, bf16[256,2,512]{2,1,0:T(2,128)(2,1)} %bitcast.32), kind=kOutput, calls=%fused_computation.10 | convolution fusion | flops 268697600 | bytes 2097152 | tf_op jit(solution)/shard_map/qprs,spc->rqc/dot_general | solution.py:123
  37.0 1.5 %fusion.5 = f32[2,256,512]{2,1,0:T(8,128)S(1)} fusion(f32[2,256,512]{2,1,0:T(8,128)S(1)} %convolution_bitcast_fusion.1, f32[2,256,512]{2,1,0:T(8,128)S(1)} %copy-done.4, bf16[1,2,256,256]{3,2,1,0:T(8,128)(2,1)S(1)} %copy-done.2, bf16[1,2,256,256]{3,2,1,0:T(8,128)(2,1)S(1)} %get-tuple-element.35, bf16[256,2,512]{2,1,0:T(2,128)(2,1)} %bitcast.26), kind=kOutput, calls=%fused_computation.14 | convolution fusion | flops 269221888 | bytes 4194304 | tf_op jit(solution)/shard_map/qprs,spc->rqc/dot_general | solution.py:123
  39.0 1.3 %copy.78 = bf16[1,256,2,512]{3,2,0,1:T(2,128)(2,1)} copy(bf16[1,256,2,512]{3,1,2,0:T(8,128)(2,1)S(1)} %fusion.8) | data formatting | bytes 1048576 | tf_op jit(solution)/shard_map/broadcast_in_dim | solution.py:129
  40.3 12.8 %all-to-all-done = bf16[16,8,2,2,512]{4,3,2,1,0:T(2,128)(2,1)S(1)} async-done(((bf16[16,8,2,2,512]{4,3,2,1,0:T(2,128)(2,1)}), bf16[16,8,2,2,512]{4,3,2,1,0:T(2,128)(2,1)S(1)}, u32[]{:S(2)}, u32[]{:S(2)}) %all-to-all-start) | async-done | bytes 524320 | tf_op jit(solution)/shard_map/all_to_all | solution.py:108
  53.1 12.2 %all-to-all-start.1 = ((bf16[1,256,2,512]{3,2,0,1:T(2,128)(2,1)}), bf16[1,256,2,512]{3,2,0,1:T(2,128)(2,1)S(1)}, u32[]{:S(2)}, u32[]{:S(2)}) async-start(bf16[1,256,2,512]{3,2,0,1:T(2,128)(2,1)} %copy.78), calls=%async_computation.1 | async-start | bytes 1048576 | tf_op jit(solution)/shard_map/all_to_all | solution.py:130
  66.9 2.5 %collective-permute-start = (bf16[16,4,2,2,512]{4,3,2,1,0:T(2,128)(2,1)S(1)}, bf16[16,4,2,2,512]{4,3,2,1,0:T(2,128)(2,1)S(1)}, u32[]{:S(2)}, u32[]{:S(2)}) collective-permute-start(bf16[16,4,2,2,512]{4,3,2,1,0:T(2,128)(2,1)S(1)} %bitcast.138), channel_id=1, source_target_pairs={{0,256},{256,0},{1,257},{257,1},{2,258},{258,2},{3,259},{259,3},{4... | collective-permute-start | bytes 786440 | tf_op jit(solution)/shard_map/ppermute | solution.py:140
  69.4 5.3 %tables.1 = bf16[2,768,1024]{2,1,0:T(8,128)(2,1)} custom-call(f32[48]{0:T(128)} %reshape.128.weights_ref, s32[8]{0:T(128)} %delays_ref.1, bf16[256,1024]{1,0:T(8,128)(2,1)} %copy-done.1), custom_call_target="tpu_custom_call" | custom-call | flops 1610612736 | bytes 4194304 | tf_op jit(solution)/shard_map/tables/pallas_call | solution.py:73
  75.0 3.2 %collective-permute-done = bf16[16,4,2,2,512]{4,3,2,1,0:T(2,128)(2,1)S(1)} collective-permute-done((bf16[16,4,2,2,512]{4,3,2,1,0:T(2,128)(2,1)S(1)}, bf16[16,4,2,2,512]{4,3,2,1,0:T(2,128)(2,1)S(1)}, u32[]{:S(2)}, u32[]{:S(2)}) %collective-permute-start) | collective-permute-done | bytes 262176 | tf_op jit(solution)/shard_map/ppermute | solution.py:140
  78.9 5.3 %collective-permute-start.2 = (bf16[2,16,2,2,512]{4,3,2,1,0:T(2,128)(2,1)S(1)}, bf16[2,16,2,2,512]{4,3,2,1,0:T(2,128)(2,1)S(1)}, u32[]{:S(2)}, u32[]{:S(2)}) collective-permute-start(bf16[2,16,2,2,512]{4,3,2,1,0:T(2,128)(2,1)S(1)} %get-tuple-element.27), channel_id=1, source_target_pairs={{0,128},{64,192},{128,0},{192,64},{1,129},{65,193},{129,1},{193,65... | collective-permute-start | bytes 393224 | tf_op jit(solution)/shard_map/ppermute | solution.py:147
  84.3 3.0 %collective-permute-start.3 = (bf16[2,16,2,2,512]{4,3,2,1,0:T(2,128)(2,1)S(1)}, bf16[2,16,2,2,512]{4,3,2,1,0:T(2,128)(2,1)S(1)}, u32[]{:S(2)}, u32[]{:S(2)}) collective-permute-start(bf16[2,16,2,2,512]{4,3,2,1,0:T(2,128)(2,1)S(1)} %get-tuple-element.28), channel_id=1, source_target_pairs={{0,192},{64,0},{128,64},{192,128},{1,193},{65,1},{129,65},{193,129... | collective-permute-start | bytes 393224 | tf_op jit(solution)/shard_map/ppermute | solution.py:147
  87.3 3.0 %collective-permute-start.1 = (bf16[2,16,2,2,512]{4,3,2,1,0:T(2,128)(2,1)S(1)}, bf16[2,16,2,2,512]{4,3,2,1,0:T(2,128)(2,1)S(1)}, u32[]{:S(2)}, u32[]{:S(2)}) collective-permute-start(bf16[2,16,2,2,512]{4,3,2,1,0:T(2,128)(2,1)S(1)} %get-tuple-element.26), channel_id=1, source_target_pairs={{0,64},{64,128},{128,192},{192,0},{1,65},{65,129},{129,193},{193,1... | collective-permute-start | bytes 393224 | tf_op jit(solution)/shard_map/ppermute | solution.py:147
  92.0 3.3 %collective-permute-done.1 = bf16[2,16,2,2,512]{4,3,2,1,0:T(2,128)(2,1)S(1)} collective-permute-done((bf16[2,16,2,2,512]{4,3,2,1,0:T(2,128)(2,1)S(1)}, bf16[2,16,2,2,512]{4,3,2,1,0:T(2,128)(2,1)S(1)}, u32[]{:S(2)}, u32[]{:S(2)}) %collective-permute-start.1) | collective-permute-done | bytes 131104 | tf_op jit(solution)/shard_map/ppermute | solution.py:147
  95.4 1.0 pad_maximum_fusion.1
  99.0 3.3 %collective-permute-start.7 = (bf16[256,512]{0,1:T(8,128)(2,1)S(1)}, bf16[256,512]{0,1:T(8,128)(2,1)S(1)}, u32[]{:S(2)}, u32[]{:S(2)}) collective-permute-start(bf16[256,512]{0,1:T(8,128)(2,1)S(1)} %copy.82), channel_id=1, source_target_pairs={{0,4},{4,8},{8,12},{12,16},{16,20},{20,24},{24,28},{28,32},{32,36}... | collective-permute-start | bytes 786440 | tf_op jit(solution)/shard_map/ppermute | solution.py:187
  102.3 7.0 %collective-permute-start.8 = (bf16[256,512]{0,1:T(8,128)(2,1)S(1)}, bf16[256,512]{0,1:T(8,128)(2,1)S(1)}, u32[]{:S(2)}, u32[]{:S(2)}) collective-permute-start(bf16[256,512]{0,1:T(8,128)(2,1)S(1)} %copy.81), channel_id=1, source_target_pairs={{4,0},{8,4},{12,8},{16,12},{20,16},{24,20},{28,24},{32,28},{36,32}... | collective-permute-start | bytes 786440 | tf_op jit(solution)/shard_map/ppermute | solution.py:188
  109.3 1.9 %fusion.10 = f32[512,1024]{1,0:T(8,128)S(1)} fusion(bf16[2,768,1024]{2,1,0:T(8,128)(2,1)} %tables.1, bf16[256,512]{0,1:T(8,128)(2,1)S(1)} %copy.82, bf16[256,512]{0,1:T(8,128)(2,1)S(1)} %copy.81), kind=kOutput, calls=%fused_computation.21 | convolution fusion | flops 537919488 | bytes 3670016 | tf_op jit(solution)/shard_map/dot_general | solution.py:167
  113.7 1.5 %pad_maximum_fusion = bf16[2,512,1024]{2,1,0:T(8,128)(2,1)} fusion(bf16[1,512,1024]{2,1,0:T(8,128)(2,1)S(1)} %fusion.2, bf16[1,512,1024]{2,1,0:T(8,128)(2,1)S(1)} %fusion.3), kind=kLoop, calls=%fused_computation.4 | loop fusion | flops 1048576 | bytes 4194304 | tf_op jit(solution)/shard_map/stack | solution.py:198
  (61 shorter events, 13.5 us)
Async XLA Ops:
  0.0 23.9 %copy-start.3 = (bf16[1,256,2,1024]{3,2,1,0:T(2,128)(2,1)S(1)}, bf16[1,256,2,1024]{3,2,1,0:T(2,128)(2,1)}, u32[]{:S(2)}) copy-start(bf16[1,256,2,1024]{3,2,1,0:T(2,128)(2,1)} %param.4) | copy-start | bytes 3145732
  0.0 33.0 %collective-permute-start.5 = (bf16[1,256,2,512]{3,2,1,0:T(2,128)(2,1)}, bf16[1,256,2,512]{3,2,1,0:T(2,128)(2,1)}, u32[]{:S(2)}, u32[]{:S(2)}) collective-permute-start(bf16[1,256,2,512]{3,2,1,0:T(2,128)(2,1)} %param.5), channel_id=1, source_target_pairs={{0,2},{1,3},{2,0},{3,1},{4,6},{5,7},{6,4},{7,5},{8,10},{9,11},{10,... | collective-permute-start | bytes 1572872 | tf_op jit(solution)/shard_map/ppermute | solution.py:101
  4.3 32.6 %collective-permute-start.4 = (bf16[1,256,2,512]{3,2,1,0:T(2,128)(2,1)}, bf16[1,256,2,512]{3,2,1,0:T(2,128)(2,1)}, u32[]{:S(2)}, u32[]{:S(2)}) collective-permute-start(bf16[1,256,2,512]{3,2,1,0:T(2,128)(2,1)} %param.5), channel_id=1, source_target_pairs={{0,1},{1,0},{2,3},{3,2},{4,5},{5,4},{6,7},{7,6},{8,9},{9,8},{10,11... | collective-permute-start | bytes 1572872 | tf_op jit(solution)/shard_map/ppermute | solution.py:101
  8.6 44.5 %all-to-all-start = ((bf16[16,8,2,2,512]{4,3,2,1,0:T(2,128)(2,1)}), bf16[16,8,2,2,512]{4,3,2,1,0:T(2,128)(2,1)S(1)}, u32[]{:S(2)}, u32[]{:S(2)}) async-start(bf16[16,8,2,2,512]{4,3,2,1,0:T(2,128)(2,1)} %copy.67), calls=%async_computation | async-start | bytes 1048576 | tf_op jit(solution)/shard_map/all_to_all | solution.py:108
  30.2 39.2 %copy-start.1 = (bf16[256,1024]{1,0:T(8,128)(2,1)}, bf16[256,1024]{1,0:T(8,128)(2,1)S(1)}, u32[]{:S(2)}) copy-start(bf16[256,1024]{1,0:T(8,128)(2,1)S(1)} %convert_element_type.46.table_ref) | copy-start | bytes 1572868
  30.2 6.7 %copy-start.2 = (bf16[1,2,256,256]{3,2,1,0:T(8,128)(2,1)S(1)}, bf16[1,2,256,256]{3,2,1,0:T(8,128)(2,1)}, u32[]{:S(2)}) copy-start(bf16[1,2,256,256]{3,2,1,0:T(8,128)(2,1)} %get-tuple-element.36) | copy-start | bytes 786436
  33.1 5.4 %collective-permute-start.6 = (bf16[1,256,2,512]{3,2,1,0:T(2,128)(2,1)}, bf16[1,256,2,512]{3,2,1,0:T(2,128)(2,1)S(1)}, u32[]{:S(2)}, u32[]{:S(2)}) collective-permute-start(bf16[1,256,2,512]{3,2,1,0:T(2,128)(2,1)} %collective-permute-done.5), channel_id=1, source_target_pairs={{0,1},{1,0},{2,3},{3,2},{4,5},{5,4},{6,7},{7,6},{8,9},{9,8},{10,11... | collective-permute-start | bytes 1572872 | tf_op jit(solution)/shard_map/ppermute | solution.py:101
  35.2 1.8 %copy-start.4 = (f32[2,256,512]{2,1,0:T(8,128)S(1)}, f32[2,256,512]{2,1,0:T(8,128)}, u32[]{:S(2)}) copy-start(f32[2,256,512]{2,1,0:T(8,128)} %convolution_bitcast_fusion.3) | copy-start | bytes 3145732
  38.5 26.9 %copy-start.5 = (f32[3,8,2]{1,2,0:T(2,128)S(1)}, f32[3,8,2]{1,2,0:T(2,128)}, u32[]{:S(2)}) copy-start(f32[3,8,2]{1,2,0:T(2,128)} %param.6) | copy-start | bytes 580
  53.1 45.0 %all-to-all-start.1 = ((bf16[1,256,2,512]{3,2,0,1:T(2,128)(2,1)}), bf16[1,256,2,512]{3,2,0,1:T(2,128)(2,1)S(1)}, u32[]{:S(2)}, u32[]{:S(2)}) async-start(bf16[1,256,2,512]{3,2,0,1:T(2,128)(2,1)} %copy.78), calls=%async_computation.1 | async-start | bytes 1048576 | tf_op jit(solution)/shard_map/all_to_all | solution.py:130
  66.9 11.3 %collective-permute-start = (bf16[16,4,2,2,512]{4,3,2,1,0:T(2,128)(2,1)S(1)}, bf16[16,4,2,2,512]{4,3,2,1,0:T(2,128)(2,1)S(1)}, u32[]{:S(2)}, u32[]{:S(2)}) collective-permute-start(bf16[16,4,2,2,512]{4,3,2,1,0:T(2,128)(2,1)S(1)} %bitcast.138), channel_id=1, source_target_pairs={{0,256},{256,0},{1,257},{257,1},{2,258},{258,2},{3,259},{259,3},{4... | collective-permute-start | bytes 786440 | tf_op jit(solution)/shard_map/ppermute | solution.py:140
  78.9 13.1 %collective-permute-start.2 = (bf16[2,16,2,2,512]{4,3,2,1,0:T(2,128)(2,1)S(1)}, bf16[2,16,2,2,512]{4,3,2,1,0:T(2,128)(2,1)S(1)}, u32[]{:S(2)}, u32[]{:S(2)}) collective-permute-start(bf16[2,16,2,2,512]{4,3,2,1,0:T(2,128)(2,1)S(1)} %get-tuple-element.27), channel_id=1, source_target_pairs={{0,128},{64,192},{128,0},{192,64},{1,129},{65,193},{129,1},{193,65... | collective-permute-start | bytes 393224 | tf_op jit(solution)/shard_map/ppermute | solution.py:147
  84.3 7.7 %collective-permute-start.3 = (bf16[2,16,2,2,512]{4,3,2,1,0:T(2,128)(2,1)S(1)}, bf16[2,16,2,2,512]{4,3,2,1,0:T(2,128)(2,1)S(1)}, u32[]{:S(2)}, u32[]{:S(2)}) collective-permute-start(bf16[2,16,2,2,512]{4,3,2,1,0:T(2,128)(2,1)S(1)} %get-tuple-element.28), channel_id=1, source_target_pairs={{0,192},{64,0},{128,64},{192,128},{1,193},{65,1},{129,65},{193,129... | collective-permute-start | bytes 393224 | tf_op jit(solution)/shard_map/ppermute | solution.py:147
  87.3 8.1 %collective-permute-start.1 = (bf16[2,16,2,2,512]{4,3,2,1,0:T(2,128)(2,1)S(1)}, bf16[2,16,2,2,512]{4,3,2,1,0:T(2,128)(2,1)S(1)}, u32[]{:S(2)}, u32[]{:S(2)}) collective-permute-start(bf16[2,16,2,2,512]{4,3,2,1,0:T(2,128)(2,1)S(1)} %get-tuple-element.26), channel_id=1, source_target_pairs={{0,64},{64,128},{128,192},{192,0},{1,65},{65,129},{129,193},{193,1... | collective-permute-start | bytes 393224 | tf_op jit(solution)/shard_map/ppermute | solution.py:147
  99.0 12.3 %copy-start = (bf16[2,768,1024]{2,1,0:T(8,128)(2,1)S(1)}, bf16[2,768,1024]{2,1,0:T(8,128)(2,1)}, u32[]{:S(2)}) copy-start(bf16[2,768,1024]{2,1,0:T(8,128)(2,1)} %tables.1) | copy-start | bytes 9437188
  99.0 13.0 %collective-permute-start.7 = (bf16[256,512]{0,1:T(8,128)(2,1)S(1)}, bf16[256,512]{0,1:T(8,128)(2,1)S(1)}, u32[]{:S(2)}, u32[]{:S(2)}) collective-permute-start(bf16[256,512]{0,1:T(8,128)(2,1)S(1)} %copy.82), channel_id=1, source_target_pairs={{0,4},{4,8},{8,12},{12,16},{16,20},{20,24},{24,28},{28,32},{32,36}... | collective-permute-start | bytes 786440 | tf_op jit(solution)/shard_map/ppermute | solution.py:187
  102.3 10.9 %collective-permute-start.8 = (bf16[256,512]{0,1:T(8,128)(2,1)S(1)}, bf16[256,512]{0,1:T(8,128)(2,1)S(1)}, u32[]{:S(2)}, u32[]{:S(2)}) collective-permute-start(bf16[256,512]{0,1:T(8,128)(2,1)S(1)} %copy.81), channel_id=1, source_target_pairs={{4,0},{8,4},{12,8},{16,12},{20,16},{24,20},{28,24},{32,28},{36,32}... | collective-permute-start | bytes 786440 | tf_op jit(solution)/shard_map/ppermute | solution.py:188

commit v7 on v6

--- a/solution.py
+++ b/solution.py
@@ -190,12 +190,14 @@
     rest = [
         data[s].astype(jnp.float32) - to_time(own, basis[s, : 2 * rows]) for s in range(2)
     ]
-    result = []
+    result = lax.optimization_barrier(jnp.zeros((2, columns, NT), jnp.bfloat16))
     for s, halo in enumerate((before, after)):
         residual = rest[s] - to_time(turned(halo), basis[s, 2 * rows :])
         shrunk = residual - jnp.clip(residual, -shrink_level, shrink_level)
-        result.append(shrunk.astype(jnp.bfloat16))
-    return jnp.stack(result)
+        result = lax.dynamic_update_index_in_dim(
+            result, shrunk.astype(jnp.bfloat16), s, axis=0
+        )
+    return result
 
 
 def solution(mesh):

time: 116 us -> 116 us (level)
  other arithmetic: 8.47 us -> 6.92 us
  local copies, waits for them, and re-layouts: 9.81 us -> 11.2 us
    another operation x2 -> x1, other arithmetic: 3.96 us -> 2.46 us
    unnamed x22 -> x28, local copies, waits for them, and re-layouts: 1.67 us -> 2.87 us
  transfers between devices with their start and end apart: 11 -> 11, of which waited for: 4 -> 5; matrix products, arithmetic and copies ran while one was open for 23% -> 23% of each run, Pallas kernels for 5% -> 5%
where the time goes in v7:
time: 116 us
  starting transfers between devices  59.4 us (51%)
  waiting for transfers between devices  20.3 us (18%)
  matrix products  11.8 us (10%)
  local copies, waits for them, and re-layouts  11.2 us (10%)
  other arithmetic  6.92 us (6%)
  Pallas kernels  5.32 us (5%)
    all_to_all x1, starting transfers between devices, body(): lax.all_to_all(by_target, 'z', split_axis=0, concat_axis=0, tiled=True)  15.2 us
    all_to_all x1, waiting for transfers between devices, body(): lax.all_to_all(by_target, 'z', split_axis=0, concat_axis=0, tiled=True)  12.9 us
    all_to_all x1, starting transfers between devices, body(): lax.all_to_all(spectra, FREQ, split_axis=1, concat_axis=0, tiled=True)  12.2 us
    ppermute x3, starting transfers between devices, body(): piece = natural(lax.ppermute(piece, 'x', links))  10.8 us
    ppermute x3, starting transfers between devices, across(): return with_layout_constraint(lax.ppermute(value, ROW, pairs), plain)  8.36 us
    ppermute x1, starting transfers between devices, body(): after = lax.ppermute(first, FREQ, backward)  6.79 us
    dot_general x4, matrix products, product(): jnp.einsum('qprs,spc->rqc', block, segment[0], preferred_element_type=jnp...  6.15 us
    dot_general x6, matrix products, to_time(): jnp.dot(spectra, basis, preferred_element_type=jnp.float32)  5.6 us
  transfers between devices with their start and end apart: 11, of which 5 were waited for; matrix products, arithmetic and copies ran while one was open for 23% of the time, Pallas kernels for 5%

profile of v7, /device:TPU:8, one launch (start us, length us, event | category | flops | bytes accessed | tf_op | source)
XLA Modules:
  0.0 115.5 jit_solution(1899335385521259707)
XLA Ops:
  0.0 4.3 %collective-permute-start.5 = (bf16[1,256,2,512]{3,2,1,0:T(2,128)(2,1)}, bf16[1,256,2,512]{3,2,1,0:T(2,128)(2,1)}, u32[]{:S(2)}, u32[]{:S(2)}) collective-permute-start(bf16[1,256,2,512]{3,2,1,0:T(2,128)(2,1)} %param.5), channel_id=1, source_target_pairs={{0,2},{1,3},{2,0},{3,1},{4,6},{5,7},{6,4},{7,5},{8,10},{9,11},{10,... | collective-permute-start | bytes 1572872 | tf_op jit(solution)/shard_map/ppermute | solution.py:101
  4.3 1.9 %collective-permute-start.4 = (bf16[1,256,2,512]{3,2,1,0:T(2,128)(2,1)}, bf16[1,256,2,512]{3,2,1,0:T(2,128)(2,1)}, u32[]{:S(2)}, u32[]{:S(2)}) collective-permute-start(bf16[1,256,2,512]{3,2,1,0:T(2,128)(2,1)} %param.5), channel_id=1, source_target_pairs={{0,1},{1,0},{2,3},{3,2},{4,5},{5,4},{6,7},{7,6},{8,9},{9,8},{10,11... | collective-permute-start | bytes 1572872 | tf_op jit(solution)/shard_map/ppermute | solution.py:101
  6.3 2.3 %copy.67 = bf16[16,8,2,2,512]{4,3,2,1,0:T(2,128)(2,1)} copy(bf16[16,8,2,2,512]{4,3,2,0,1:T(2,128)(2,1)} %bitcast.140) | data formatting | bytes 1048576 | tf_op jit(solution)/shard_map/transpose | solution.py:107
  8.6 15.2 %all-to-all-start = ((bf16[16,8,2,2,512]{4,3,2,1,0:T(2,128)(2,1)}), bf16[16,8,2,2,512]{4,3,2,1,0:T(2,128)(2,1)S(1)}, u32[]{:S(2)}, u32[]{:S(2)}) async-start(bf16[16,8,2,2,512]{4,3,2,1,0:T(2,128)(2,1)} %copy.67), calls=%async_computation | async-start | bytes 1048576 | tf_op jit(solution)/shard_map/all_to_all | solution.py:108
  24.1 2.5 %multiply_convert_fusion.1 = (bf16[128,1,1024]{2,0,1:T(8,128)(2,1)S(1)}, bf16[128,1,1024]{2,0,1:T(8,128)(2,1)S(1)}) fusion(s32[128]{0:T(128)S(1)} %iota_add_fusion), kind=kLoop, calls=%fused_computation.56 | loop fusion | flops 2490368 | bytes 524800 | tf_op jit(solution)/shard_map/convert
  30.4 2.5 %convolution_bitcast_fusion.3 = f32[2,256,512]{2,1,0:T(8,128)} fusion(bf16[1,2,256,256]{3,2,1,0:T(8,128)(2,1)S(1)} %copy-done.7, bf16[1,2,256,256]{3,2,1,0:T(8,128)(2,1)S(1)} %copy-done.6, bf16[256,2,512]{2,1,0:T(2,128)(2,1)} %bitcast.141), kind=kOutput, calls=%fused_computation.13 | convolution fusion | flops 268697600 | bytes 2097152 | tf_op jit(solution)/shard_map/qprs,spc->rqc/dot_general | solution.py:123
  32.9 2.1 %collective-permute-start.6 = (bf16[1,256,2,512]{3,2,1,0:T(2,128)(2,1)}, bf16[1,256,2,512]{3,2,1,0:T(2,128)(2,1)S(1)}, u32[]{:S(2)}, u32[]{:S(2)}) collective-permute-start(bf16[1,256,2,512]{3,2,1,0:T(2,128)(2,1)} %collective-permute-done.5), channel_id=1, source_target_pairs={{0,1},{1,0},{2,3},{3,2},{4,5},{5,4},{6,7},{7,6},{8,9},{9,8},{10,11... | collective-permute-start | bytes 1572872 | tf_op jit(solution)/shard_map/ppermute | solution.py:101
  35.1 1.7 %convolution_bitcast_fusion.1 = f32[2,256,512]{2,1,0:T(8,128)S(1)} fusion(bf16[1,2,256,256]{3,2,1,0:T(8,128)(2,1)} %get-tuple-element.40, bf16[1,2,256,256]{3,2,1,0:T(8,128)(2,1)} %get-tuple-element.39, bf16[256,2,512]{2,1,0:T(2,128)(2,1)} %bitcast.32), kind=kOutput, calls=%fused_computation.11 | convolution fusion | flops 268697600 | bytes 2097152 | tf_op jit(solution)/shard_map/qprs,spc->rqc/dot_general | solution.py:123
  36.9 1.5 %fusion.7 = f32[2,256,512]{2,1,0:T(8,128)S(1)} fusion(f32[2,256,512]{2,1,0:T(8,128)S(1)} %convolution_bitcast_fusion.1, f32[2,256,512]{2,1,0:T(8,128)S(1)} %copy-done.5, bf16[1,2,256,256]{3,2,1,0:T(8,128)(2,1)S(1)} %copy-done.3, bf16[1,2,256,256]{3,2,1,0:T(8,128)(2,1)S(1)} %get-tuple-element.35, bf16[256,2,512]{2,1,0:T(2,128)(2,1)} %bitcast.26), kind=kOutput, calls=%fused_computation.15 | convolution fusion | flops 269221888 | bytes 4194304 | tf_op jit(solution)/shard_map/qprs,spc->rqc/dot_general | solution.py:123
  38.8 1.3 %copy.78 = bf16[1,256,2,512]{3,2,0,1:T(2,128)(2,1)} copy(bf16[1,256,2,512]{3,1,2,0:T(8,128)(2,1)S(1)} %fusion.10) | data formatting | bytes 1048576 | tf_op jit(solution)/shard_map/broadcast_in_dim | solution.py:129
  40.2 12.9 %all-to-all-done = bf16[16,8,2,2,512]{4,3,2,1,0:T(2,128)(2,1)S(1)} async-done(((bf16[16,8,2,2,512]{4,3,2,1,0:T(2,128)(2,1)}), bf16[16,8,2,2,512]{4,3,2,1,0:T(2,128)(2,1)S(1)}, u32[]{:S(2)}, u32[]{:S(2)}) %all-to-all-start) | async-done | bytes 524320 | tf_op jit(solution)/shard_map/all_to_all | solution.py:108
  53.1 12.2 %all-to-all-start.1 = ((bf16[1,256,2,512]{3,2,0,1:T(2,128)(2,1)}), bf16[1,256,2,512]{3,2,0,1:T(2,128)(2,1)S(1)}, u32[]{:S(2)}, u32[]{:S(2)}) async-start(bf16[1,256,2,512]{3,2,0,1:T(2,128)(2,1)} %copy.78), calls=%async_computation.1 | async-start | bytes 1048576 | tf_op jit(solution)/shard_map/all_to_all | solution.py:130
  66.8 2.5 %collective-permute-start = (bf16[16,4,2,2,512]{4,3,2,1,0:T(2,128)(2,1)S(1)}, bf16[16,4,2,2,512]{4,3,2,1,0:T(2,128)(2,1)S(1)}, u32[]{:S(2)}, u32[]{:S(2)}) collective-permute-start(bf16[16,4,2,2,512]{4,3,2,1,0:T(2,128)(2,1)S(1)} %bitcast.142), channel_id=1, source_target_pairs={{0,256},{256,0},{1,257},{257,1},{2,258},{258,2},{3,259},{259,3},{4... | collective-permute-start | bytes 786440 | tf_op jit(solution)/shard_map/ppermute | solution.py:140
  69.3 5.3 %tables.1 = bf16[2,768,1024]{2,1,0:T(8,128)(2,1)} custom-call(f32[48]{0:T(128)} %reshape.128.weights_ref, s32[8]{0:T(128)} %delays_ref.1, bf16[256,1024]{1,0:T(8,128)(2,1)} %copy-done.1), custom_call_target="tpu_custom_call" | custom-call | flops 1610612736 | bytes 4194304 | tf_op jit(solution)/shard_map/tables/pallas_call | solution.py:73
  74.9 3.2 %collective-permute-done = bf16[16,4,2,2,512]{4,3,2,1,0:T(2,128)(2,1)S(1)} collective-permute-done((bf16[16,4,2,2,512]{4,3,2,1,0:T(2,128)(2,1)S(1)}, bf16[16,4,2,2,512]{4,3,2,1,0:T(2,128)(2,1)S(1)}, u32[]{:S(2)}, u32[]{:S(2)}) %collective-permute-start) | collective-permute-done | bytes 262176 | tf_op jit(solution)/shard_map/ppermute | solution.py:140
  78.9 5.2 %collective-permute-start.3 = (bf16[2,16,2,2,512]{4,3,2,1,0:T(2,128)(2,1)S(1)}, bf16[2,16,2,2,512]{4,3,2,1,0:T(2,128)(2,1)S(1)}, u32[]{:S(2)}, u32[]{:S(2)}) collective-permute-start(bf16[2,16,2,2,512]{4,3,2,1,0:T(2,128)(2,1)S(1)} %get-tuple-element.28), channel_id=1, source_target_pairs={{0,192},{64,0},{128,64},{192,128},{1,193},{65,1},{129,65},{193,129... | collective-permute-start | bytes 393224 | tf_op jit(solution)/shard_map/ppermute | solution.py:147
  84.1 2.5 %collective-permute-start.2 = (bf16[2,16,2,2,512]{4,3,2,1,0:T(2,128)(2,1)S(1)}, bf16[2,16,2,2,512]{4,3,2,1,0:T(2,128)(2,1)S(1)}, u32[]{:S(2)}, u32[]{:S(2)}) collective-permute-start(bf16[2,16,2,2,512]{4,3,2,1,0:T(2,128)(2,1)S(1)} %get-tuple-element.27), channel_id=1, source_target_pairs={{0,128},{64,192},{128,0},{192,64},{1,129},{65,193},{129,1},{193,65... | collective-permute-start | bytes 393224 | tf_op jit(solution)/shard_map/ppermute | solution.py:147
  86.6 3.1 %collective-permute-start.1 = (bf16[2,16,2,2,512]{4,3,2,1,0:T(2,128)(2,1)S(1)}, bf16[2,16,2,2,512]{4,3,2,1,0:T(2,128)(2,1)S(1)}, u32[]{:S(2)}, u32[]{:S(2)}) collective-permute-start(bf16[2,16,2,2,512]{4,3,2,1,0:T(2,128)(2,1)S(1)} %get-tuple-element.26), channel_id=1, source_target_pairs={{0,64},{64,128},{128,192},{192,0},{1,65},{65,129},{129,193},{193,1... | collective-permute-start | bytes 393224 | tf_op jit(solution)/shard_map/ppermute | solution.py:147
  91.3 2.5 %collective-permute-done.2 = bf16[2,16,2,2,512]{4,3,2,1,0:T(2,128)(2,1)S(1)} collective-permute-done((bf16[2,16,2,2,512]{4,3,2,1,0:T(2,128)(2,1)S(1)}, bf16[2,16,2,2,512]{4,3,2,1,0:T(2,128)(2,1)S(1)}, u32[]{:S(2)}, u32[]{:S(2)}) %collective-permute-start.2) | collective-permute-done | bytes 131104 | tf_op jit(solution)/shard_map/ppermute | solution.py:147
  93.8 1.4 %collective-permute-done.1 = bf16[2,16,2,2,512]{4,3,2,1,0:T(2,128)(2,1)S(1)} collective-permute-done((bf16[2,16,2,2,512]{4,3,2,1,0:T(2,128)(2,1)S(1)}, bf16[2,16,2,2,512]{4,3,2,1,0:T(2,128)(2,1)S(1)}, u32[]{:S(2)}, u32[]{:S(2)}) %collective-permute-start.1) | collective-permute-done | bytes 131104 | tf_op jit(solution)/shard_map/ppermute | solution.py:147
  98.8 3.5 %collective-permute-start.7 = (bf16[256,512]{0,1:T(8,128)(2,1)S(1)}, bf16[256,512]{0,1:T(8,128)(2,1)S(1)}, u32[]{:S(2)}, u32[]{:S(2)}) collective-permute-start(bf16[256,512]{0,1:T(8,128)(2,1)S(1)} %copy.82), channel_id=1, source_target_pairs={{0,4},{4,8},{8,12},{12,16},{16,20},{20,24},{24,28},{28,32},{32,36}... | collective-permute-start | bytes 786440 | tf_op jit(solution)/shard_map/ppermute | solution.py:187
  102.4 6.8 %collective-permute-start.8 = (bf16[256,512]{0,1:T(8,128)(2,1)S(1)}, bf16[256,512]{0,1:T(8,128)(2,1)S(1)}, u32[]{:S(2)}, u32[]{:S(2)}) collective-permute-start(bf16[256,512]{0,1:T(8,128)(2,1)S(1)} %copy.81), channel_id=1, source_target_pairs={{4,0},{8,4},{12,8},{16,12},{20,16},{24,20},{28,24},{32,28},{36,32}... | collective-permute-start | bytes 786440 | tf_op jit(solution)/shard_map/ppermute | solution.py:188
  109.2 1.9 %fusion.12 = f32[512,1024]{1,0:T(8,128)S(1)} fusion(bf16[2,768,1024]{2,1,0:T(8,128)(2,1)} %tables.1, bf16[256,512]{0,1:T(8,128)(2,1)S(1)} %copy.82, bf16[256,512]{0,1:T(8,128)(2,1)S(1)} %copy.81), kind=kOutput, calls=%fused_computation.22 | convolution fusion | flops 537919488 | bytes 3670016 | tf_op jit(solution)/shard_map/dot_general | solution.py:167
  114.0 1.5 %fusion.3 = bf16[2,512,1024]{2,1,0:T(8,128)(2,1)} fusion(bf16[2,512,1024]{2,1,0:T(8,128)(2,1)} %copy-done.2, f32[512,1024]{1,0:T(8,128)S(1)} %fusion.11, bf16[512,1024]{1,0:T(8,128)(2,1)S(1)} %convolution_convert_fusion, bf16[2,768,1024]{2,1,0:T(8,128)(2,1)S(1)} %copy-done, bf16[256,512]{0,1:T(8,128)(2,1)S(1)} %collective-permute-done.8), kind=kOutput, calls=%fused_computation.7 | convolution fusion | flops 271581184 | bytes 4980736 | tf_op jit(solution)/shard_map/dot_general | solution.py:167
  (67 shorter events, 14.9 us)
Async XLA Ops:
  0.0 23.8 %copy-start.4 = (bf16[1,256,2,1024]{3,2,1,0:T(2,128)(2,1)S(1)}, bf16[1,256,2,1024]{3,2,1,0:T(2,128)(2,1)}, u32[]{:S(2)}) copy-start(bf16[1,256,2,1024]{3,2,1,0:T(2,128)(2,1)} %param.4) | copy-start | bytes 3145732
  0.0 32.9 %collective-permute-start.5 = (bf16[1,256,2,512]{3,2,1,0:T(2,128)(2,1)}, bf16[1,256,2,512]{3,2,1,0:T(2,128)(2,1)}, u32[]{:S(2)}, u32[]{:S(2)}) collective-permute-start(bf16[1,256,2,512]{3,2,1,0:T(2,128)(2,1)} %param.5), channel_id=1, source_target_pairs={{0,2},{1,3},{2,0},{3,1},{4,6},{5,7},{6,4},{7,5},{8,10},{9,11},{10,... | collective-permute-start | bytes 1572872 | tf_op jit(solution)/shard_map/ppermute | solution.py:101
  4.3 32.5 %collective-permute-start.4 = (bf16[1,256,2,512]{3,2,1,0:T(2,128)(2,1)}, bf16[1,256,2,512]{3,2,1,0:T(2,128)(2,1)}, u32[]{:S(2)}, u32[]{:S(2)}) collective-permute-start(bf16[1,256,2,512]{3,2,1,0:T(2,128)(2,1)} %param.5), channel_id=1, source_target_pairs={{0,1},{1,0},{2,3},{3,2},{4,5},{5,4},{6,7},{7,6},{8,9},{9,8},{10,11... | collective-permute-start | bytes 1572872 | tf_op jit(solution)/shard_map/ppermute | solution.py:101
  8.6 44.5 %all-to-all-start = ((bf16[16,8,2,2,512]{4,3,2,1,0:T(2,128)(2,1)}), bf16[16,8,2,2,512]{4,3,2,1,0:T(2,128)(2,1)S(1)}, u32[]{:S(2)}, u32[]{:S(2)}) async-start(bf16[16,8,2,2,512]{4,3,2,1,0:T(2,128)(2,1)} %copy.67), calls=%async_computation | async-start | bytes 1048576 | tf_op jit(solution)/shard_map/all_to_all | solution.py:108
  29.4 1.0 copy-start.6
  29.4 1.0 copy-start.7
  30.2 39.1 %copy-start.1 = (bf16[256,1024]{1,0:T(8,128)(2,1)}, bf16[256,1024]{1,0:T(8,128)(2,1)S(1)}, u32[]{:S(2)}) copy-start(bf16[256,1024]{1,0:T(8,128)(2,1)S(1)} %convert_element_type.46.table_ref) | copy-start | bytes 1572868
  30.4 6.4 %copy-start.3 = (bf16[1,2,256,256]{3,2,1,0:T(8,128)(2,1)S(1)}, bf16[1,2,256,256]{3,2,1,0:T(8,128)(2,1)}, u32[]{:S(2)}) copy-start(bf16[1,2,256,256]{3,2,1,0:T(8,128)(2,1)} %get-tuple-element.36) | copy-start | bytes 786436
  32.9 5.4 %collective-permute-start.6 = (bf16[1,256,2,512]{3,2,1,0:T(2,128)(2,1)}, bf16[1,256,2,512]{3,2,1,0:T(2,128)(2,1)S(1)}, u32[]{:S(2)}, u32[]{:S(2)}) collective-permute-start(bf16[1,256,2,512]{3,2,1,0:T(2,128)(2,1)} %collective-permute-done.5), channel_id=1, source_target_pairs={{0,1},{1,0},{2,3},{3,2},{4,5},{5,4},{6,7},{7,6},{8,9},{9,8},{10,11... | collective-permute-start | bytes 1572872 | tf_op jit(solution)/shard_map/ppermute | solution.py:101
  35.1 1.8 %copy-start.5 = (f32[2,256,512]{2,1,0:T(8,128)S(1)}, f32[2,256,512]{2,1,0:T(8,128)}, u32[]{:S(2)}) copy-start(f32[2,256,512]{2,1,0:T(8,128)} %convolution_bitcast_fusion.3) | copy-start | bytes 3145732
  38.4 27.1 %copy-start.8 = (f32[3,8,2]{1,2,0:T(2,128)S(1)}, f32[3,8,2]{1,2,0:T(2,128)}, u32[]{:S(2)}) copy-start(f32[3,8,2]{1,2,0:T(2,128)} %param.6) | copy-start | bytes 580
  53.1 44.8 %all-to-all-start.1 = ((bf16[1,256,2,512]{3,2,0,1:T(2,128)(2,1)}), bf16[1,256,2,512]{3,2,0,1:T(2,128)(2,1)S(1)}, u32[]{:S(2)}, u32[]{:S(2)}) async-start(bf16[1,256,2,512]{3,2,0,1:T(2,128)(2,1)} %copy.78), calls=%async_computation.1 | async-start | bytes 1048576 | tf_op jit(solution)/shard_map/all_to_all | solution.py:130
  66.8 11.3 %collective-permute-start = (bf16[16,4,2,2,512]{4,3,2,1,0:T(2,128)(2,1)S(1)}, bf16[16,4,2,2,512]{4,3,2,1,0:T(2,128)(2,1)S(1)}, u32[]{:S(2)}, u32[]{:S(2)}) collective-permute-start(bf16[16,4,2,2,512]{4,3,2,1,0:T(2,128)(2,1)S(1)} %bitcast.142), channel_id=1, source_target_pairs={{0,256},{256,0},{1,257},{257,1},{2,258},{258,2},{3,259},{259,3},{4... | collective-permute-start | bytes 786440 | tf_op jit(solution)/shard_map/ppermute | solution.py:140
  78.9 12.5 %collective-permute-start.3 = (bf16[2,16,2,2,512]{4,3,2,1,0:T(2,128)(2,1)S(1)}, bf16[2,16,2,2,512]{4,3,2,1,0:T(2,128)(2,1)S(1)}, u32[]{:S(2)}, u32[]{:S(2)}) collective-permute-start(bf16[2,16,2,2,512]{4,3,2,1,0:T(2,128)(2,1)S(1)} %get-tuple-element.28), channel_id=1, source_target_pairs={{0,192},{64,0},{128,64},{192,128},{1,193},{65,1},{129,65},{193,129... | collective-permute-start | bytes 393224 | tf_op jit(solution)/shard_map/ppermute | solution.py:147
  84.1 9.7 %collective-permute-start.2 = (bf16[2,16,2,2,512]{4,3,2,1,0:T(2,128)(2,1)S(1)}, bf16[2,16,2,2,512]{4,3,2,1,0:T(2,128)(2,1)S(1)}, u32[]{:S(2)}, u32[]{:S(2)}) collective-permute-start(bf16[2,16,2,2,512]{4,3,2,1,0:T(2,128)(2,1)S(1)} %get-tuple-element.27), channel_id=1, source_target_pairs={{0,128},{64,192},{128,0},{192,64},{1,129},{65,193},{129,1},{193,65... | collective-permute-start | bytes 393224 | tf_op jit(solution)/shard_map/ppermute | solution.py:147
  86.6 8.6 %collective-permute-start.1 = (bf16[2,16,2,2,512]{4,3,2,1,0:T(2,128)(2,1)S(1)}, bf16[2,16,2,2,512]{4,3,2,1,0:T(2,128)(2,1)S(1)}, u32[]{:S(2)}, u32[]{:S(2)}) collective-permute-start(bf16[2,16,2,2,512]{4,3,2,1,0:T(2,128)(2,1)S(1)} %get-tuple-element.26), channel_id=1, source_target_pairs={{0,64},{64,128},{128,192},{192,0},{1,65},{65,129},{129,193},{193,1... | collective-permute-start | bytes 393224 | tf_op jit(solution)/shard_map/ppermute | solution.py:147
  98.8 12.3 %copy-start = (bf16[2,768,1024]{2,1,0:T(8,128)(2,1)S(1)}, bf16[2,768,1024]{2,1,0:T(8,128)(2,1)}, u32[]{:S(2)}) copy-start(bf16[2,768,1024]{2,1,0:T(8,128)(2,1)} %tables.1) | copy-start | bytes 9437188
  98.8 13.0 %collective-permute-start.7 = (bf16[256,512]{0,1:T(8,128)(2,1)S(1)}, bf16[256,512]{0,1:T(8,128)(2,1)S(1)}, u32[]{:S(2)}, u32[]{:S(2)}) collective-permute-start(bf16[256,512]{0,1:T(8,128)(2,1)S(1)} %copy.82), channel_id=1, source_target_pairs={{0,4},{4,8},{8,12},{12,16},{16,20},{20,24},{24,28},{28,32},{32,36}... | collective-permute-start | bytes 786440 | tf_op jit(solution)/shard_map/ppermute | solution.py:187
  102.4 10.7 %collective-permute-start.8 = (bf16[256,512]{0,1:T(8,128)(2,1)S(1)}, bf16[256,512]{0,1:T(8,128)(2,1)S(1)}, u32[]{:S(2)}, u32[]{:S(2)}) collective-permute-start(bf16[256,512]{0,1:T(8,128)(2,1)S(1)} %copy.81), channel_id=1, source_target_pairs={{4,0},{8,4},{12,8},{16,12},{20,16},{24,20},{28,24},{32,28},{36,32}... | collective-permute-start | bytes 786440 | tf_op jit(solution)/shard_map/ppermute | solution.py:188
  112.7 1.3 %copy-start.2 = (bf16[2,512,1024]{2,1,0:T(8,128)(2,1)}, bf16[2,512,1024]{2,1,0:T(8,128)(2,1)S(1)}, u32[]{:S(2)}) copy-start(bf16[2,512,1024]{2,1,0:T(8,128)(2,1)S(1)} %fusion.5) | copy-start | bytes 6291460
